TPU v7x, 256 devices: a whole 4x4x8 slice. The times are simulated.
256 devices in a mesh: gz: 8 (over x, core), gx: 4 (over y), gy: 8 (over z).
Axes of the slice: x: 4, y: 4, z: 8, core: 2. Of those that a mesh axis runs over, the one named last changes fastest.
Arguments:
- right_side: float32 [64, 3, 64, 1024], P('gz', None, 'gy', 'gx'), may hold values from -6 to 6
- start_field: float32 [64, 3, 64, 1024], P('gz', None, 'gy', 'gx'), may hold values from -6 to 6
- layer_material: int32 [64], P('gz'), may hold values from 0 to 7
- stiffness: float32 [8, 3, 3, 3], replicated, may hold values from -0.2 to 8, as said below
- line_factors: float32 [8, 3, 3, 3], replicated, may hold values from -0.05 to 1
Outputs:
- solution_field: float32 [64, 3, 64, 1024], P('gz', None, 'gy', 'gx')
- final_residual: float32 [64, 3, 64, 1024], P('gz', None, 'gy', 'gx')
Inputs may be any that keep to these rules, and one draw needn't show every extreme that they name: `stiffness`: diagonal blocks dominate each row over the lateral and vertical couplings of the stencil.
All inputs are finite; a program needn't handle non-finite values.
Results may differ from a plain program's by a relative error of at most 0.0001.
Values sent between devices are 32-bit elements; how exact they have to be, the bound alone decides.
No kernel may reach another device: no remote copies, remote signals or barrier semaphores. Data moves between devices by JAX's collectives and lax.ppermute only.
A program may use at most 64 MiB of HBM per device.

v0:
```python
import jax
import jax.numpy as jnp
from jax import lax
from jax.sharding import PartitionSpec as P

SWEEPS = 3


def padded_2(value, sides, width):
    edges = {}
    for axis, dim in sides:
        size, length = (lax.axis_size(axis), value.shape[dim])
        up = [(i, (i + 1) % size) for i in range(size - 1)]
        last = lax.slice_in_dim(value, length - width, length, axis=dim)
        leading = lax.slice_in_dim(value, 0, width, axis=dim)
        edges[dim] = (
            lax.ppermute(last, axis, up),
            lax.ppermute(leading, axis, [(b, a) for a, b in up]),
        )
    done = []
    for _, dim in sides:
        low, high = edges[dim]
        around = [(width, width) if d in done else (0, 0) for d in range(value.ndim)]
        value = jnp.concatenate([jnp.pad(low, around), value, jnp.pad(high, around)], axis=dim)
        done.append(dim)
    return value


def sent_to_all(value, axis):
    length = lax.axis_size(axis)
    return lax.all_to_all(
        jnp.broadcast_to(value[None], (length, *value.shape)), axis, 0, 0, tiled=True
    )


def combined_pairwise(pieces, combine):
    while len(jax.tree.leaves(pieces)[0]) > 1:
        pieces = jax.vmap(combine)(
            *(jax.tree.map(lambda part: part[side::2], pieces) for side in (0, 1))
        )
    return jax.tree.map(lambda part: part[0], pieces)


def prefix(value, axis, combine, identity, reverse):
    length, place = (lax.axis_size(axis), lax.axis_index(axis))
    passed = jnp.arange(length) > place if reverse else jnp.arange(length) < place

    def kept(part, zero, own):
        part = jnp.where(
            passed.reshape(-1, *(1 for _ in own.shape)), part, jnp.asarray(zero, own.dtype)
        )
        return part[::-1] if reverse else part

    pieces = jax.tree.map(lambda part: sent_to_all(part, axis), value)
    return combined_pairwise(jax.tree.map(kept, pieces, identity, value), combine)


def apply_block(blocks, field):
    columns = []
    for row_index in range(3):
        summed = blocks[..., row_index, 0, None, None] * field[..., 0, :, :]
        for col_index in (1, 2):
            summed = (
                summed + blocks[..., row_index, col_index, None, None] * field[..., col_index, :, :]
            )
        columns.append(summed)
    return jnp.stack(columns, axis=-3)


def chain_link(earlier, later):
    earlier_map, earlier_vec = earlier
    later_map, later_vec = later
    joined = jnp.matmul(later_map, earlier_map, precision=lax.Precision.HIGHEST)
    return (joined, later_vec + apply_block(later_map, earlier_vec))


def running_chain(multipliers, sources):

    def advance(carry, item):
        joined = chain_link(carry, item)
        return (joined, joined)

    start = (jnp.eye(3, dtype=jnp.float32), jnp.zeros(sources.shape[1:], jnp.float32))
    _, (maps, vectors) = lax.scan(advance, start, (multipliers, sources), unroll=True)
    return (maps, vectors)


def layer_blocks(table, layer_ids):
    onehot = (layer_ids[:, None] == jnp.arange(table.shape[0])[None, :]).astype(jnp.float32)
    return jnp.sum(onehot[:, :, None, None, None] * table[None], axis=1)


def padded_field(field):
    return padded_2(field, (("gz", 0), ("gx", 3), ("gy", 2)), 1)


def operate(field, diag_block, lateral_block, vertical_block):
    padded = padded_field(field)
    lateral = padded[1:-1, :, 1:-1, 2:] + padded[1:-1, :, 1:-1, :-2]
    lateral = lateral + padded[1:-1, :, 2:, 1:-1] + padded[1:-1, :, :-2, 1:-1]
    vertical = padded[2:, :, 1:-1, 1:-1] + padded[:-2, :, 1:-1, 1:-1]
    return (
        apply_block(diag_block, field)
        - apply_block(lateral_block, lateral)
        - apply_block(vertical_block, vertical)
    )


def line_solve(resid, factor_blocks):
    identity = (jnp.eye(3, dtype=jnp.float32), jnp.zeros(resid.shape[1:], jnp.float32))
    weighted = apply_block(factor_blocks[:, 0], resid)
    forward_maps, upward = running_chain(factor_blocks[:, 1], weighted)
    forward_in = prefix((forward_maps[-1], upward[-1]), "gz", chain_link, identity, False)
    upward = upward + apply_block(forward_maps, forward_in[1][None])
    backward_maps, downward = running_chain(factor_blocks[::-1, 2], upward[::-1])
    backward_in = prefix((backward_maps[-1], downward[-1]), "gz", chain_link, identity, True)
    downward = downward + apply_block(backward_maps, backward_in[1][None])
    return downward[::-1]


def on_device(right_side, start_field, layer_material, stiffness, line_factors):
    load, field = (right_side, start_field)
    fine_sten = layer_blocks(stiffness, layer_material)
    coarse_sten = layer_blocks(stiffness, layer_material[0::2])
    fine_fac = layer_blocks(line_factors, layer_material)
    coarse_fac = layer_blocks(line_factors, layer_material[0::2])
    fine_args = (fine_sten[:, 0], fine_sten[:, 1], fine_sten[:, 2])
    coarse_args = (coarse_sten[:, 0], coarse_sten[:, 1], 0.25 * coarse_sten[:, 2])
    for counter in range(SWEEPS):
        field = field + line_solve(load - operate(field, *fine_args), fine_fac)
    resid = load - operate(field, *fine_args)
    paired = resid.reshape(resid.shape[0] // 2, 2, 3, resid.shape[2], resid.shape[3])
    coarse_rhs = paired[:, 0] + paired[:, 1]
    correction = line_solve(coarse_rhs, coarse_fac)
    for counter in range(SWEEPS - 1):
        correction = correction + line_solve(
            coarse_rhs - operate(correction, *coarse_args), coarse_fac
        )
    solution_field = field + jnp.repeat(correction, 2, axis=0)
    final_residual = load - operate(solution_field, *fine_args)
    return (solution_field, final_residual)


def solution(mesh):
    return jax.shard_map(
        on_device,
        mesh=mesh,
        in_specs=(P("gz", None, "gy", "gx"), P("gz", None, "gy", "gx"), P("gz"), P(), P()),
        out_specs=(P("gz", None, "gy", "gx"), P("gz", None, "gy", "gx")),
        check_vma=False,
    )
```

profile of v0, /device:TPU:104, one launch (start us, length us, event | category | flops | bytes accessed | tf_op | source)
XLA Modules:
  0.0 756.7 jit_solution(15165506708034781757)
XLA Ops:
  15.8 6.8 all-to-all-start.1
  96.8 5.7 multiply_add_fusion.314
  141.3 5.9 all-to-all-done
  164.8 5.7 multiply_add_fusion.290
  176.0 5.6 multiply_add_fusion.284
  187.3 5.7 add_bitcast_fusion.40
  197.2 6.7 all-to-all-done.2
  228.6 5.7 multiply_add_fusion.275
  274.2 6.7 all-to-all-done.4
  298.3 5.7 multiply_add_fusion.248
  320.7 5.7 add_bitcast_fusion.34
  362.1 5.7 multiply_add_fusion.236
  407.7 6.7 all-to-all-done.6
  431.9 5.7 multiply_add_fusion.212
  454.3 5.7 add_bitcast_fusion.24
  465.1 5.9 all-to-all-done.7
  495.7 5.7 multiply_add_fusion.200
  506.9 5.8 add_bitcast_fusion.21
  518.9 6.7 all-to-all-done.8
  537.3 5.7 multiply_add_fusion.188
  553.7 5.9 all-to-all-done.10
  560.0 5.7 multiply_add_fusion.185
  584.1 5.7 multiply_add_fusion.182
  595.3 5.8 add_bitcast_fusion.15
  601.2 11.9 %all_to_all.88 = f32[8,3,8,256]{3,2,1,0:T(8,128)S(1)} all-to-all(f32[8,3,8,256]{3,2,1,0:T(8,128)S(1)} %broadcast_in_dim.512), channel_id=1, replica_groups=mesh['gz'=8,'gx'=4,'gy'=8] {'gz'}, dimensions={0} | all-to-all | bytes 393216 | tf_op jit(solution)/shard_map/all_to_all | solution.py:31
  624.8 5.7 multiply_add_fusion.173
  636.3 9.2 %all_to_all.89 = f32[8,3,8,256]{3,2,1,0:T(8,128)S(1)} all-to-all(f32[8,3,8,256]{3,2,1,0:T(8,128)S(1)} %broadcast_in_dim.514), channel_id=1, replica_groups=mesh['gz'=8,'gx'=4,'gy'=8] {'gz'}, dimensions={0} | all-to-all | bytes 393216 | tf_op jit(solution)/shard_map/all_to_all | solution.py:31
  669.9 5.7 multiply_add_fusion.170
  681.1 5.8 add_bitcast_fusion.5
  687.0 11.9 %all_to_all.90 = f32[8,3,8,256]{3,2,1,0:T(8,128)S(1)} all-to-all(f32[8,3,8,256]{3,2,1,0:T(8,128)S(1)} %broadcast_in_dim.516), channel_id=1, replica_groups=mesh['gz'=8,'gx'=4,'gy'=8] {'gz'}, dimensions={0} | all-to-all | bytes 393216 | tf_op jit(solution)/shard_map/all_to_all | solution.py:31
  710.8 5.7 multiply_add_fusion.161
  722.2 9.2 %all_to_all.91 = f32[8,3,8,256]{3,2,1,0:T(8,128)S(1)} all-to-all(f32[8,3,8,256]{3,2,1,0:T(8,128)S(1)} %broadcast_in_dim.518), channel_id=1, replica_groups=mesh['gz'=8,'gx'=4,'gy'=8] {'gz'}, dimensions={0} | all-to-all | bytes 393216 | tf_op jit(solution)/shard_map/all_to_all | solution.py:31
  (678 shorter events, 522.2 us)
Async XLA Ops:
  1.4 92.3 %collective-permute-start = (f32[1,3,8,256]{3,2,1,0:T(8,128)S(1)}, f32[1,3,8,256]{3,2,1,0:T(8,128)S(1)}, u32[]{:S(2)}, u32[]{:S(2)}) collective-permute-start(f32[1,3,8,256]{3,2,1,0:T(8,128)S(1)} %get-tuple-element.246), channel_id=1, source_target_pairs={{0,32},{32,64},{64,96},{96,128},{128,160},{160,192},{192,224},{1,3... | collective-permute-start | bytes 73736 | tf_op jit(solution)/shard_map/ppermute | solution.py:17
  3.1 90.6 %collective-permute-start.1 = (f32[1,3,8,256]{3,2,1,0:T(8,128)S(1)}, f32[1,3,8,256]{3,2,1,0:T(8,128)S(1)}, u32[]{:S(2)}, u32[]{:S(2)}) collective-permute-start(f32[1,3,8,256]{3,2,1,0:T(8,128)S(1)} %get-tuple-element.245), channel_id=1, source_target_pairs={{32,0},{64,32},{96,64},{128,96},{160,128},{192,160},{224,192},{33,... | collective-permute-start | bytes 73736 | tf_op jit(solution)/shard_map/ppermute | solution.py:18
  5.6 83.0 %collective-permute-start.2 = (f32[8,3,8,1]{3,2,1,0:T(8,128)S(1)}, f32[8,3,8,1]{3,2,1,0:T(8,128)S(1)}, u32[]{:S(2)}, u32[]{:S(2)}) collective-permute-start(f32[8,3,8,1]{3,2,1,0:T(8,128)S(1)} %get-tuple-element.244), channel_id=1, source_target_pairs={{8,0},{16,8},{24,16},{9,1},{17,9},{25,17},{10,2},{18,10},{26,18},{... | collective-permute-start | bytes 2312 | tf_op jit(solution)/shard_map/ppermute | solution.py:18
  8.0 85.7 %collective-permute-start.3 = (f32[8,3,8,1]{3,2,1,0:T(8,128)S(1)}, f32[8,3,8,1]{3,2,1,0:T(8,128)S(1)}, u32[]{:S(2)}, u32[]{:S(2)}) collective-permute-start(f32[8,3,8,1]{3,2,1,0:T(8,128)S(1)} %get-tuple-element.243), channel_id=1, source_target_pairs={{0,8},{8,16},{16,24},{1,9},{9,17},{17,25},{2,10},{10,18},{18,26},{... | collective-permute-start | bytes 2312 | tf_op jit(solution)/shard_map/ppermute | solution.py:17
  11.6 82.2 %collective-permute-start.4 = (f32[8,3,1,256]{3,2,1,0:T(1,128)S(1)}, f32[8,3,1,256]{3,2,1,0:T(1,128)S(1)}, u32[]{:S(2)}, u32[]{:S(2)}) collective-permute-start(f32[8,3,1,256]{3,2,1,0:T(1,128)S(1)} %get-tuple-element.241), channel_id=1, source_target_pairs={{1,0},{2,1},{3,2},{4,3},{5,4},{6,5},{7,6},{9,8},{10,9},{11,10},{12... | collective-permute-start | bytes 73736 | tf_op jit(solution)/shard_map/ppermute | solution.py:18
  15.8 41.1 %all-to-all-start.1 = ((f32[8,3,3]{2,1,0:T(4,128)}), f32[8,3,3]{2,1,0:T(4,128)S(1)}, u32[]{:S(2)}, u32[]{:S(2)}) async-start(f32[8,3,3]{2,1,0:T(4,128)} %broadcast_in_dim.241), calls=%async_computation.1 | async-start | bytes 32768 | tf_op jit(solution)/shard_map/all_to_all | solution.py:31
  57.5 10.2 %all-to-all-start.3 = ((f32[8,3,3]{2,1,0:T(4,128)}), f32[8,3,3]{2,1,0:T(4,128)S(1)}, u32[]{:S(2)}, u32[]{:S(2)}) async-start(f32[8,3,3]{2,1,0:T(4,128)} %broadcast_in_dim.488), calls=%async_computation.3 | async-start | bytes 32768 | tf_op jit(solution)/shard_map/all_to_all | solution.py:31
  137.0 10.2 %all-to-all-start = ((f32[8,3,8,256]{3,2,1,0:T(8,128)}), f32[8,3,8,256]{3,2,1,0:T(8,128)S(1)}, u32[]{:S(2)}, u32[]{:S(2)}) async-start(f32[8,3,8,256]{3,2,1,0:T(8,128)} %broadcast_in_dim.238), calls=%async_computation | async-start | bytes 393216 | tf_op jit(solution)/shard_map/all_to_all | solution.py:31
  193.7 10.2 %all-to-all-start.2 = ((f32[8,3,8,256]{3,2,1,0:T(8,128)}), f32[8,3,8,256]{3,2,1,0:T(8,128)S(1)}, u32[]{:S(2)}, u32[]{:S(2)}) async-start(f32[8,3,8,256]{3,2,1,0:T(8,128)} %broadcast_in_dim.486), calls=%async_computation.2 | async-start | bytes 393216 | tf_op jit(solution)/shard_map/all_to_all | solution.py:31
  210.2 16.1 %collective-permute-start.6 = (f32[1,3,8,256]{3,2,1,0:T(8,128)S(1)}, f32[1,3,8,256]{3,2,1,0:T(8,128)S(1)}, u32[]{:S(2)}, u32[]{:S(2)}) collective-permute-start(f32[1,3,8,256]{3,2,1,0:T(8,128)S(1)} %get-tuple-element.219), channel_id=1, source_target_pairs={{0,32},{32,64},{64,96},{96,128},{128,160},{160,192},{192,224},{1,3... | collective-permute-start | bytes 73736 | tf_op jit(solution)/shard_map/ppermute | solution.py:17
  211.7 14.6 %collective-permute-start.7 = (f32[1,3,8,256]{3,2,1,0:T(8,128)S(1)}, f32[1,3,8,256]{3,2,1,0:T(8,128)S(1)}, u32[]{:S(2)}, u32[]{:S(2)}) collective-permute-start(f32[1,3,8,256]{3,2,1,0:T(8,128)S(1)} %get-tuple-element.220), channel_id=1, source_target_pairs={{32,0},{64,32},{96,64},{128,96},{160,128},{192,160},{224,192},{33,... | collective-permute-start | bytes 73736 | tf_op jit(solution)/shard_map/ppermute | solution.py:18
  215.4 10.9 %collective-permute-start.9 = (f32[8,3,8,1]{3,2,1,0:T(8,128)S(1)}, f32[8,3,8,1]{3,2,1,0:T(8,128)S(1)}, u32[]{:S(2)}, u32[]{:S(2)}) collective-permute-start(f32[8,3,8,1]{3,2,1,0:T(8,128)S(1)} %get-tuple-element.221), channel_id=1, source_target_pairs={{0,8},{8,16},{16,24},{1,9},{9,17},{17,25},{2,10},{10,18},{18,26},{... | collective-permute-start | bytes 2312 | tf_op jit(solution)/shard_map/ppermute | solution.py:17
  268.8 12.1 %all-to-all-start.4 = ((f32[8,3,8,256]{3,2,1,0:T(8,128)}), f32[8,3,8,256]{3,2,1,0:T(8,128)S(1)}, u32[]{:S(2)}, u32[]{:S(2)}) async-start(f32[8,3,8,256]{3,2,1,0:T(8,128)} %broadcast_in_dim.490), calls=%async_computation.4 | async-start | bytes 393216 | tf_op jit(solution)/shard_map/all_to_all | solution.py:31
  327.2 10.2 %all-to-all-start.5 = ((f32[8,3,8,256]{3,2,1,0:T(8,128)}), f32[8,3,8,256]{3,2,1,0:T(8,128)S(1)}, u32[]{:S(2)}, u32[]{:S(2)}) async-start(f32[8,3,8,256]{3,2,1,0:T(8,128)} %broadcast_in_dim.492), calls=%async_computation.5 | async-start | bytes 393216 | tf_op jit(solution)/shard_map/all_to_all | solution.py:31
  343.8 16.1 %collective-permute-start.12 = (f32[1,3,8,256]{3,2,1,0:T(8,128)S(1)}, f32[1,3,8,256]{3,2,1,0:T(8,128)S(1)}, u32[]{:S(2)}, u32[]{:S(2)}) collective-permute-start(f32[1,3,8,256]{3,2,1,0:T(8,128)S(1)} %get-tuple-element.199), channel_id=1, source_target_pairs={{0,32},{32,64},{64,96},{96,128},{128,160},{160,192},{192,224},{1,3... | collective-permute-start | bytes 73736 | tf_op jit(solution)/shard_map/ppermute | solution.py:17
  345.3 14.6 %collective-permute-start.13 = (f32[1,3,8,256]{3,2,1,0:T(8,128)S(1)}, f32[1,3,8,256]{3,2,1,0:T(8,128)S(1)}, u32[]{:S(2)}, u32[]{:S(2)}) collective-permute-start(f32[1,3,8,256]{3,2,1,0:T(8,128)S(1)} %get-tuple-element.200), channel_id=1, source_target_pairs={{32,0},{64,32},{96,64},{128,96},{160,128},{192,160},{224,192},{33,... | collective-permute-start | bytes 73736 | tf_op jit(solution)/shard_map/ppermute | solution.py:18
  348.9 10.9 %collective-permute-start.15 = (f32[8,3,8,1]{3,2,1,0:T(8,128)S(1)}, f32[8,3,8,1]{3,2,1,0:T(8,128)S(1)}, u32[]{:S(2)}, u32[]{:S(2)}) collective-permute-start(f32[8,3,8,1]{3,2,1,0:T(8,128)S(1)} %get-tuple-element.201), channel_id=1, source_target_pairs={{0,8},{8,16},{16,24},{1,9},{9,17},{17,25},{2,10},{10,18},{18,26},{... | collective-permute-start | bytes 2312 | tf_op jit(solution)/shard_map/ppermute | solution.py:17
  402.3 12.1 %all-to-all-start.6 = ((f32[8,3,8,256]{3,2,1,0:T(8,128)}), f32[8,3,8,256]{3,2,1,0:T(8,128)S(1)}, u32[]{:S(2)}, u32[]{:S(2)}) async-start(f32[8,3,8,256]{3,2,1,0:T(8,128)} %broadcast_in_dim.494), calls=%async_computation.6 | async-start | bytes 393216 | tf_op jit(solution)/shard_map/all_to_all | solution.py:31
  460.8 10.2 %all-to-all-start.7 = ((f32[8,3,8,256]{3,2,1,0:T(8,128)}), f32[8,3,8,256]{3,2,1,0:T(8,128)S(1)}, u32[]{:S(2)}, u32[]{:S(2)}) async-start(f32[8,3,8,256]{3,2,1,0:T(8,128)} %broadcast_in_dim.496), calls=%async_computation.7 | async-start | bytes 393216 | tf_op jit(solution)/shard_map/all_to_all | solution.py:31
  477.5 16.1 %collective-permute-start.18 = (f32[1,3,8,256]{3,2,1,0:T(8,128)S(1)}, f32[1,3,8,256]{3,2,1,0:T(8,128)S(1)}, u32[]{:S(2)}, u32[]{:S(2)}) collective-permute-start(f32[1,3,8,256]{3,2,1,0:T(8,128)S(1)} %get-tuple-element.179), channel_id=1, source_target_pairs={{0,32},{32,64},{64,96},{96,128},{128,160},{160,192},{192,224},{1,3... | collective-permute-start | bytes 73736 | tf_op jit(solution)/shard_map/ppermute | solution.py:17
  478.9 14.6 %collective-permute-start.19 = (f32[1,3,8,256]{3,2,1,0:T(8,128)S(1)}, f32[1,3,8,256]{3,2,1,0:T(8,128)S(1)}, u32[]{:S(2)}, u32[]{:S(2)}) collective-permute-start(f32[1,3,8,256]{3,2,1,0:T(8,128)S(1)} %get-tuple-element.180), channel_id=1, source_target_pairs={{32,0},{64,32},{96,64},{128,96},{160,128},{192,160},{224,192},{33,... | collective-permute-start | bytes 73736 | tf_op jit(solution)/shard_map/ppermute | solution.py:18
  482.6 10.9 %collective-permute-start.21 = (f32[8,3,8,1]{3,2,1,0:T(8,128)S(1)}, f32[8,3,8,1]{3,2,1,0:T(8,128)S(1)}, u32[]{:S(2)}, u32[]{:S(2)}) collective-permute-start(f32[8,3,8,1]{3,2,1,0:T(8,128)S(1)} %get-tuple-element.181), channel_id=1, source_target_pairs={{0,8},{8,16},{16,24},{1,9},{9,17},{17,25},{2,10},{10,18},{18,26},{... | collective-permute-start | bytes 2312 | tf_op jit(solution)/shard_map/ppermute | solution.py:17
  513.5 12.1 %all-to-all-start.8 = ((f32[8,3,8,256]{3,2,1,0:T(8,128)}), f32[8,3,8,256]{3,2,1,0:T(8,128)S(1)}, u32[]{:S(2)}, u32[]{:S(2)}) async-start(f32[8,3,8,256]{3,2,1,0:T(8,128)} %broadcast_in_dim.502), calls=%async_computation.8 | async-start | bytes 393216 | tf_op jit(solution)/shard_map/all_to_all | solution.py:31
  566.0 16.2 %collective-permute-start.24 = (f32[1,3,8,256]{3,2,1,0:T(8,128)S(1)}, f32[1,3,8,256]{3,2,1,0:T(8,128)S(1)}, u32[]{:S(2)}, u32[]{:S(2)}) collective-permute-start(f32[1,3,8,256]{3,2,1,0:T(8,128)S(1)} %get-tuple-element.317), channel_id=1, source_target_pairs={{0,32},{32,64},{64,96},{96,128},{128,160},{160,192},{192,224},{1,3... | collective-permute-start | bytes 73736 | tf_op jit(solution)/shard_map/ppermute | solution.py:17
  567.4 14.8 %collective-permute-start.25 = (f32[1,3,8,256]{3,2,1,0:T(8,128)S(1)}, f32[1,3,8,256]{3,2,1,0:T(8,128)S(1)}, u32[]{:S(2)}, u32[]{:S(2)}) collective-permute-start(f32[1,3,8,256]{3,2,1,0:T(8,128)S(1)} %get-tuple-element.318), channel_id=1, source_target_pairs={{32,0},{64,32},{96,64},{128,96},{160,128},{192,160},{224,192},{33,... | collective-permute-start | bytes 73736 | tf_op jit(solution)/shard_map/ppermute | solution.py:18
  571.1 11.0 %collective-permute-start.27 = (f32[4,3,8,1]{3,2,1,0:T(8,128)S(1)}, f32[4,3,8,1]{3,2,1,0:T(8,128)S(1)}, u32[]{:S(2)}, u32[]{:S(2)}) collective-permute-start(f32[4,3,8,1]{3,2,1,0:T(8,128)S(1)} %slice.6486), channel_id=1, source_target_pairs={{0,8},{8,16},{16,24},{1,9},{9,17},{17,25},{2,10},{10,18},{18,26},{... | collective-permute-start | bytes 1160 | tf_op jit(solution)/shard_map/ppermute | solution.py:17
  652.0 16.1 %collective-permute-start.30 = (f32[1,3,8,256]{3,2,1,0:T(8,128)S(1)}, f32[1,3,8,256]{3,2,1,0:T(8,128)S(1)}, u32[]{:S(2)}, u32[]{:S(2)}) collective-permute-start(f32[1,3,8,256]{3,2,1,0:T(8,128)S(1)} %get-tuple-element.278), channel_id=1, source_target_pairs={{0,32},{32,64},{64,96},{96,128},{128,160},{160,192},{192,224},{1,3... | collective-permute-start | bytes 73736 | tf_op jit(solution)/shard_map/ppermute | solution.py:17
  653.5 14.6 %collective-permute-start.31 = (f32[1,3,8,256]{3,2,1,0:T(8,128)S(1)}, f32[1,3,8,256]{3,2,1,0:T(8,128)S(1)}, u32[]{:S(2)}, u32[]{:S(2)}) collective-permute-start(f32[1,3,8,256]{3,2,1,0:T(8,128)S(1)} %get-tuple-element.279), channel_id=1, source_target_pairs={{32,0},{64,32},{96,64},{128,96},{160,128},{192,160},{224,192},{33,... | collective-permute-start | bytes 73736 | tf_op jit(solution)/shard_map/ppermute | solution.py:18
  657.1 10.9 %collective-permute-start.33 = (f32[4,3,8,1]{3,2,1,0:T(8,128)S(1)}, f32[4,3,8,1]{3,2,1,0:T(8,128)S(1)}, u32[]{:S(2)}, u32[]{:S(2)}) collective-permute-start(f32[4,3,8,1]{3,2,1,0:T(8,128)S(1)} %get-tuple-element.280), channel_id=1, source_target_pairs={{0,8},{8,16},{16,24},{1,9},{9,17},{17,25},{2,10},{10,18},{18,26},{... | collective-permute-start | bytes 1160 | tf_op jit(solution)/shard_map/ppermute | solution.py:17
  738.1 16.1 %collective-permute-start.36 = (f32[1,3,8,256]{3,2,1,0:T(8,128)S(1)}, f32[1,3,8,256]{3,2,1,0:T(8,128)S(1)}, u32[]{:S(2)}, u32[]{:S(2)}) collective-permute-start(f32[1,3,8,256]{3,2,1,0:T(8,128)S(1)} %get-tuple-element.158), channel_id=1, source_target_pairs={{0,32},{32,64},{64,96},{96,128},{128,160},{160,192},{192,224},{1,3... | collective-permute-start | bytes 73736 | tf_op jit(solution)/shard_map/ppermute | solution.py:17
  739.5 14.6 %collective-permute-start.37 = (f32[1,3,8,256]{3,2,1,0:T(8,128)S(1)}, f32[1,3,8,256]{3,2,1,0:T(8,128)S(1)}, u32[]{:S(2)}, u32[]{:S(2)}) collective-permute-start(f32[1,3,8,256]{3,2,1,0:T(8,128)S(1)} %get-tuple-element.159), channel_id=1, source_target_pairs={{32,0},{64,32},{96,64},{128,96},{160,128},{192,160},{224,192},{33,... | collective-permute-start | bytes 73736 | tf_op jit(solution)/shard_map/ppermute | solution.py:18
  743.2 10.9 %collective-permute-start.39 = (f32[8,3,8,1]{3,2,1,0:T(8,128)S(1)}, f32[8,3,8,1]{3,2,1,0:T(8,128)S(1)}, u32[]{:S(2)}, u32[]{:S(2)}) collective-permute-start(f32[8,3,8,1]{3,2,1,0:T(8,128)S(1)} %get-tuple-element.160), channel_id=1, source_target_pairs={{0,8},{8,16},{16,24},{1,9},{9,17},{17,25},{2,10},{10,18},{18,26},{... | collective-permute-start | bytes 2312 | tf_op jit(solution)/shard_map/ppermute | solution.py:17
  (28 other events, 201.6 us)
where the time goes:
time: 768 us; the launch traced here: 757 us
  other arithmetic  419 us (55%)
  starting transfers between devices  163 us (21%)
  waiting for transfers between devices  71 us (9%)
  blocking collectives  42.2 us (5%)
  local copies, waits for them, and re-layouts  30.2 us (4%)
  between operations  26.8 us (3%)
    add x135, other arithmetic, apply_block(): summed + blocks[..., row_index, col_index, None, None] * field[..., col_i...  343 us
    ppermute x21, starting transfers between devices, padded_2(): lax.ppermute(last, axis, up)  72.4 us
    another operation x22, other arithmetic, apply_block(): return jnp.stack(columns, axis=-3)  68.7 us
    all_to_all x12, waiting for transfers between devices, sent_to_all(): lax.all_to_all(jnp.broadcast_to(value[None], (length, *value.shape)), axi...  62.2 us
    all_to_all x12, starting transfers between devices, sent_to_all(): lax.all_to_all(jnp.broadcast_to(value[None], (length, *value.shape)), axi...  51.2 us
    all_to_all x4, blocking collectives, sent_to_all(): lax.all_to_all(jnp.broadcast_to(value[None], (length, *value.shape)), axi...  42.2 us
    ppermute x21, starting transfers between devices, padded_2(): lax.ppermute(leading, axis, [(b, a) for a, b in up])  39.2 us
  transfers between devices with their start and end apart: 54, of which 18 were waited for; matrix products, arithmetic and copies ran while one was open for 4% of the time, Pallas kernels for 0%

commit v1 on v0

v1 whole, which is shorter than its diff:
```python
import jax
import jax.numpy as jnp
from jax import lax
from jax.experimental import pallas as pl
from jax.experimental.pallas import tpu as pltpu
from jax.sharding import PartitionSpec as P

F32 = jnp.float32
BF16 = jnp.bfloat16
HALO = 7
XH = 8
XT = 32
XW = XT + 2 * XH
YT = 8
YW = YT + 2 * HALO
NZ = 64
NC = NZ // 2
VMEM = pl.BlockSpec(memory_space=pltpu.VMEM)
SMEM = pl.BlockSpec(memory_space=pltpu.SMEM)


def params():
    return pltpu.CompilerParams(vmem_limit_bytes=40 * 1024 * 1024)


def swap_blocks(tile):
    sub = lax.broadcasted_iota(jnp.int32, tile.shape, 1)
    blk = lax.broadcasted_iota(jnp.int32, tile.shape, 2) // 32
    for bit in (1, 2, 4):
        up = pltpu.roll(pltpu.roll(tile, 8 - bit, axis=1), 32 * bit, axis=2)
        down = pltpu.roll(pltpu.roll(tile, bit, axis=1), 256 - 32 * bit, axis=2)
        in_sub = (sub & bit) != 0
        in_blk = (blk & bit) != 0
        tile = jnp.where(in_sub == in_blk, tile, jnp.where(in_blk, up, down))
    return tile


def pack_kernel(load_ref, start_ref, out_ref):
    for f, ref in enumerate((load_ref, start_ref)):
        for c in range(3):
            tile = swap_blocks(ref[:, c])
            for z in range(8):
                for h in range(2):
                    at = h * 48 + f * 24 + c * 8 + z
                    out_ref[pl.ds(at, 8, stride=96), :] = tile[z, :, h * 128 : h * 128 + 128]


def unpack_kernel(got_ref, start_ref, field_ref, resid_ref):
    for f, ref in enumerate((field_ref, resid_ref)):
        for c in range(3):
            halves = []
            for h in range(2):
                at = h * 48 + f * 24 + c * 8
                rows = [got_ref[pl.ds(at + z, 8, stride=96), :] for z in range(8)]
                halves.append(jnp.stack(rows, axis=0))
            tile = swap_blocks(jnp.concatenate(halves, axis=2))
            if f == 0:
                tile = tile + start_ref[:, c]
            ref[:, c] = tile


def turn_kernel(got_ref, own_ref, low_ref, high_ref):
    halves = []
    for h in range(2):
        rows = [got_ref[g, h * 48 + q * 8 : h * 48 + q * 8 + 8] for q in range(6) for g in range(8)]
        halves.append(jnp.transpose(jnp.concatenate(rows, axis=0)))
    turned = jnp.concatenate(halves, axis=0).reshape(YT, XT, 384)
    own_ref[...] = turned
    low_ref[...] = turned[:HALO]
    high_ref[...] = turned[YT - HALO :]


def sides_kernel(own_ref, above_ref, below_ref, left_ref, right_ref):
    for ref, cols in ((left_ref, slice(0, XH)), (right_ref, slice(XT - XH, XT))):
        ref[0:HALO] = above_ref[:, cols]
        ref[HALO : HALO + YT] = own_ref[:, cols]
        ref[HALO + YT :] = below_ref[:, cols]


def split(value):
    high = value.astype(BF16)
    return high, (value - high.astype(F32)).astype(BF16)


def line_rows(mats_ref, factor_ref, dst_ref, layers, step):
    lane = lax.broadcasted_iota(jnp.int32, (1, 3 * layers), 1)

    def up(z, state):
        base = mats_ref[z * step] * 27
        new = []
        for i in range(3):
            row = jnp.zeros((1, 3 * layers), F32)
            for j in range(3):
                row = jnp.where(lane == j * layers + z, factor_ref[base + i * 3 + j], row)
            for j in range(3):
                row = row + factor_ref[base + 9 + i * 3 + j] * state[j]
            dst_ref[pl.ds(i * layers + z, 1), :] = row
            new.append(row)
        return tuple(new)

    def down(t, state):
        z = layers - 1 - t
        base = mats_ref[z * step] * 27
        new = []
        for i in range(3):
            row = dst_ref[pl.ds(i * layers + z, 1), :]
            for j in range(3):
                row = row + factor_ref[base + 18 + i * 3 + j] * state[j]
            dst_ref[pl.ds(i * layers + z, 1), :] = row
            new.append(row)
        return tuple(new)

    zero = tuple(jnp.zeros((1, 3 * layers), F32) for _ in range(3))
    lax.fori_loop(0, layers, up, zero, unroll=8)
    lax.fori_loop(0, layers, down, zero, unroll=8)


def couple(sten, which, blocks):
    out = []
    for i in range(3):
        total = None
        for j in range(3):
            at = which * 9 + i * 3 + j
            term = sten[:, at : at + 1] * blocks[j]
            total = term if total is None else total + term
        out.append(total)
    return out


def above_below(block):
    row = lax.broadcasted_iota(jnp.int32, block.shape, 0)
    n = block.shape[0]
    low = jnp.where(row == 0, 0.0, pltpu.roll(block, 1, axis=0))
    high = jnp.where(row == n - 1, 0.0, pltpu.roll(block, n - 1, axis=0))
    return low + high


def store_split(ref, at, rows):
    value = jnp.transpose(jnp.concatenate(rows, axis=0))
    high, low = split(value)
    ref[0, :, at : at + value.shape[1]] = high
    ref[1, :, at : at + value.shape[1]] = low


def setup_kernel(
    mats_ref, factor_ref, sten_ref, fine_ref, coarse_ref, first_ref, line_ref, cline_ref
):
    sten = sten_ref[...]
    line_rows(mats_ref, factor_ref, line_ref, NZ, 1)
    line_rows(mats_ref, factor_ref, cline_ref, NC, 2)

    row = lax.broadcasted_iota(jnp.int32, (NZ, 256), 0)
    lane = lax.broadcasted_iota(jnp.int32, (NZ, 256), 1)
    comp = lane // NZ - 1
    layer = lane % NZ
    same = (row == layer) & (comp >= 0)
    near = ((row == layer + 1) | (row == layer - 1)) & (comp >= 0)

    def picked(which, i):
        at = which * 9 + i * 3
        return jnp.where(
            comp == 0,
            sten[:, at : at + 1],
            jnp.where(comp == 1, sten[:, at + 1 : at + 2], sten[:, at + 2 : at + 3]),
        )

    store_split(
        first_ref,
        0,
        [jnp.where(same, picked(0, i), jnp.where(near, -picked(2, i), 0.0)) for i in range(3)],
    )
    store_split(first_ref, 256, [jnp.where(same, picked(1, i), 0.0) for i in range(3)])

    def level(sten_part, scale, ref, layers):
        blocks = [ref[i * layers : (i + 1) * layers, :] for i in range(3)]
        lateral = couple(sten_part, 1, blocks)
        diag = couple(sten_part, 0, blocks)
        vert = couple(sten_part, 2, [above_below(block) for block in blocks])
        if scale is not None:
            vert = [scale * part for part in vert]
        wide = blocks[0].shape
        r = lax.broadcasted_iota(jnp.int32, wide, 0)
        q = lax.broadcasted_iota(jnp.int32, wide, 1)
        kept = [
            jnp.where(q == r + i * layers, 1.0, 0.0) - (diag[i] - vert[i]) for i in range(3)
        ]
        return blocks, kept, lateral

    blocks, kept, lateral = level(sten, None, line_ref, NZ)
    store_split(fine_ref, 0, blocks)
    store_split(fine_ref, 256, kept)
    store_split(fine_ref, 512, lateral)

    def exact(a, b):
        return jnp.dot(a, b, precision=lax.Precision.HIGHEST, preferred_element_type=F32)

    layer_at = lax.broadcasted_iota(jnp.int32, (NC, NZ), 1) // 2
    pairs = (lax.broadcasted_iota(jnp.int32, (NC, NZ), 0) == layer_at).astype(F32)
    layer_at = lax.broadcasted_iota(jnp.int32, (NZ, NC), 0) // 2
    repeats = (lax.broadcasted_iota(jnp.int32, (NZ, NC), 1) == layer_at).astype(F32)

    def paired(part):
        return [exact(pairs, block) for block in part]

    store_split(fine_ref, 768, paired(kept))
    store_split(fine_ref, 896, paired(lateral))

    coarse_sten = sten_ref[pl.ds(0, NC, stride=2), :]
    cblocks, ckept, clateral = level(coarse_sten, 0.25, cline_ref, NC)
    store_split(coarse_ref, 0, ckept)
    store_split(coarse_ref, 128, clateral)
    spread = [exact(repeats, block) for block in cblocks]
    diag = couple(sten, 0, spread)
    vert = couple(sten, 2, [above_below(block) for block in spread])
    store_split(coarse_ref, 256, spread)
    store_split(coarse_ref, 512, [d - v for d, v in zip(diag, vert)])
    store_split(coarse_ref, 768, couple(sten, 1, spread))


def cycle_kernel(
    own_ref,
    above_ref,
    below_ref,
    left_ref,
    right_ref,
    fine_ref,
    coarse_ref,
    first_ref,
    out_ref,
    x_ref,
    r_ref,
    keep_ref,
    side_ref,
    sum_ref,
    rc_ref,
    ckeep_ref,
    cside_ref,
    csum_ref,
):
    gz, gx, gy = (lax.axis_index(axis) for axis in ("gz", "gx", "gy"))
    at_left = (gx == 0) & (gz == 0)
    at_right = (gx == lax.axis_size("gx") - 1) & (gz == lax.axis_size("gz") - 1)
    at_top = gy == 0
    at_bottom = gy == lax.axis_size("gy") - 1

    x_ref[:, 0:XH] = left_ref[...]
    x_ref[:, XH + XT :] = right_ref[...]
    x_ref[0:HALO, XH : XH + XT] = above_ref[...]
    x_ref[HALO : HALO + YT, XH : XH + XT] = own_ref[...]
    x_ref[HALO + YT :, XH : XH + XT] = below_ref[...]

    def product(halves, w_ref, at, width):
        high, low = halves
        wh = w_ref[0, :, at : at + width]
        wl = w_ref[1, :, at : at + width]

        def dot(a, b):
            return jnp.dot(a, b, preferred_element_type=F32)

        return dot(high, wh) + (dot(high, wl) + dot(low, wh))

    def chunks(lo, hi, size):
        return [(y, min(y + size, hi)) for y in range(lo, hi, size)]

    def apply(src, lanes, lo, hi, w_ref, jobs, size=4):
        for a, b in chunks(lo, hi, size):
            value = src[a:b, :, lanes].reshape((b - a) * XW, -1)
            halves = split(value)
            for at, width, dst in jobs:
                dst[a:b] = product(halves, w_ref, at, width).reshape(b - a, XW, width)

    def spread(side, y):
        mid = side[y]
        return (side[y - 1] + side[y + 1]) + (
            pltpu.roll(mid, 1, axis=0) + pltpu.roll(mid, XW - 1, axis=0)
        )

    def clear(ref, lo, hi):
        width = ref.shape[2]

        @pl.when(at_left)
        def _():
            ref[lo:hi, 0:XH] = jnp.zeros((hi - lo, XH, width), F32)

        @pl.when(at_right)
        def _():
            ref[lo:hi, XH + XT :] = jnp.zeros((hi - lo, XH, width), F32)

        if lo < HALO:

            @pl.when(at_top)
            def _():
                ref[lo:HALO] = jnp.zeros((HALO - lo, XW, width), F32)

        if hi > HALO + YT:

            @pl.when(at_bottom)
            def _():
                ref[HALO + YT : hi] = jnp.zeros((hi - HALO - YT, XW, width), F32)

    own = slice(HALO, HALO + YT)
    inner = slice(XH, XH + XT)
    every = slice(None)

    apply(
        x_ref, slice(128, 384), 0, YW, first_ref, [(0, 192, keep_ref), (256, 192, side_ref)]
    )
    for y in range(1, YW - 1):
        r_ref[y] = (x_ref[y, :, 0:192] - keep_ref[y]) + spread(side_ref, y)
    clear(r_ref, 1, YW - 1)
    sum_ref[...] = r_ref[own, inner]

    for sweep in (1, 2):
        lo, hi = sweep, YW - sweep
        apply(r_ref, every, lo, hi, fine_ref, [(256, 192, keep_ref), (512, 192, side_ref)])
        for y in range(lo + 1, hi - 1):
            r_ref[y] = keep_ref[y] + spread(side_ref, y)
        clear(r_ref, lo + 1, hi - 1)
        sum_ref[...] += r_ref[own, inner]

    apply(r_ref, every, 3, YW - 3, fine_ref, [(768, 96, ckeep_ref), (896, 96, cside_ref)])
    apply(
        r_ref, every, HALO - 1, HALO + YT + 1, fine_ref, [(256, 192, keep_ref), (512, 192, side_ref)], 5
    )
    for y in range(4, YW - 4):
        rc_ref[y] = ckeep_ref[y] + spread(cside_ref, y)
    clear(rc_ref, 4, YW - 4)
    for y in range(HALO, HALO + YT):
        r_ref[y] = keep_ref[y] + spread(side_ref, y)
    csum_ref[HALO - 1 : HALO + YT + 1] = rc_ref[HALO - 1 : HALO + YT + 1]

    for sweep in (4, 5):
        lo, hi = sweep, YW - sweep
        apply(rc_ref, every, lo, hi, coarse_ref, [(0, 96, ckeep_ref), (128, 96, cside_ref)], 5)
        for y in range(lo + 1, hi - 1):
            rc_ref[y] = ckeep_ref[y] + spread(cside_ref, y)
        clear(rc_ref, lo + 1, hi - 1)
        csum_ref[HALO - 1 : HALO + YT + 1] += rc_ref[HALO - 1 : HALO + YT + 1]

    apply(
        csum_ref,
        every,
        HALO - 1,
        HALO + YT + 1,
        coarse_ref,
        [(512, 192, keep_ref), (768, 192, side_ref)],
        5,
    )
    resid = []
    for y in range(HALO, HALO + YT):
        resid.append(((r_ref[y] - keep_ref[y]) + spread(side_ref, y))[inner])
    resid = jnp.concatenate(resid, axis=0)
    change = product(split(sum_ref[...].reshape(YT * XT, 192)), fine_ref, 0, 192)
    change = change + product(
        split(csum_ref[own, inner].reshape(YT * XT, 96)), coarse_ref, 256, 192
    )
    for f, value in enumerate((change, resid)):
        turned = jnp.transpose(value)
        for c in range(3):
            for g in range(8):
                rows = turned[c * NZ + g * 8 : c * NZ + g * 8 + 8]
                for h in range(2):
                    at = h * 48 + f * 24 + c * 8
                    out_ref[g, at : at + 8, :] = rows[:, h * 128 : h * 128 + 128]


def shape(*dims, dtype=F32):
    return jax.ShapeDtypeStruct(dims, dtype)


def on_device(right_side, start_field, layer_material, stiffness, line_factors):
    size_y = lax.axis_size("gy")
    mats = lax.all_gather(layer_material, "gz", axis=0, tiled=True)
    packed = pl.pallas_call(
        pack_kernel,
        out_shape=shape(768, 128),
        in_specs=[VMEM, VMEM],
        out_specs=VMEM,
        compiler_params=params(),
        name="pack",
    )(right_side, start_field)
    got = lax.all_to_all(packed.reshape(8, 96, 128), "gz", 0, 0, tiled=True)

    onehot = (mats[:, None] == jnp.arange(stiffness.shape[0])[None, :]).astype(F32)
    sten = jnp.sum(onehot[:, :, None] * stiffness.reshape(1, -1, 27), axis=1)
    sten = jnp.pad(sten, ((0, 0), (0, 128 - 27)))
    fine, coarse, first = pl.pallas_call(
        setup_kernel,
        out_shape=(
            shape(2, 192, 1024, dtype=BF16),
            shape(2, 96, 1024, dtype=BF16),
            shape(2, 256, 512, dtype=BF16),
        ),
        in_specs=[SMEM, SMEM, VMEM],
        out_specs=(VMEM, VMEM, VMEM),
        scratch_shapes=[
            pltpu.VMEM((192, 192), F32),
            pltpu.VMEM((96, 96), F32),
        ],
        compiler_params=params(),
        name="setup",
    )(mats, line_factors.reshape(-1), sten)

    own, low, high = pl.pallas_call(
        turn_kernel,
        out_shape=(shape(YT, XT, 384), shape(HALO, XT, 384), shape(HALO, XT, 384)),
        in_specs=[VMEM],
        out_specs=(VMEM, VMEM, VMEM),
        compiler_params=params(),
        name="turn",
    )(got)
    ahead = [(i, i + 1) for i in range(size_y - 1)]
    above = lax.ppermute(high, "gy", ahead)
    below = lax.ppermute(low, "gy", [(b, a) for a, b in ahead])
    to_left, to_right = pl.pallas_call(
        sides_kernel,
        out_shape=(shape(YW, XH, 384), shape(YW, XH, 384)),
        in_specs=[VMEM, VMEM, VMEM],
        out_specs=(VMEM, VMEM),
        compiler_params=params(),
        name="sides",
    )(own, above, below)
    count_x, count_z = lax.axis_size("gx"), lax.axis_size("gz")
    along = [(i % count_z) * count_x + i // count_z for i in range(count_x * count_z)]
    ahead = list(zip(along[:-1], along[1:]))
    left = lax.ppermute(to_right, ("gz", "gx"), ahead)
    right = lax.ppermute(to_left, ("gz", "gx"), [(b, a) for a, b in ahead])

    out = pl.pallas_call(
        cycle_kernel,
        out_shape=shape(8, 96, 128),
        in_specs=[VMEM] * 8,
        out_specs=VMEM,
        scratch_shapes=[
            pltpu.VMEM((YW, XW, 384), F32),
            pltpu.VMEM((YW, XW, 192), F32),
            pltpu.VMEM((YW, XW, 192), F32),
            pltpu.VMEM((YW, XW, 192), F32),
            pltpu.VMEM((YT, XT, 192), F32),
            pltpu.VMEM((YW, XW, 96), F32),
            pltpu.VMEM((YW, XW, 96), F32),
            pltpu.VMEM((YW, XW, 96), F32),
            pltpu.VMEM((YW, XW, 96), F32),
        ],
        compiler_params=params(),
        name="cycle",
    )(own, above, below, left, right, fine, coarse, first)
    back = lax.all_to_all(out, "gz", 0, 0, tiled=True)
    return pl.pallas_call(
        unpack_kernel,
        out_shape=(shape(8, 3, 8, 256), shape(8, 3, 8, 256)),
        in_specs=[VMEM, VMEM],
        out_specs=(VMEM, VMEM),
        compiler_params=params(),
        name="unpack",
    )(back.reshape(768, 128), start_field)


def solution(mesh):
    return jax.shard_map(
        on_device,
        mesh=mesh,
        in_specs=(P("gz", None, "gy", "gx"), P("gz", None, "gy", "gx"), P("gz"), P(), P()),
        out_specs=(P("gz", None, "gy", "gx"), P("gz", None, "gy", "gx")),
        check_vma=False,
    )
```

time: 768 us -> 68.8 us (0.09); the launches traced: 757 us -> 68.3 us
  other arithmetic: 419 us -> 0.11 us
  starting transfers between devices: 163 us -> 14.6 us
  waiting for transfers between devices: 71 us -> 0.08 us
  between operations: 26.8 us -> 1.46 us
  local copies, waits for them, and re-layouts: 30.2 us -> 4.96 us
  Pallas kernels: 0 us -> 14.3 us
  blocking collectives: 42.2 us -> 32.8 us
    add x270 -> x0, other arithmetic: 347 us -> none  [the longest x135 343 us: apply_block(): summed + blocks[..., row_index, col_index, None, None] * field[..., col_i...]
    ppermute x42 -> x4, starting transfers between devices: 112 us -> 14.6 us  [the longest x1 5.75 us: on_device(): right = lax.ppermute(to_left, ('gz', 'gx'), [(b, a) for a, b in ahead])]
    another operation x22 -> x0, other arithmetic: 68.7 us -> none  [apply_block(): return jnp.stack(columns, axis=-3)]
    all_to_all x12 -> x0, waiting for transfers between devices: 62.2 us -> none  [sent_to_all(): lax.all_to_all(jnp.broadcast_to(value[None], (length, *value.shape)), axi...]
    all_to_all x12 -> x0, starting transfers between devices: 51.2 us -> none  [sent_to_all(): lax.all_to_all(jnp.broadcast_to(value[None], (length, *value.shape)), axi...]
    slice x113 -> x0, local copies, waits for them, and re-layouts: 19.1 us -> none  [the longest x41 14.8 us: apply_block(): summed = blocks[..., row_index, 0, None, None] * field[..., 0, :, :]]
    all_to_all x4 -> x2, blocking collectives: 42.2 us -> 25.2 us  [the longest x1 13 us: on_device(): got = lax.all_to_all(packed.reshape(8, 96, 128), 'gz', 0, 0, tiled=True)]
    pallas_call x0 -> x6, Pallas kernels: none -> 14.3 us  [the longest x1 6.7 us: on_device(): pl.pallas_call(cycle_kernel, out_shape=shape(8, 96, 128), in_specs=[VMEM]...]
  transfers between devices with their start and end apart: 54 -> 4, of which waited for: 18 -> 1; matrix products, arithmetic and copies ran while one was open for 4% -> 2% of each run, Pallas kernels for 0% -> 7%
where the time goes in v1:
time: 68.8 us; the launch traced here: 68.3 us
  blocking collectives  32.8 us (48%)
  starting transfers between devices  14.6 us (21%)
  Pallas kernels  14.3 us (21%)
  local copies, waits for them, and re-layouts  4.96 us (7%)
  between operations  1.46 us (2%)
    all_to_all x1, blocking collectives, on_device(): got = lax.all_to_all(packed.reshape(8, 96, 128), 'gz', 0, 0, tiled=True)  13 us
    all_to_all x1, blocking collectives, on_device(): back = lax.all_to_all(out, 'gz', 0, 0, tiled=True)  12.1 us
    unnamed x1, blocking collectives  7.63 us
    pallas_call x1, Pallas kernels, on_device(): pl.pallas_call(cycle_kernel, out_shape=shape(8, 96, 128), in_specs=[VMEM]...  6.7 us
    ppermute x1, starting transfers between devices, on_device(): right = lax.ppermute(to_left, ('gz', 'gx'), [(b, a) for a, b in ahead])  5.75 us
    ppermute x1, starting transfers between devices, on_device(): above = lax.ppermute(high, 'gy', ahead)  5.04 us
    pallas_call x1, Pallas kernels, on_device(): pl.pallas_call(setup_kernel, out_shape=(shape(2, 192, 1024, dtype=BF16),...  4.92 us
    unnamed x18, local copies, waits for them, and re-layouts  4.7 us
  transfers between devices with their start and end apart: 4, of which 1 were waited for; matrix products, arithmetic and copies ran while one was open for 2% of the time, Pallas kernels for 7%

profile of v1, /device:TPU:104, one launch (start us, length us, event | category | flops | bytes accessed | tf_op | source)
XLA Modules:
  0.0 68.3 jit_solution(8144132491573253260)
XLA Ops:
  0.6 0.0 copy-start
  0.6 0.9 %copy-done = f32[8,3,8,256]{3,2,1,0:T(8,128)S(1)} copy-done((f32[8,3,8,256]{3,2,1,0:T(8,128)S(1)}, f32[8,3,8,256]{3,2,1,0:T(8,128)}, u32[]{:S(2)}) %copy-start) | copy-done | bytes 196632
  1.6 0.9 %copy-done.2 = f32[8,3,8,256]{3,2,1,0:T(8,128)S(1)} copy-done((f32[8,3,8,256]{3,2,1,0:T(8,128)S(1)}, f32[8,3,8,256]{3,2,1,0:T(8,128)}, u32[]{:S(2)}) %copy-start.2) | copy-done | bytes 196632
  2.5 0.9 %pack.1 = f32[768,128]{1,0:T(8,128)S(1)} custom-call(f32[8,3,8,256]{3,2,1,0:T(8,128)S(1)} %copy-done.2, f32[8,3,8,256]{3,2,1,0:T(8,128)S(1)} %copy-done), custom_call_target="tpu_custom_call" | custom-call | tf_op jit(solution)/shard_map/pack/pallas_call | solution.py:374
  3.4 13.0 %all_to_all.10.got_ref = f32[8,96,128]{2,1,0:T(8,128)S(1)} all-to-all(f32[8,96,128]{2,1,0:T(8,128)S(1)} %bitcast.6), channel_id=1, replica_groups=mesh['gz'=8,'gx'=4,'gy'=8] {'gz'}, dimensions={0} | all-to-all | bytes 786432 | tf_op jit(solution)/shard_map/all_to_all | solution.py:382
  16.4 0.2 turn.1
  16.6 5.0 %collective-permute-start = (f32[7,32,384]{2,1,0:T(8,128)S(1)}, f32[7,32,384]{2,1,0:T(8,128)S(1)}, u32[]{:S(2)}, u32[]{:S(2)}) collective-permute-start(f32[7,32,384]{2,1,0:T(8,128)S(1)} %get-tuple-element.11), channel_id=1, source_target_pairs={{0,1},{1,2},{2,3},{3,4},{4,5},{5,6},{6,7},{8,9},{9,10},{10,11},{11... | collective-permute-start | bytes 1032200 | tf_op jit(solution)/shard_map/ppermute | solution.py:413
  21.7 1.9 %collective-permute-start.1 = (f32[7,32,384]{2,1,0:T(8,128)S(1)}, f32[7,32,384]{2,1,0:T(8,128)S(1)}, u32[]{:S(2)}, u32[]{:S(2)}) collective-permute-start(f32[7,32,384]{2,1,0:T(8,128)S(1)} %get-tuple-element.12), channel_id=1, source_target_pairs={{1,0},{2,1},{3,2},{4,3},{5,4},{6,5},{7,6},{9,8},{10,9},{11,10},{12... | collective-permute-start | bytes 1032200 | tf_op jit(solution)/shard_map/ppermute | solution.py:414
  23.6 0.0 copy-start.6
  23.6 0.7 copy-done.6
  24.3 0.6 dynamic-slice
  25.5 0.0 copy-start.5
  25.6 0.6 copy-done.5
  26.2 0.2 dynamic-update-slice
  26.4 7.6 %all-reduce.1.mats_ref = s32[64]{0:T(128)S(1)} all-reduce(s32[64]{0:T(128)S(1)} %dynamic-update-slice), channel_id=1, replica_groups=mesh['gz'=8,'gx'=4,'gy'=8] {'gz'}, use_global_device_ids=true, to_apply=%add.1 | all-reduce | flops 64 | bytes 512
  34.0 0.0 collective-permute-done.above_ref
  34.0 0.1 collective-permute-done.1.below_ref
  34.1 1.9 %collective-permute-start.2 = (f32[22,8,384]{2,1,0:T(8,128)S(1)}, f32[22,8,384]{2,1,0:T(8,128)S(1)}, u32[]{:S(2)}, u32[]{:S(2)}) collective-permute-start(f32[22,8,384]{2,1,0:T(8,128)S(1)} %get-tuple-element.13), channel_id=1, source_target_pairs={{0,32},{32,64},{64,96},{96,128},{128,160},{160,192},{192,224},{224... | collective-permute-start | bytes 811016 | tf_op jit(solution)/shard_map/ppermute | solution.py:426
  36.1 5.8 %collective-permute-start.3 = (f32[22,8,384]{2,1,0:T(8,128)S(1)}, f32[22,8,384]{2,1,0:T(8,128)S(1)}, u32[]{:S(2)}, u32[]{:S(2)}) collective-permute-start(f32[22,8,384]{2,1,0:T(8,128)S(1)} %get-tuple-element.14), channel_id=1, source_target_pairs={{32,0},{64,32},{96,64},{128,96},{160,128},{192,160},{224,192},{8,2... | collective-permute-start | bytes 811016 | tf_op jit(solution)/shard_map/ppermute | solution.py:427
  41.8 0.1 multiply_reduce_fusion
  42.0 0.0 copy-start.4
  42.0 0.1 copy.11
  42.1 0.6 copy-done.4
  42.7 0.1 copy.10
  42.8 0.2 reshape.38.factor_ref
  43.0 4.9 %setup.1 = (bf16[2,192,1024]{2,1,0:T(8,128)(2,1)S(1)}, bf16[2,96,1024]{2,1,0:T(8,128)(2,1)S(1)}, bf16[2,256,512]{2,1,0:T(8,128)(2,1)S(1)}) custom-call(s32[64]{0:T(128)S(1)} %all-reduce.1.mats_ref, f32[216]{0:T(256)S(1)} %reshape.38.factor_ref, f32[64,128]{1,0:T(8,128)S(1)} %pad.4.sten_ref), custom_call_target="tpu_custom_call" | custom-call | tf_op jit(solution)/shard_map/setup/pallas_call | solution.py:387
  47.9 0.0 collective-permute-done.2.left_ref
  47.9 0.0 collective-permute-done.3.right_ref
  47.9 6.7 %cycle.1 = f32[8,96,128]{2,1,0:T(8,128)S(1)} custom-call(f32[8,32,384]{2,1,0:T(8,128)S(1)} %get-tuple-element.10.own_ref, f32[7,32,384]{2,1,0:T(8,128)S(1)} %collective-permute-done.above_ref, f32[7,32,384]{2,1,0:T(8,128)S(1)} %collective-permute-done.1.below_ref, f32[22,8,384]{2,1,0:T(8,128)S(1)} %collective-permute-done.2.left_ref, ...), custom_call_target="tpu_custom_call" | custom-call | tf_op jit(solution)/shard_map/cycle/pallas_call | solution.py:429
  54.6 0.0 copy-start.1
  54.6 12.1 %all_to_all.11 = f32[8,96,128]{2,1,0:T(8,128)S(1)} all-to-all(f32[8,96,128]{2,1,0:T(8,128)S(1)} %cycle.1), channel_id=1, replica_groups=mesh['gz'=8,'gx'=4,'gy'=8] {'gz'}, dimensions={0} | all-to-all | bytes 786432 | tf_op jit(solution)/shard_map/all_to_all | solution.py:448
  66.8 1.5 %unpack.1 = (f32[8,3,8,256]{3,2,1,0:T(8,128)}, f32[8,3,8,256]{3,2,1,0:T(8,128)}) custom-call(f32[768,128]{1,0:T(8,128)S(1)} %bitcast.5, f32[8,3,8,256]{3,2,1,0:T(8,128)S(1)} %copy-done.1), custom_call_target="tpu_custom_call" | custom-call | tf_op jit(solution)/shard_map/unpack/pallas_call | solution.py:449
  (9 shorter events, 0.1 us)
Async XLA Ops:
  0.6 0.9 %copy-start = (f32[8,3,8,256]{3,2,1,0:T(8,128)S(1)}, f32[8,3,8,256]{3,2,1,0:T(8,128)}, u32[]{:S(2)}) copy-start(f32[8,3,8,256]{3,2,1,0:T(8,128)} %start_ref.3) | copy-start | bytes 589828
  1.6 0.9 %copy-start.2 = (f32[8,3,8,256]{3,2,1,0:T(8,128)S(1)}, f32[8,3,8,256]{3,2,1,0:T(8,128)}, u32[]{:S(2)}) copy-start(f32[8,3,8,256]{3,2,1,0:T(8,128)} %load_ref.1) | copy-start | bytes 589828
  16.4 7.2 %copy-start.3 = (f32[8,3,3,3]{0,3,2,1:T(4,128)S(1)}, f32[8,3,3,3]{0,3,2,1:T(4,128)}, u32[]{:S(2)}) copy-start(f32[8,3,3,3]{0,3,2,1:T(4,128)} %param.8) | copy-start | bytes 2596
  16.6 17.4 %collective-permute-start = (f32[7,32,384]{2,1,0:T(8,128)S(1)}, f32[7,32,384]{2,1,0:T(8,128)S(1)}, u32[]{:S(2)}, u32[]{:S(2)}) collective-permute-start(f32[7,32,384]{2,1,0:T(8,128)S(1)} %get-tuple-element.11), channel_id=1, source_target_pairs={{0,1},{1,2},{2,3},{3,4},{4,5},{5,6},{6,7},{8,9},{9,10},{10,11},{11... | collective-permute-start | bytes 1032200 | tf_op jit(solution)/shard_map/ppermute | solution.py:413
  21.7 12.4 %collective-permute-start.1 = (f32[7,32,384]{2,1,0:T(8,128)S(1)}, f32[7,32,384]{2,1,0:T(8,128)S(1)}, u32[]{:S(2)}, u32[]{:S(2)}) collective-permute-start(f32[7,32,384]{2,1,0:T(8,128)S(1)} %get-tuple-element.12), channel_id=1, source_target_pairs={{1,0},{2,1},{3,2},{4,3},{5,4},{6,5},{7,6},{9,8},{10,9},{11,10},{12... | collective-permute-start | bytes 1032200 | tf_op jit(solution)/shard_map/ppermute | solution.py:414
  23.6 0.7 copy-start.6
  25.5 0.7 copy-start.5
  34.1 13.8 %collective-permute-start.2 = (f32[22,8,384]{2,1,0:T(8,128)S(1)}, f32[22,8,384]{2,1,0:T(8,128)S(1)}, u32[]{:S(2)}, u32[]{:S(2)}) collective-permute-start(f32[22,8,384]{2,1,0:T(8,128)S(1)} %get-tuple-element.13), channel_id=1, source_target_pairs={{0,32},{32,64},{64,96},{96,128},{128,160},{160,192},{192,224},{224... | collective-permute-start | bytes 811016 | tf_op jit(solution)/shard_map/ppermute | solution.py:426
  36.1 11.9 %collective-permute-start.3 = (f32[22,8,384]{2,1,0:T(8,128)S(1)}, f32[22,8,384]{2,1,0:T(8,128)S(1)}, u32[]{:S(2)}, u32[]{:S(2)}) collective-permute-start(f32[22,8,384]{2,1,0:T(8,128)S(1)} %get-tuple-element.14), channel_id=1, source_target_pairs={{32,0},{64,32},{96,64},{128,96},{160,128},{192,160},{224,192},{8,2... | collective-permute-start | bytes 811016 | tf_op jit(solution)/shard_map/ppermute | solution.py:427
  42.0 0.7 %copy-start.4 = (f32[8,3,3,3]{0,3,2,1:T(4,128)S(1)}, f32[8,3,3,3]{0,3,2,1:T(4,128)}, u32[]{:S(2)}) copy-start(f32[8,3,3,3]{0,3,2,1:T(4,128)} %param.9) | copy-start | bytes 2596
  54.6 12.1 %copy-start.1 = (f32[8,3,8,256]{3,2,1,0:T(8,128)S(1)}, f32[8,3,8,256]{3,2,1,0:T(8,128)}, u32[]{:S(2)}) copy-start(f32[8,3,8,256]{3,2,1,0:T(8,128)} %start_ref.3) | copy-start | bytes 589828

commit v2 on v1

--- a/solution.py
+++ b/solution.py
@@ -13,9 +13,11 @@
 XW = XT + 2 * XH
 YT = 8
 YW = YT + 2 * HALO
+ROWS = 104
 NZ = 64
 NC = NZ // 2
 VMEM = pl.BlockSpec(memory_space=pltpu.VMEM)
+HBM = pl.BlockSpec(memory_space=pltpu.HBM)
 SMEM = pl.BlockSpec(memory_space=pltpu.SMEM)
 
 
@@ -35,18 +37,39 @@
     return tile
 
 
-def pack_kernel(load_ref, start_ref, out_ref):
-    for f, ref in enumerate((load_ref, start_ref)):
-        for c in range(3):
-            tile = swap_blocks(ref[:, c])
-            for z in range(8):
-                for h in range(2):
-                    at = h * 48 + f * 24 + c * 8 + z
-                    out_ref[pl.ds(at, 8, stride=96), :] = tile[z, :, h * 128 : h * 128 + 128]
-
-
-def unpack_kernel(got_ref, start_ref, field_ref, resid_ref):
-    for f, ref in enumerate((field_ref, resid_ref)):
+def fetches(pairs, sems):
+    copies = [pltpu.make_async_copy(src, dst, sems.at[i]) for i, (src, dst) in enumerate(pairs)]
+    for copy in copies:
+        copy.start()
+    return copies
+
+
+def pack_kernel(load_hbm, start_hbm, mats_hbm, out_ref, in_ref, mats_ref, sems, mats_sem):
+    mats_copy = pltpu.make_async_copy(mats_hbm, mats_ref, mats_sem)
+    mats_copy.start()
+    order = [(f, c) for f in range(2) for c in range(3)]
+    copies = fetches(
+        [((load_hbm, start_hbm)[f].at[:, c], in_ref.at[i]) for i, (f, c) in enumerate(order)], sems
+    )
+    for i, (f, c) in enumerate(order):
+        copies[i].wait()
+        tile = swap_blocks(in_ref[i])
+        for z in range(8):
+            for h in range(2):
+                at = h * 48 + f * 24 + c * 8 + z
+                out_ref[pl.ds(at, 8, stride=ROWS), :] = tile[z, :, h * 128 : h * 128 + 128]
+    mats_copy.wait()
+    lane = lax.broadcasted_iota(jnp.int32, (8, 128), 1)
+    ids = jnp.zeros((8, 128), jnp.int32)
+    for z in range(8):
+        ids = jnp.where(lane == z, mats_ref[z], ids)
+    for k in range(8):
+        out_ref[k * ROWS + 96 : k * ROWS + 104, :] = ids.astype(F32)
+
+
+def unpack_kernel(got_ref, start_ref, field_hbm, resid_hbm, out_ref, sems):
+    copies = []
+    for f, ref in enumerate((field_hbm, resid_hbm)):
         for c in range(3):
             halves = []
             for h in range(2):
@@ -56,7 +79,13 @@
             tile = swap_blocks(jnp.concatenate(halves, axis=2))
             if f == 0:
                 tile = tile + start_ref[:, c]
-            ref[:, c] = tile
+            i = f * 3 + c
+            out_ref[i] = tile
+            copy = pltpu.make_async_copy(out_ref.at[i], ref.at[:, c], sems.at[i])
+            copy.start()
+            copies.append(copy)
+    for copy in copies:
+        copy.wait()
 
 
 def turn_kernel(got_ref, own_ref, low_ref, high_ref):
@@ -70,7 +99,7 @@
     high_ref[...] = turned[YT - HALO :]
 
 
-def sides_kernel(own_ref, above_ref, below_ref, left_ref, right_ref):
+def sides_kernel(own_ref, above_ref, below_ref, after_ref, left_ref, right_ref):
     for ref, cols in ((left_ref, slice(0, XH)), (right_ref, slice(XT - XH, XT))):
         ref[0:HALO] = above_ref[:, cols]
         ref[HALO : HALO + YT] = own_ref[:, cols]
@@ -370,16 +399,22 @@
 
 def on_device(right_side, start_field, layer_material, stiffness, line_factors):
     size_y = lax.axis_size("gy")
-    mats = lax.all_gather(layer_material, "gz", axis=0, tiled=True)
     packed = pl.pallas_call(
         pack_kernel,
-        out_shape=shape(768, 128),
-        in_specs=[VMEM, VMEM],
+        out_shape=shape(8 * ROWS, 128),
+        in_specs=[HBM, HBM, HBM],
         out_specs=VMEM,
+        scratch_shapes=[
+            pltpu.VMEM((6, 8, 8, 256), F32),
+            pltpu.SMEM((8,), jnp.int32),
+            pltpu.SemaphoreType.DMA((6,)),
+            pltpu.SemaphoreType.DMA,
+        ],
         compiler_params=params(),
         name="pack",
-    )(right_side, start_field)
-    got = lax.all_to_all(packed.reshape(8, 96, 128), "gz", 0, 0, tiled=True)
+    )(right_side, start_field, layer_material)
+    got = lax.all_to_all(packed.reshape(8, ROWS, 128), "gz", 0, 0, tiled=True)
+    mats = got[:, 96, :8].reshape(-1).astype(jnp.int32)
 
     onehot = (mats[:, None] == jnp.arange(stiffness.shape[0])[None, :]).astype(F32)
     sten = jnp.sum(onehot[:, :, None] * stiffness.reshape(1, -1, 27), axis=1)
@@ -415,11 +450,11 @@
     to_left, to_right = pl.pallas_call(
         sides_kernel,
         out_shape=(shape(YW, XH, 384), shape(YW, XH, 384)),
-        in_specs=[VMEM, VMEM, VMEM],
+        in_specs=[VMEM, VMEM, VMEM, pl.BlockSpec(memory_space=pl.ANY)],
         out_specs=(VMEM, VMEM),
         compiler_params=params(),
         name="sides",
-    )(own, above, below)
+    )(own, above, below, fine)
     count_x, count_z = lax.axis_size("gx"), lax.axis_size("gz")
     along = [(i % count_z) * count_x + i // count_z for i in range(count_x * count_z)]
     ahead = list(zip(along[:-1], along[1:]))
@@ -450,7 +485,8 @@
         unpack_kernel,
         out_shape=(shape(8, 3, 8, 256), shape(8, 3, 8, 256)),
         in_specs=[VMEM, VMEM],
-        out_specs=(VMEM, VMEM),
+        out_specs=(HBM, HBM),
+        scratch_shapes=[pltpu.VMEM((6, 8, 8, 256), F32), pltpu.SemaphoreType.DMA((6,))],
         compiler_params=params(),
         name="unpack",
     )(back.reshape(768, 128), start_field)

time: 68.8 us -> 71.3 us (1.036)
  blocking collectives: 32.8 us -> 14.3 us
  waiting for transfers between devices: 0.08 us -> 17.5 us
  starting transfers between devices: 14.6 us -> 18.9 us
  local copies, waits for them, and re-layouts: 4.96 us -> 3.69 us
  Pallas kernels: 14.3 us -> 15.5 us
    all_to_all x1 -> x0, blocking collectives: 13 us -> none  [on_device(): got = lax.all_to_all(packed.reshape(8, 96, 128), 'gz', 0, 0, tiled=True)]
    all_to_all x0 -> x1, waiting for transfers between devices: none -> 8.27 us  [on_device(): got = lax.all_to_all(packed.reshape(8, ROWS, 128), 'gz', 0, 0, tiled=True)]
    unnamed x1 -> x0, blocking collectives: 7.63 us -> none
    ppermute x1, waiting for transfers between devices: 0.08 us -> 5.24 us  [on_device(): below = lax.ppermute(low, 'gy', [(b, a) for a, b in ahead])]
    all_to_all x0 -> x1, starting transfers between devices: none -> 4.31 us  [on_device(): got = lax.all_to_all(packed.reshape(8, ROWS, 128), 'gz', 0, 0, tiled=True)]
    ppermute x1, waiting for transfers between devices: 0.01 us -> 2.2 us  [on_device(): left = lax.ppermute(to_right, ('gz', 'gx'), ahead)]
    all_to_all x1, blocking collectives: 12.1 us -> 14.3 us  [on_device(): back = lax.all_to_all(out, 'gz', 0, 0, tiled=True)]
    ppermute x1, waiting for transfers between devices: 0.01 us -> 1.76 us  [on_device(): right = lax.ppermute(to_left, ('gz', 'gx'), [(b, a) for a, b in ahead])]
  transfers between devices with their start and end apart: 4 -> 5, of which waited for: 1 -> 4; matrix products, arithmetic and copies ran while one was open for 2% -> 1% of each run, Pallas kernels for 7% -> 7%
where the time goes in v2:
time: 71.3 us; the launch traced here: 70.8 us
  starting transfers between devices  18.9 us (27%)
  waiting for transfers between devices  17.5 us (25%)
  Pallas kernels  15.5 us (22%)
  blocking collectives  14.3 us (20%)
  local copies, waits for them, and re-layouts  3.69 us (5%)
  between operations  0.76 us (1%)
    all_to_all x1, blocking collectives, on_device(): back = lax.all_to_all(out, 'gz', 0, 0, tiled=True)  14.3 us
    all_to_all x1, waiting for transfers between devices, on_device(): got = lax.all_to_all(packed.reshape(8, ROWS, 128), 'gz', 0, 0, tiled=True)  8.27 us
    pallas_call x1, Pallas kernels, on_device(): pl.pallas_call(cycle_kernel, out_shape=shape(8, 96, 128), in_specs=[VMEM]...  6.72 us
    ppermute x1, starting transfers between devices, on_device(): right = lax.ppermute(to_left, ('gz', 'gx'), [(b, a) for a, b in ahead])  5.75 us
    ppermute x1, waiting for transfers between devices, on_device(): below = lax.ppermute(low, 'gy', [(b, a) for a, b in ahead])  5.24 us
    ppermute x1, starting transfers between devices, on_device(): above = lax.ppermute(high, 'gy', ahead)  5.04 us
    pallas_call x1, Pallas kernels, on_device(): pl.pallas_call(setup_kernel, out_shape=(shape(2, 192, 1024, dtype=BF16),...  4.92 us
    all_to_all x1, starting transfers between devices, on_device(): got = lax.all_to_all(packed.reshape(8, ROWS, 128), 'gz', 0, 0, tiled=True)  4.31 us
  transfers between devices with their start and end apart: 5, of which 4 were waited for; matrix products, arithmetic and copies ran while one was open for 1% of the time, Pallas kernels for 7%

profile of v2, /device:TPU:104, one launch (start us, length us, event | category | flops | bytes accessed | tf_op | source)
XLA Modules:
  0.0 70.8 jit_solution(17598795109663340018)
XLA Ops:
  0.6 0.0 copy-start
  0.6 0.9 %copy-done = f32[8,3,8,256]{3,2,1,0:T(8,128)S(1)} copy-done((f32[8,3,8,256]{3,2,1,0:T(8,128)S(1)}, f32[8,3,8,256]{3,2,1,0:T(8,128)}, u32[]{:S(2)}) %copy-start) | copy-done | bytes 196632
  1.6 0.0 copy-start.2
  1.6 0.9 %copy-done.2 = f32[8,3,8,256]{3,2,1,0:T(8,128)S(1)} copy-done((f32[8,3,8,256]{3,2,1,0:T(8,128)S(1)}, f32[8,3,8,256]{3,2,1,0:T(8,128)}, u32[]{:S(2)}) %copy-start.2) | copy-done | bytes 196632
  2.5 0.7 copy-done.3
  3.1 2.1 %pack.1 = f32[832,128]{1,0:T(8,128)} custom-call(f32[8,3,8,256]{3,2,1,0:T(8,128)S(1)} %copy-done.2, f32[8,3,8,256]{3,2,1,0:T(8,128)S(1)} %copy-done, s32[8]{0:T(128)S(1)} %copy-done.3), custom_call_target="tpu_custom_call" | custom-call | tf_op jit(solution)/shard_map/pack/pallas_call | solution.py:402
  5.3 0.0 copy-start.4
  5.3 4.3 %all-to-all-start = ((f32[8,104,128]{2,1,0:T(8,128)}), f32[8,104,128]{2,1,0:T(8,128)S(1)}, u32[]{:S(2)}, u32[]{:S(2)}) async-start(f32[8,104,128]{2,1,0:T(8,128)} %bitcast), calls=%async_computation | async-start | bytes 851968 | tf_op jit(solution)/shard_map/all_to_all | solution.py:416
  9.6 0.0 copy-done.4
  9.6 0.0 copy-start.5
  9.6 0.7 copy-done.5
  10.3 0.1 copy.10
  10.5 0.2 reshape.43.factor_ref
  10.6 8.3 %all-to-all-done.got_ref = f32[8,104,128]{2,1,0:T(8,128)S(1)} async-done(((f32[8,104,128]{2,1,0:T(8,128)}), f32[8,104,128]{2,1,0:T(8,128)S(1)}, u32[]{:S(2)}, u32[]{:S(2)}) %all-to-all-start) | async-done | bytes 426016 | tf_op jit(solution)/shard_map/all_to_all | solution.py:416
  18.9 0.2 turn.1
  19.1 5.0 %collective-permute-start = (f32[7,32,384]{2,1,0:T(8,128)S(1)}, f32[7,32,384]{2,1,0:T(8,128)S(1)}, u32[]{:S(2)}, u32[]{:S(2)}) collective-permute-start(f32[7,32,384]{2,1,0:T(8,128)S(1)} %get-tuple-element.11), channel_id=1, source_target_pairs={{0,1},{1,2},{2,3},{3,4},{4,5},{5,6},{6,7},{8,9},{9,10},{10,11},{11... | collective-permute-start | bytes 1032200 | tf_op jit(solution)/shard_map/ppermute | solution.py:448
  24.1 1.9 %collective-permute-start.1 = (f32[7,32,384]{2,1,0:T(8,128)S(1)}, f32[7,32,384]{2,1,0:T(8,128)S(1)}, u32[]{:S(2)}, u32[]{:S(2)}) collective-permute-start(f32[7,32,384]{2,1,0:T(8,128)S(1)} %get-tuple-element.12), channel_id=1, source_target_pairs={{1,0},{2,1},{3,2},{4,3},{5,4},{6,5},{7,6},{9,8},{10,9},{11,10},{12... | collective-permute-start | bytes 1032200 | tf_op jit(solution)/shard_map/ppermute | solution.py:449
  26.1 0.1 convert_element_type.15.mats_ref
  26.1 0.1 multiply_reduce_fusion
  26.3 0.1 copy.11
  26.4 4.9 %setup.1 = (bf16[2,192,1024]{2,1,0:T(8,128)(2,1)S(1)}, bf16[2,96,1024]{2,1,0:T(8,128)(2,1)S(1)}, bf16[2,256,512]{2,1,0:T(8,128)(2,1)S(1)}) custom-call(s32[64]{0:T(128)S(1)} %convert_element_type.15.mats_ref, f32[216]{0:T(256)S(1)} %reshape.43.factor_ref, f32[64,128]{1,0:T(8,128)S(1)} %pad.4.sten_ref), custom_call_target="tpu_custom_call" | custom-call | tf_op jit(solution)/shard_map/setup/pallas_call | solution.py:422
  31.3 0.0 collective-permute-done.above_ref
  31.3 5.2 %collective-permute-done.1.below_ref = f32[7,32,384]{2,1,0:T(8,128)S(1)} collective-permute-done((f32[7,32,384]{2,1,0:T(8,128)S(1)}, f32[7,32,384]{2,1,0:T(8,128)S(1)}, u32[]{:S(2)}, u32[]{:S(2)}) %collective-permute-start.1) | collective-permute-done | bytes 344096 | tf_op jit(solution)/shard_map/ppermute | solution.py:449
  36.6 1.9 %collective-permute-start.2 = (f32[22,8,384]{2,1,0:T(8,128)S(1)}, f32[22,8,384]{2,1,0:T(8,128)S(1)}, u32[]{:S(2)}, u32[]{:S(2)}) collective-permute-start(f32[22,8,384]{2,1,0:T(8,128)S(1)} %get-tuple-element.14), channel_id=1, source_target_pairs={{0,32},{32,64},{64,96},{96,128},{128,160},{160,192},{192,224},{224... | collective-permute-start | bytes 811016 | tf_op jit(solution)/shard_map/ppermute | solution.py:461
  38.5 5.8 %collective-permute-start.3 = (f32[22,8,384]{2,1,0:T(8,128)S(1)}, f32[22,8,384]{2,1,0:T(8,128)S(1)}, u32[]{:S(2)}, u32[]{:S(2)}) collective-permute-start(f32[22,8,384]{2,1,0:T(8,128)S(1)} %get-tuple-element.15), channel_id=1, source_target_pairs={{32,0},{64,32},{96,64},{128,96},{160,128},{192,160},{224,192},{8,2... | collective-permute-start | bytes 811016 | tf_op jit(solution)/shard_map/ppermute | solution.py:462
  44.3 2.2 %collective-permute-done.2.left_ref = f32[22,8,384]{2,1,0:T(8,128)S(1)} collective-permute-done((f32[22,8,384]{2,1,0:T(8,128)S(1)}, f32[22,8,384]{2,1,0:T(8,128)S(1)}, u32[]{:S(2)}, u32[]{:S(2)}) %collective-permute-start.2) | collective-permute-done | bytes 270368 | tf_op jit(solution)/shard_map/ppermute | solution.py:461
  46.5 1.8 %collective-permute-done.3.right_ref = f32[22,8,384]{2,1,0:T(8,128)S(1)} collective-permute-done((f32[22,8,384]{2,1,0:T(8,128)S(1)}, f32[22,8,384]{2,1,0:T(8,128)S(1)}, u32[]{:S(2)}, u32[]{:S(2)}) %collective-permute-start.3) | collective-permute-done | bytes 270368 | tf_op jit(solution)/shard_map/ppermute | solution.py:462
  48.2 6.7 %cycle.1 = f32[8,96,128]{2,1,0:T(8,128)S(1)} custom-call(f32[8,32,384]{2,1,0:T(8,128)S(1)} %get-tuple-element.10.own_ref, f32[7,32,384]{2,1,0:T(8,128)S(1)} %collective-permute-done.above_ref, f32[7,32,384]{2,1,0:T(8,128)S(1)} %collective-permute-done.1.below_ref, f32[22,8,384]{2,1,0:T(8,128)S(1)} %collective-permute-done.2.left_ref, ...), custom_call_target="tpu_custom_call" | custom-call | tf_op jit(solution)/shard_map/cycle/pallas_call | solution.py:464
  54.9 0.0 copy-start.1
  54.9 14.3 %all_to_all.10 = f32[8,96,128]{2,1,0:T(8,128)S(1)} all-to-all(f32[8,96,128]{2,1,0:T(8,128)S(1)} %cycle.1), channel_id=1, replica_groups=mesh['gz'=8,'gx'=4,'gy'=8] {'gz'}, dimensions={0} | all-to-all | bytes 786432 | tf_op jit(solution)/shard_map/all_to_all | solution.py:483
  69.2 0.0 copy-done.1
  69.2 1.5 %unpack.1 = (f32[8,3,8,256]{3,2,1,0:T(8,128)}, f32[8,3,8,256]{3,2,1,0:T(8,128)}) custom-call(f32[768,128]{1,0:T(8,128)S(1)} %bitcast.4, f32[8,3,8,256]{3,2,1,0:T(8,128)S(1)} %copy-done.1), custom_call_target="tpu_custom_call" | custom-call | tf_op jit(solution)/shard_map/unpack/pallas_call | solution.py:484
  (6 shorter events, 0.1 us)
Async XLA Ops:
  0.6 0.9 %copy-start = (f32[8,3,8,256]{3,2,1,0:T(8,128)S(1)}, f32[8,3,8,256]{3,2,1,0:T(8,128)}, u32[]{:S(2)}) copy-start(f32[8,3,8,256]{3,2,1,0:T(8,128)} %start_ref.1) | copy-start | bytes 589828
  1.6 0.9 %copy-start.2 = (f32[8,3,8,256]{3,2,1,0:T(8,128)S(1)}, f32[8,3,8,256]{3,2,1,0:T(8,128)}, u32[]{:S(2)}) copy-start(f32[8,3,8,256]{3,2,1,0:T(8,128)} %load_hbm.1) | copy-start | bytes 589828
  2.5 0.7 copy-start.3
  5.3 4.3 %copy-start.4 = (f32[8,3,3,3]{0,3,2,1:T(4,128)S(1)}, f32[8,3,3,3]{0,3,2,1:T(4,128)}, u32[]{:S(2)}) copy-start(f32[8,3,3,3]{0,3,2,1:T(4,128)} %param.8) | copy-start | bytes 2596
  5.3 13.6 %all-to-all-start = ((f32[8,104,128]{2,1,0:T(8,128)}), f32[8,104,128]{2,1,0:T(8,128)S(1)}, u32[]{:S(2)}, u32[]{:S(2)}) async-start(f32[8,104,128]{2,1,0:T(8,128)} %bitcast), calls=%async_computation | async-start | bytes 851968 | tf_op jit(solution)/shard_map/all_to_all | solution.py:416
  9.6 0.7 %copy-start.5 = (f32[8,3,3,3]{0,3,2,1:T(4,128)S(1)}, f32[8,3,3,3]{0,3,2,1:T(4,128)}, u32[]{:S(2)}) copy-start(f32[8,3,3,3]{0,3,2,1:T(4,128)} %param.9) | copy-start | bytes 2596
  19.1 12.2 %collective-permute-start = (f32[7,32,384]{2,1,0:T(8,128)S(1)}, f32[7,32,384]{2,1,0:T(8,128)S(1)}, u32[]{:S(2)}, u32[]{:S(2)}) collective-permute-start(f32[7,32,384]{2,1,0:T(8,128)S(1)} %get-tuple-element.11), channel_id=1, source_target_pairs={{0,1},{1,2},{2,3},{3,4},{4,5},{5,6},{6,7},{8,9},{9,10},{10,11},{11... | collective-permute-start | bytes 1032200 | tf_op jit(solution)/shard_map/ppermute | solution.py:448
  24.1 12.4 %collective-permute-start.1 = (f32[7,32,384]{2,1,0:T(8,128)S(1)}, f32[7,32,384]{2,1,0:T(8,128)S(1)}, u32[]{:S(2)}, u32[]{:S(2)}) collective-permute-start(f32[7,32,384]{2,1,0:T(8,128)S(1)} %get-tuple-element.12), channel_id=1, source_target_pairs={{1,0},{2,1},{3,2},{4,3},{5,4},{6,5},{7,6},{9,8},{10,9},{11,10},{12... | collective-permute-start | bytes 1032200 | tf_op jit(solution)/shard_map/ppermute | solution.py:449
  36.6 9.9 %collective-permute-start.2 = (f32[22,8,384]{2,1,0:T(8,128)S(1)}, f32[22,8,384]{2,1,0:T(8,128)S(1)}, u32[]{:S(2)}, u32[]{:S(2)}) collective-permute-start(f32[22,8,384]{2,1,0:T(8,128)S(1)} %get-tuple-element.14), channel_id=1, source_target_pairs={{0,32},{32,64},{64,96},{96,128},{128,160},{160,192},{192,224},{224... | collective-permute-start | bytes 811016 | tf_op jit(solution)/shard_map/ppermute | solution.py:461
  38.5 9.7 %collective-permute-start.3 = (f32[22,8,384]{2,1,0:T(8,128)S(1)}, f32[22,8,384]{2,1,0:T(8,128)S(1)}, u32[]{:S(2)}, u32[]{:S(2)}) collective-permute-start(f32[22,8,384]{2,1,0:T(8,128)S(1)} %get-tuple-element.15), channel_id=1, source_target_pairs={{32,0},{64,32},{96,64},{128,96},{160,128},{192,160},{224,192},{8,2... | collective-permute-start | bytes 811016 | tf_op jit(solution)/shard_map/ppermute | solution.py:462
  54.9 14.3 %copy-start.1 = (f32[8,3,8,256]{3,2,1,0:T(8,128)S(1)}, f32[8,3,8,256]{3,2,1,0:T(8,128)}, u32[]{:S(2)}) copy-start(f32[8,3,8,256]{3,2,1,0:T(8,128)} %start_ref.1) | copy-start | bytes 589828

commit v3 on v2

--- a/solution.py
+++ b/solution.py
@@ -21,8 +21,8 @@
 SMEM = pl.BlockSpec(memory_space=pltpu.SMEM)
 
 
-def params():
-    return pltpu.CompilerParams(vmem_limit_bytes=40 * 1024 * 1024)
+def params(mib=40):
+    return pltpu.CompilerParams(vmem_limit_bytes=mib * 1024 * 1024)
 
 
 def swap_blocks(tile):
@@ -88,22 +88,21 @@
         copy.wait()
 
 
-def turn_kernel(got_ref, own_ref, low_ref, high_ref):
+def turn_kernel(got_ref, own_ref, low_ref, high_ref, *side_refs):
+    left_refs, right_refs = side_refs[:3], side_refs[3:]
     halves = []
     for h in range(2):
         rows = [got_ref[g, h * 48 + q * 8 : h * 48 + q * 8 + 8] for q in range(6) for g in range(8)]
         halves.append(jnp.transpose(jnp.concatenate(rows, axis=0)))
     turned = jnp.concatenate(halves, axis=0).reshape(YT, XT, 384)
     own_ref[...] = turned
-    low_ref[...] = turned[:HALO]
-    high_ref[...] = turned[YT - HALO :]
-
-
-def sides_kernel(own_ref, above_ref, below_ref, after_ref, left_ref, right_ref):
-    for ref, cols in ((left_ref, slice(0, XH)), (right_ref, slice(XT - XH, XT))):
-        ref[0:HALO] = above_ref[:, cols]
-        ref[HALO : HALO + YT] = own_ref[:, cols]
-        ref[HALO + YT :] = below_ref[:, cols]
+    low, high = turned[:HALO], turned[YT - HALO :]
+    for ref, value in ((low_ref, low), (high_ref, high)):
+        ref[...] = value
+    for refs, value in ((left_refs, (turned, low, high)), (right_refs, (turned, low, high))):
+        cols = slice(0, XH) if refs is left_refs else slice(XT - XH, XT)
+        for ref, part in zip(refs, value):
+            ref[...] = part[:, cols]
 
 
 def split(value):
@@ -251,7 +250,11 @@
     above_ref,
     below_ref,
     left_ref,
+    left_above_ref,
+    left_below_ref,
     right_ref,
+    right_above_ref,
+    right_below_ref,
     fine_ref,
     coarse_ref,
     first_ref,
@@ -272,8 +275,13 @@
     at_top = gy == 0
     at_bottom = gy == lax.axis_size("gy") - 1
 
-    x_ref[:, 0:XH] = left_ref[...]
-    x_ref[:, XH + XT :] = right_ref[...]
+    for cols, refs in (
+        (slice(0, XH), (left_above_ref, left_ref, left_below_ref)),
+        (slice(XH + XT, XW), (right_above_ref, right_ref, right_below_ref)),
+    ):
+        x_ref[0:HALO, cols] = refs[0][...]
+        x_ref[HALO : HALO + YT, cols] = refs[1][...]
+        x_ref[HALO + YT :, cols] = refs[2][...]
     x_ref[0:HALO, XH : XH + XT] = above_ref[...]
     x_ref[HALO : HALO + YT, XH : XH + XT] = own_ref[...]
     x_ref[HALO + YT :, XH : XH + XT] = below_ref[...]
@@ -410,7 +418,7 @@
             pltpu.SemaphoreType.DMA((6,)),
             pltpu.SemaphoreType.DMA,
         ],
-        compiler_params=params(),
+        compiler_params=params(60),
         name="pack",
     )(right_side, start_field, layer_material)
     got = lax.all_to_all(packed.reshape(8, ROWS, 128), "gz", 0, 0, tiled=True)
@@ -436,35 +444,39 @@
         name="setup",
     )(mats, line_factors.reshape(-1), sten)
 
-    own, low, high = pl.pallas_call(
+    side = (shape(YT, XH, 384), shape(HALO, XH, 384), shape(HALO, XH, 384))
+    own, low, high, *sides = pl.pallas_call(
         turn_kernel,
-        out_shape=(shape(YT, XT, 384), shape(HALO, XT, 384), shape(HALO, XT, 384)),
+        out_shape=(shape(YT, XT, 384), shape(HALO, XT, 384), shape(HALO, XT, 384), *side, *side),
         in_specs=[VMEM],
-        out_specs=(VMEM, VMEM, VMEM),
+        out_specs=(VMEM,) * 9,
         compiler_params=params(),
         name="turn",
     )(got)
-    ahead = [(i, i + 1) for i in range(size_y - 1)]
-    above = lax.ppermute(high, "gy", ahead)
-    below = lax.ppermute(low, "gy", [(b, a) for a, b in ahead])
-    to_left, to_right = pl.pallas_call(
-        sides_kernel,
-        out_shape=(shape(YW, XH, 384), shape(YW, XH, 384)),
-        in_specs=[VMEM, VMEM, VMEM, pl.BlockSpec(memory_space=pl.ANY)],
-        out_specs=(VMEM, VMEM),
-        compiler_params=params(),
-        name="sides",
-    )(own, above, below, fine)
-    count_x, count_z = lax.axis_size("gx"), lax.axis_size("gz")
-    along = [(i % count_z) * count_x + i // count_z for i in range(count_x * count_z)]
-    ahead = list(zip(along[:-1], along[1:]))
-    left = lax.ppermute(to_right, ("gz", "gx"), ahead)
-    right = lax.ppermute(to_left, ("gz", "gx"), [(b, a) for a, b in ahead])
+    lefts, rights = sides[:3], sides[3:]
+    count_z, count_x, count_y = (lax.axis_size(axis) for axis in ("gz", "gx", "gy"))
+
+    def sent(value, step_x, step_y):
+        pairs = []
+        for x in range(count_x * count_z):
+            for y in range(count_y):
+                if 0 <= x + step_x < count_x * count_z and 0 <= y + step_y < count_y:
+                    ends = [
+                        ((p % count_z) * count_x + p // count_z) * count_y + q
+                        for p, q in ((x, y), (x + step_x, y + step_y))
+                    ]
+                    pairs.append(tuple(ends))
+        return lax.ppermute(value, ("gz", "gx", "gy"), pairs)
+
+    above, below = sent(high, 0, 1), sent(low, 0, -1)
+    left_above, left_below = sent(rights[2], 1, 1), sent(rights[1], 1, -1)
+    right_above, right_below = sent(lefts[2], -1, 1), sent(lefts[1], -1, -1)
+    left, right = sent(rights[0], 1, 0), sent(lefts[0], -1, 0)
 
     out = pl.pallas_call(
         cycle_kernel,
         out_shape=shape(8, 96, 128),
-        in_specs=[VMEM] * 8,
+        in_specs=[VMEM] * 12,
         out_specs=VMEM,
         scratch_shapes=[
             pltpu.VMEM((YW, XW, 384), F32),
@@ -479,7 +491,20 @@
         ],
         compiler_params=params(),
         name="cycle",
-    )(own, above, below, left, right, fine, coarse, first)
+    )(
+        own,
+        above,
+        below,
+        left,
+        left_above,
+        left_below,
+        right,
+        right_above,
+        right_below,
+        fine,
+        coarse,
+        first,
+    )
     back = lax.all_to_all(out, "gz", 0, 0, tiled=True)
     return pl.pallas_call(
         unpack_kernel,

time: 71.3 us -> 74.7 us (1.048)
  starting transfers between devices: 18.9 us -> 33.8 us
  waiting for transfers between devices: 17.5 us -> 10 us
  blocking collectives: 14.3 us -> 11.5 us
  local copies, waits for them, and re-layouts: 3.69 us -> 1.19 us
  Pallas kernels: 15.5 us -> 16.3 us
    ppermute x4 -> x8, starting transfers between devices: 14.6 us -> 29.5 us  [sent(): return lax.ppermute(value, ('gz', 'gx', 'gy'), pairs)]
    ppermute x4 -> x8, waiting for transfers between devices: 9.2 us -> 1.72 us  [sent(): return lax.ppermute(value, ('gz', 'gx', 'gy'), pairs)]
    all_to_all x1, blocking collectives: 14.3 us -> 11.5 us  [on_device(): back = lax.all_to_all(out, 'gz', 0, 0, tiled=True)]
    unnamed x13 -> x7, local copies, waits for them, and re-layouts: 3.35 us -> 0.85 us
    pallas_call x1, Pallas kernels: 2.12 us -> 2.9 us  [on_device(): pl.pallas_call(pack_kernel, out_shape=shape(8 * ROWS, 128), in_specs=[HBM...]
  transfers between devices with their start and end apart: 5 -> 9, of which waited for: 4 -> 2; matrix products, arithmetic and copies ran while one was open for 1% -> 1% of each run, Pallas kernels for 7% -> 7%
where the time goes in v3:
time: 74.7 us; the launch traced here: 73.7 us
  starting transfers between devices  33.8 us (45%)
  Pallas kernels  16.3 us (22%)
  blocking collectives  11.5 us (15%)
  waiting for transfers between devices  10 us (13%)
  local copies, waits for them, and re-layouts  1.19 us (2%)
  between operations  0.83 us (1%)
    ppermute x8, starting transfers between devices, sent(): return lax.ppermute(value, ('gz', 'gx', 'gy'), pairs)  29.5 us
    all_to_all x1, blocking collectives, on_device(): back = lax.all_to_all(out, 'gz', 0, 0, tiled=True)  11.5 us
    all_to_all x1, waiting for transfers between devices, on_device(): got = lax.all_to_all(packed.reshape(8, ROWS, 128), 'gz', 0, 0, tiled=True)  8.27 us
    pallas_call x1, Pallas kernels, on_device(): pl.pallas_call(cycle_kernel, out_shape=shape(8, 96, 128), in_specs=[VMEM]...  6.79 us
    pallas_call x1, Pallas kernels, on_device(): pl.pallas_call(setup_kernel, out_shape=(shape(2, 192, 1024, dtype=BF16),...  4.92 us
    all_to_all x1, starting transfers between devices, on_device(): got = lax.all_to_all(packed.reshape(8, ROWS, 128), 'gz', 0, 0, tiled=True)  4.31 us
    pallas_call x1, Pallas kernels, on_device(): pl.pallas_call(pack_kernel, out_shape=shape(8 * ROWS, 128), in_specs=[HBM...  2.9 us
    ppermute x8, waiting for transfers between devices, sent(): return lax.ppermute(value, ('gz', 'gx', 'gy'), pairs)  1.72 us
  transfers between devices with their start and end apart: 9, of which 2 were waited for; matrix products, arithmetic and copies ran while one was open for 1% of the time, Pallas kernels for 7%

profile of v3, /device:TPU:104, one launch (start us, length us, event | category | flops | bytes accessed | tf_op | source)
XLA Modules:
  0.0 73.7 jit_solution(8908113443648778997)
XLA Ops:
  0.6 2.9 %pack.1 = f32[832,128]{1,0:T(8,128)} custom-call(f32[8,3,8,256]{3,2,1,0:T(8,128)} %load_hbm.1, f32[8,3,8,256]{3,2,1,0:T(8,128)} %start_ref.1, s32[8]{0:T(128)} %mats_hbm.1), custom_call_target="tpu_custom_call" | custom-call | tf_op jit(solution)/shard_map/pack/pallas_call | solution.py:410
  3.5 0.0 copy-start.1
  3.5 4.3 %all-to-all-start = ((f32[8,104,128]{2,1,0:T(8,128)}), f32[8,104,128]{2,1,0:T(8,128)S(1)}, u32[]{:S(2)}, u32[]{:S(2)}) async-start(f32[8,104,128]{2,1,0:T(8,128)} %bitcast.5), calls=%async_computation | async-start | bytes 851968 | tf_op jit(solution)/shard_map/all_to_all | solution.py:424
  7.9 0.0 copy-start.2
  7.9 0.7 copy-done.2
  8.6 0.1 copy.10
  8.7 0.2 reshape.43.factor_ref
  8.9 8.3 %all-to-all-done.got_ref = f32[8,104,128]{2,1,0:T(8,128)S(1)} async-done(((f32[8,104,128]{2,1,0:T(8,128)}), f32[8,104,128]{2,1,0:T(8,128)S(1)}, u32[]{:S(2)}, u32[]{:S(2)}) %all-to-all-start) | async-done | bytes 426016 | tf_op jit(solution)/shard_map/all_to_all | solution.py:424
  17.2 0.1 convert_element_type.15.mats_ref
  17.3 0.2 turn.1
  17.4 4.3 %collective-permute-start.3 = (f32[7,8,384]{2,1,0:T(8,128)S(1)}, f32[7,8,384]{2,1,0:T(8,128)S(1)}, u32[]{:S(2)}, u32[]{:S(2)}) collective-permute-start(f32[7,8,384]{2,1,0:T(8,128)S(1)} %get-tuple-element.18), channel_id=1, source_target_pairs={{0,33},{1,34},{2,35},{3,36},{4,37},{5,38},{6,39},{32,65},{33,66},{... | collective-permute-start | bytes 258056 | tf_op jit(solution)/shard_map/ppermute | solution.py:469
  21.7 2.9 %collective-permute-start = (f32[7,32,384]{2,1,0:T(8,128)S(1)}, f32[7,32,384]{2,1,0:T(8,128)S(1)}, u32[]{:S(2)}, u32[]{:S(2)}) collective-permute-start(f32[7,32,384]{2,1,0:T(8,128)S(1)} %get-tuple-element.15), channel_id=1, source_target_pairs={{0,1},{1,2},{2,3},{3,4},{4,5},{5,6},{6,7},{32,33},{33,34},{34,35},... | collective-permute-start | bytes 1032200 | tf_op jit(solution)/shard_map/ppermute | solution.py:469
  24.7 2.9 %collective-permute-start.1 = (f32[7,32,384]{2,1,0:T(8,128)S(1)}, f32[7,32,384]{2,1,0:T(8,128)S(1)}, u32[]{:S(2)}, u32[]{:S(2)}) collective-permute-start(f32[7,32,384]{2,1,0:T(8,128)S(1)} %get-tuple-element.16), channel_id=1, source_target_pairs={{1,0},{2,1},{3,2},{4,3},{5,4},{6,5},{7,6},{33,32},{34,33},{35,34},... | collective-permute-start | bytes 1032200 | tf_op jit(solution)/shard_map/ppermute | solution.py:469
  27.6 2.1 %collective-permute-start.4 = (f32[7,8,384]{2,1,0:T(8,128)S(1)}, f32[7,8,384]{2,1,0:T(8,128)S(1)}, u32[]{:S(2)}, u32[]{:S(2)}) collective-permute-start(f32[7,8,384]{2,1,0:T(8,128)S(1)} %get-tuple-element.19), channel_id=1, source_target_pairs={{1,32},{2,33},{3,34},{4,35},{5,36},{6,37},{7,38},{33,64},{34,65},{... | collective-permute-start | bytes 258056 | tf_op jit(solution)/shard_map/ppermute | solution.py:469
  29.7 7.7 %collective-permute-start.6 = (f32[7,8,384]{2,1,0:T(8,128)S(1)}, f32[7,8,384]{2,1,0:T(8,128)S(1)}, u32[]{:S(2)}, u32[]{:S(2)}) collective-permute-start(f32[7,8,384]{2,1,0:T(8,128)S(1)} %get-tuple-element.21), channel_id=1, source_target_pairs={{32,1},{33,2},{34,3},{35,4},{36,5},{37,6},{38,7},{64,33},{65,34},{... | collective-permute-start | bytes 258056 | tf_op jit(solution)/shard_map/ppermute | solution.py:469
  37.4 0.0 collective-permute-done.3.left_above_ref
  37.4 1.9 %collective-permute-start.7 = (f32[7,8,384]{2,1,0:T(8,128)S(1)}, f32[7,8,384]{2,1,0:T(8,128)S(1)}, u32[]{:S(2)}, u32[]{:S(2)}) collective-permute-start(f32[7,8,384]{2,1,0:T(8,128)S(1)} %get-tuple-element.22), channel_id=1, source_target_pairs={{33,0},{34,1},{35,2},{36,3},{37,4},{38,5},{39,6},{65,32},{66,33},{... | collective-permute-start | bytes 258056 | tf_op jit(solution)/shard_map/ppermute | solution.py:469
  39.3 1.7 %collective-permute-done.4.left_below_ref = f32[7,8,384]{2,1,0:T(8,128)S(1)} collective-permute-done((f32[7,8,384]{2,1,0:T(8,128)S(1)}, f32[7,8,384]{2,1,0:T(8,128)S(1)}, u32[]{:S(2)}, u32[]{:S(2)}) %collective-permute-start.4) | collective-permute-done | bytes 86048 | tf_op jit(solution)/shard_map/ppermute | solution.py:469
  41.0 1.9 %collective-permute-start.2 = (f32[8,8,384]{2,1,0:T(8,128)S(1)}, f32[8,8,384]{2,1,0:T(8,128)S(1)}, u32[]{:S(2)}, u32[]{:S(2)}) collective-permute-start(f32[8,8,384]{2,1,0:T(8,128)S(1)} %get-tuple-element.17), channel_id=1, source_target_pairs={{0,32},{1,33},{2,34},{3,35},{4,36},{5,37},{6,38},{7,39},{32,64},{3... | collective-permute-start | bytes 294920 | tf_op jit(solution)/shard_map/ppermute | solution.py:469
  43.0 0.0 collective-permute-done.6.right_above_ref
  43.0 5.8 %collective-permute-start.5 = (f32[8,8,384]{2,1,0:T(8,128)S(1)}, f32[8,8,384]{2,1,0:T(8,128)S(1)}, u32[]{:S(2)}, u32[]{:S(2)}) collective-permute-start(f32[8,8,384]{2,1,0:T(8,128)S(1)} %get-tuple-element.20), channel_id=1, source_target_pairs={{32,0},{33,1},{34,2},{35,3},{36,4},{37,5},{38,6},{39,7},{64,32},{6... | collective-permute-start | bytes 294920 | tf_op jit(solution)/shard_map/ppermute | solution.py:469
  48.7 0.1 multiply_reduce_fusion
  48.8 0.1 copy.11
  48.9 4.9 %setup.1 = (bf16[2,192,1024]{2,1,0:T(8,128)(2,1)S(1)}, bf16[2,96,1024]{2,1,0:T(8,128)(2,1)S(1)}, bf16[2,256,512]{2,1,0:T(8,128)(2,1)S(1)}) custom-call(s32[64]{0:T(128)S(1)} %convert_element_type.15.mats_ref, f32[216]{0:T(256)S(1)} %reshape.43.factor_ref, f32[64,128]{1,0:T(8,128)S(1)} %pad.4.sten_ref), custom_call_target="tpu_custom_call" | custom-call | tf_op jit(solution)/shard_map/setup/pallas_call | solution.py:430
  53.9 0.0 collective-permute-done.7.right_below_ref
  53.9 0.0 collective-permute-done.2.left_ref
  53.9 0.0 collective-permute-done.5.right_ref
  53.9 0.0 collective-permute-done.1.below_ref
  53.9 6.8 %cycle.1 = f32[8,96,128]{2,1,0:T(8,128)S(1)} custom-call(f32[8,32,384]{2,1,0:T(8,128)S(1)} %get-tuple-element.14.own_ref, f32[7,32,384]{2,1,0:T(8,128)S(1)} %collective-permute-done.above_ref, f32[7,32,384]{2,1,0:T(8,128)S(1)} %collective-permute-done.1.below_ref, f32[8,8,384]{2,1,0:T(8,128)S(1)} %collective-permute-done.2.left_ref, ...), custom_call_target="tpu_custom_call" | custom-call | tf_op jit(solution)/shard_map/cycle/pallas_call | solution.py:476
  60.7 0.0 copy-start
  60.7 11.5 %all_to_all.10 = f32[8,96,128]{2,1,0:T(8,128)S(1)} all-to-all(f32[8,96,128]{2,1,0:T(8,128)S(1)} %cycle.1), channel_id=1, replica_groups=mesh['gz'=8,'gx'=4,'gy'=8] {'gz'}, dimensions={0} | all-to-all | bytes 786432 | tf_op jit(solution)/shard_map/all_to_all | solution.py:508
  72.2 1.6 %unpack.1 = (f32[8,3,8,256]{3,2,1,0:T(8,128)}, f32[8,3,8,256]{3,2,1,0:T(8,128)}) custom-call(f32[768,128]{1,0:T(8,128)S(1)} %bitcast.4, f32[8,3,8,256]{3,2,1,0:T(8,128)S(1)} %copy-done), custom_call_target="tpu_custom_call" | custom-call | tf_op jit(solution)/shard_map/unpack/pallas_call | solution.py:509
  (7 shorter events, 0.0 us)
Async XLA Ops:
  3.5 4.3 %copy-start.1 = (f32[8,3,3,3]{0,3,2,1:T(4,128)S(1)}, f32[8,3,3,3]{0,3,2,1:T(4,128)}, u32[]{:S(2)}) copy-start(f32[8,3,3,3]{0,3,2,1:T(4,128)} %param.8) | copy-start | bytes 2596
  3.5 13.6 %all-to-all-start = ((f32[8,104,128]{2,1,0:T(8,128)}), f32[8,104,128]{2,1,0:T(8,128)S(1)}, u32[]{:S(2)}, u32[]{:S(2)}) async-start(f32[8,104,128]{2,1,0:T(8,128)} %bitcast.5), calls=%async_computation | async-start | bytes 851968 | tf_op jit(solution)/shard_map/all_to_all | solution.py:424
  7.9 0.7 copy-start.2
  17.4 20.0 %collective-permute-start.3 = (f32[7,8,384]{2,1,0:T(8,128)S(1)}, f32[7,8,384]{2,1,0:T(8,128)S(1)}, u32[]{:S(2)}, u32[]{:S(2)}) collective-permute-start(f32[7,8,384]{2,1,0:T(8,128)S(1)} %get-tuple-element.18), channel_id=1, source_target_pairs={{0,33},{1,34},{2,35},{3,36},{4,37},{5,38},{6,39},{32,65},{33,66},{... | collective-permute-start | bytes 258056 | tf_op jit(solution)/shard_map/ppermute | solution.py:469
  21.7 32.2 %collective-permute-start = (f32[7,32,384]{2,1,0:T(8,128)S(1)}, f32[7,32,384]{2,1,0:T(8,128)S(1)}, u32[]{:S(2)}, u32[]{:S(2)}) collective-permute-start(f32[7,32,384]{2,1,0:T(8,128)S(1)} %get-tuple-element.15), channel_id=1, source_target_pairs={{0,1},{1,2},{2,3},{3,4},{4,5},{5,6},{6,7},{32,33},{33,34},{34,35},... | collective-permute-start | bytes 1032200 | tf_op jit(solution)/shard_map/ppermute | solution.py:469
  24.7 29.2 %collective-permute-start.1 = (f32[7,32,384]{2,1,0:T(8,128)S(1)}, f32[7,32,384]{2,1,0:T(8,128)S(1)}, u32[]{:S(2)}, u32[]{:S(2)}) collective-permute-start(f32[7,32,384]{2,1,0:T(8,128)S(1)} %get-tuple-element.16), channel_id=1, source_target_pairs={{1,0},{2,1},{3,2},{4,3},{5,4},{6,5},{7,6},{33,32},{34,33},{35,34},... | collective-permute-start | bytes 1032200 | tf_op jit(solution)/shard_map/ppermute | solution.py:469
  27.6 13.5 %collective-permute-start.4 = (f32[7,8,384]{2,1,0:T(8,128)S(1)}, f32[7,8,384]{2,1,0:T(8,128)S(1)}, u32[]{:S(2)}, u32[]{:S(2)}) collective-permute-start(f32[7,8,384]{2,1,0:T(8,128)S(1)} %get-tuple-element.19), channel_id=1, source_target_pairs={{1,32},{2,33},{3,34},{4,35},{5,36},{6,37},{7,38},{33,64},{34,65},{... | collective-permute-start | bytes 258056 | tf_op jit(solution)/shard_map/ppermute | solution.py:469
  29.7 13.2 %collective-permute-start.6 = (f32[7,8,384]{2,1,0:T(8,128)S(1)}, f32[7,8,384]{2,1,0:T(8,128)S(1)}, u32[]{:S(2)}, u32[]{:S(2)}) collective-permute-start(f32[7,8,384]{2,1,0:T(8,128)S(1)} %get-tuple-element.21), channel_id=1, source_target_pairs={{32,1},{33,2},{34,3},{35,4},{36,5},{37,6},{38,7},{64,33},{65,34},{... | collective-permute-start | bytes 258056 | tf_op jit(solution)/shard_map/ppermute | solution.py:469
  37.4 16.5 %collective-permute-start.7 = (f32[7,8,384]{2,1,0:T(8,128)S(1)}, f32[7,8,384]{2,1,0:T(8,128)S(1)}, u32[]{:S(2)}, u32[]{:S(2)}) collective-permute-start(f32[7,8,384]{2,1,0:T(8,128)S(1)} %get-tuple-element.22), channel_id=1, source_target_pairs={{33,0},{34,1},{35,2},{36,3},{37,4},{38,5},{39,6},{65,32},{66,33},{... | collective-permute-start | bytes 258056 | tf_op jit(solution)/shard_map/ppermute | solution.py:469
  41.0 12.8 %collective-permute-start.2 = (f32[8,8,384]{2,1,0:T(8,128)S(1)}, f32[8,8,384]{2,1,0:T(8,128)S(1)}, u32[]{:S(2)}, u32[]{:S(2)}) collective-permute-start(f32[8,8,384]{2,1,0:T(8,128)S(1)} %get-tuple-element.17), channel_id=1, source_target_pairs={{0,32},{1,33},{2,34},{3,35},{4,36},{5,37},{6,38},{7,39},{32,64},{3... | collective-permute-start | bytes 294920 | tf_op jit(solution)/shard_map/ppermute | solution.py:469
  43.0 10.9 %collective-permute-start.5 = (f32[8,8,384]{2,1,0:T(8,128)S(1)}, f32[8,8,384]{2,1,0:T(8,128)S(1)}, u32[]{:S(2)}, u32[]{:S(2)}) collective-permute-start(f32[8,8,384]{2,1,0:T(8,128)S(1)} %get-tuple-element.20), channel_id=1, source_target_pairs={{32,0},{33,1},{34,2},{35,3},{36,4},{37,5},{38,6},{39,7},{64,32},{6... | collective-permute-start | bytes 294920 | tf_op jit(solution)/shard_map/ppermute | solution.py:469
  60.7 11.5 %copy-start = (f32[8,3,8,256]{3,2,1,0:T(8,128)S(1)}, f32[8,3,8,256]{3,2,1,0:T(8,128)}, u32[]{:S(2)}) copy-start(f32[8,3,8,256]{3,2,1,0:T(8,128)} %start_ref.1) | copy-start | bytes 589828

commit v4 on v2

--- a/solution.py
+++ b/solution.py
@@ -21,8 +21,8 @@
 SMEM = pl.BlockSpec(memory_space=pltpu.SMEM)
 
 
-def params():
-    return pltpu.CompilerParams(vmem_limit_bytes=40 * 1024 * 1024)
+def params(mib=40):
+    return pltpu.CompilerParams(vmem_limit_bytes=mib * 1024 * 1024)
 
 
 def swap_blocks(tile):
@@ -88,22 +88,32 @@
         copy.wait()
 
 
-def turn_kernel(got_ref, own_ref, low_ref, high_ref):
+def turn_kernel(got_ref, own_ref, first_ref, second_ref):
     halves = []
     for h in range(2):
         rows = [got_ref[g, h * 48 + q * 8 : h * 48 + q * 8 + 8] for q in range(6) for g in range(8)]
         halves.append(jnp.transpose(jnp.concatenate(rows, axis=0)))
     turned = jnp.concatenate(halves, axis=0).reshape(YT, XT, 384)
     own_ref[...] = turned
-    low_ref[...] = turned[:HALO]
-    high_ref[...] = turned[YT - HALO :]
-
-
-def sides_kernel(own_ref, above_ref, below_ref, after_ref, left_ref, right_ref):
-    for ref, cols in ((left_ref, slice(0, XH)), (right_ref, slice(XT - XH, XT))):
-        ref[0:HALO] = above_ref[:, cols]
-        ref[HALO : HALO + YT] = own_ref[:, cols]
-        ref[HALO + YT :] = below_ref[:, cols]
+    even = lax.axis_index("gy") % 2 == 0
+    low, high = turned[:HALO], turned[YT - HALO :]
+    first_ref[...] = jnp.where(even, high, low)
+    second_ref[...] = jnp.where(even, low, high)
+
+
+def sides_kernel(own_ref, first_ref, second_ref, after_ref, send1_ref, send2_ref):
+    even_x = lax.axis_index("gz") % 2 == 0
+    even_y = lax.axis_index("gy") % 2 == 0
+
+    def put(rows, value):
+        left, right = value[:, 0:XH], value[:, XT - XH :]
+        send1_ref[rows] = jnp.where(even_x, right, left)
+        send2_ref[rows] = jnp.where(even_x, left, right)
+
+    first, second = first_ref[...], second_ref[...]
+    put(slice(0, HALO), jnp.where(even_y, second, first))
+    put(slice(HALO, HALO + YT), own_ref[...])
+    put(slice(HALO + YT, YW), jnp.where(even_y, first, second))
 
 
 def split(value):
@@ -248,10 +258,10 @@
 
 def cycle_kernel(
     own_ref,
-    above_ref,
-    below_ref,
-    left_ref,
-    right_ref,
+    y1_ref,
+    y2_ref,
+    x1_ref,
+    x2_ref,
     fine_ref,
     coarse_ref,
     first_ref,
@@ -272,11 +282,13 @@
     at_top = gy == 0
     at_bottom = gy == lax.axis_size("gy") - 1
 
-    x_ref[:, 0:XH] = left_ref[...]
-    x_ref[:, XH + XT :] = right_ref[...]
-    x_ref[0:HALO, XH : XH + XT] = above_ref[...]
+    even_x = gz % 2 == 0
+    even_y = gy % 2 == 0
+    x_ref[:, 0:XH] = jnp.where(even_x, x2_ref[...], x1_ref[...])
+    x_ref[:, XH + XT :] = jnp.where(even_x, x1_ref[...], x2_ref[...])
+    x_ref[0:HALO, XH : XH + XT] = jnp.where(even_y, y2_ref[...], y1_ref[...])
     x_ref[HALO : HALO + YT, XH : XH + XT] = own_ref[...]
-    x_ref[HALO + YT :, XH : XH + XT] = below_ref[...]
+    x_ref[HALO + YT :, XH : XH + XT] = jnp.where(even_y, y1_ref[...], y2_ref[...])
 
     def product(halves, w_ref, at, width):
         high, low = halves
@@ -395,6 +407,11 @@
 
 def shape(*dims, dtype=F32):
     return jax.ShapeDtypeStruct(dims, dtype)
+
+
+def swaps(line, start):
+    pairs = [(line[i], line[i + 1]) for i in range(start, len(line) - 1, 2)]
+    return pairs + [(b, a) for a, b in pairs]
 
 
 def on_device(right_side, start_field, layer_material, stiffness, line_factors):
@@ -410,7 +427,7 @@
             pltpu.SemaphoreType.DMA((6,)),
             pltpu.SemaphoreType.DMA,
         ],
-        compiler_params=params(),
+        compiler_params=params(60),
         name="pack",
     )(right_side, start_field, layer_material)
     got = lax.all_to_all(packed.reshape(8, ROWS, 128), "gz", 0, 0, tiled=True)
@@ -436,7 +453,7 @@
         name="setup",
     )(mats, line_factors.reshape(-1), sten)
 
-    own, low, high = pl.pallas_call(
+    own, send1, send2 = pl.pallas_call(
         turn_kernel,
         out_shape=(shape(YT, XT, 384), shape(HALO, XT, 384), shape(HALO, XT, 384)),
         in_specs=[VMEM],
@@ -444,22 +461,20 @@
         compiler_params=params(),
         name="turn",
     )(got)
-    ahead = [(i, i + 1) for i in range(size_y - 1)]
-    above = lax.ppermute(high, "gy", ahead)
-    below = lax.ppermute(low, "gy", [(b, a) for a, b in ahead])
-    to_left, to_right = pl.pallas_call(
+    count_x, count_y, count_z = (lax.axis_size(axis) for axis in ("gx", "gy", "gz"))
+    y1 = lax.ppermute(send1, "gy", swaps(range(count_y), 0))
+    y2 = lax.ppermute(send2, "gy", swaps(range(count_y), 1))
+    send1, send2 = pl.pallas_call(
         sides_kernel,
         out_shape=(shape(YW, XH, 384), shape(YW, XH, 384)),
         in_specs=[VMEM, VMEM, VMEM, pl.BlockSpec(memory_space=pl.ANY)],
         out_specs=(VMEM, VMEM),
         compiler_params=params(),
         name="sides",
-    )(own, above, below, fine)
-    count_x, count_z = lax.axis_size("gx"), lax.axis_size("gz")
+    )(own, y1, y2, fine)
     along = [(i % count_z) * count_x + i // count_z for i in range(count_x * count_z)]
-    ahead = list(zip(along[:-1], along[1:]))
-    left = lax.ppermute(to_right, ("gz", "gx"), ahead)
-    right = lax.ppermute(to_left, ("gz", "gx"), [(b, a) for a, b in ahead])
+    x1 = lax.ppermute(send1, ("gz", "gx"), swaps(along, 0))
+    x2 = lax.ppermute(send2, ("gz", "gx"), swaps(along, 1))
 
     out = pl.pallas_call(
         cycle_kernel,
@@ -479,7 +494,7 @@
         ],
         compiler_params=params(),
         name="cycle",
-    )(own, above, below, left, right, fine, coarse, first)
+    )(own, y1, y2, x1, x2, fine, coarse, first)
     back = lax.all_to_all(out, "gz", 0, 0, tiled=True)
     return pl.pallas_call(
         unpack_kernel,

time: 71.3 us -> 61.2 us (0.86)
  starting transfers between devices: 18.9 us -> 13.6 us
  blocking collectives: 14.3 us -> 11.5 us
  local copies, waits for them, and re-layouts: 3.69 us -> 1.19 us
  Pallas kernels: 15.5 us -> 16.3 us
    ppermute x4, starting transfers between devices: 14.6 us -> 9.27 us  [the longest x1 5.93 us: on_device(): y2 = lax.ppermute(send2, 'gy', swaps(range(count_y), 1))]
    all_to_all x1, blocking collectives: 14.3 us -> 11.5 us  [on_device(): back = lax.all_to_all(out, 'gz', 0, 0, tiled=True)]
    unnamed x13 -> x7, local copies, waits for them, and re-layouts: 3.35 us -> 0.85 us
    pallas_call x1, Pallas kernels: 2.12 us -> 2.9 us  [on_device(): pl.pallas_call(pack_kernel, out_shape=shape(8 * ROWS, 128), in_specs=[HBM...]
  transfers between devices with their start and end apart: 5 -> 5, of which waited for: 4 -> 3; matrix products, arithmetic and copies ran while one was open for 1% -> 1% of each run, Pallas kernels for 7% -> 8%
where the time goes in v4:
time: 61.2 us; the launch traced here: 60.8 us
  waiting for transfers between devices  17.4 us (28%)
  Pallas kernels  16.3 us (27%)
  starting transfers between devices  13.6 us (22%)
  blocking collectives  11.5 us (19%)
  local copies, waits for them, and re-layouts  1.19 us (2%)
  between operations  0.75 us (1%)
    all_to_all x1, blocking collectives, on_device(): back = lax.all_to_all(out, 'gz', 0, 0, tiled=True)  11.5 us
    all_to_all x1, waiting for transfers between devices, on_device(): got = lax.all_to_all(packed.reshape(8, ROWS, 128), 'gz', 0, 0, tiled=True)  8.27 us
    ppermute x1, waiting for transfers between devices, on_device(): x2 = lax.ppermute(send2, ('gz', 'gx'), swaps(along, 1))  6.82 us
    pallas_call x1, Pallas kernels, on_device(): pl.pallas_call(cycle_kernel, out_shape=shape(8, 96, 128), in_specs=[VMEM]...  6.71 us
    ppermute x1, starting transfers between devices, on_device(): y2 = lax.ppermute(send2, 'gy', swaps(range(count_y), 1))  5.93 us
    pallas_call x1, Pallas kernels, on_device(): pl.pallas_call(setup_kernel, out_shape=(shape(2, 192, 1024, dtype=BF16),...  4.92 us
    all_to_all x1, starting transfers between devices, on_device(): got = lax.all_to_all(packed.reshape(8, ROWS, 128), 'gz', 0, 0, tiled=True)  4.31 us
    ppermute x1, starting transfers between devices, on_device(): x2 = lax.ppermute(send2, ('gz', 'gx'), swaps(along, 1))  3.05 us
  transfers between devices with their start and end apart: 5, of which 3 were waited for; matrix products, arithmetic and copies ran while one was open for 1% of the time, Pallas kernels for 8%

profile of v4, /device:TPU:104, one launch (start us, length us, event | category | flops | bytes accessed | tf_op | source)
XLA Modules:
  0.0 60.8 jit_solution(1015124314292122575)
XLA Ops:
  0.6 2.9 %pack.1 = f32[832,128]{1,0:T(8,128)} custom-call(f32[8,3,8,256]{3,2,1,0:T(8,128)} %load_hbm.1, f32[8,3,8,256]{3,2,1,0:T(8,128)} %start_ref.1, s32[8]{0:T(128)} %mats_hbm.1), custom_call_target="tpu_custom_call" | custom-call | tf_op jit(solution)/shard_map/pack/pallas_call | solution.py:419
  3.5 0.0 copy-start.1
  3.6 4.3 %all-to-all-start = ((f32[8,104,128]{2,1,0:T(8,128)}), f32[8,104,128]{2,1,0:T(8,128)S(1)}, u32[]{:S(2)}, u32[]{:S(2)}) async-start(f32[8,104,128]{2,1,0:T(8,128)} %bitcast.5), calls=%async_computation | async-start | bytes 851968 | tf_op jit(solution)/shard_map/all_to_all | solution.py:433
  7.9 0.0 copy-done.1
  7.9 0.0 copy-start.2
  7.9 0.7 %copy-done.2 = f32[8,3,3,3]{0,3,2,1:T(4,128)S(1)} copy-done((f32[8,3,3,3]{0,3,2,1:T(4,128)S(1)}, f32[8,3,3,3]{0,3,2,1:T(4,128)}, u32[]{:S(2)}) %copy-start.2) | copy-done | bytes 888
  8.6 0.1 copy.10
  8.7 0.2 reshape.43.factor_ref
  8.9 8.3 %all-to-all-done.got_ref = f32[8,104,128]{2,1,0:T(8,128)S(1)} async-done(((f32[8,104,128]{2,1,0:T(8,128)}), f32[8,104,128]{2,1,0:T(8,128)S(1)}, u32[]{:S(2)}, u32[]{:S(2)}) %all-to-all-start) | async-done | bytes 426016 | tf_op jit(solution)/shard_map/all_to_all | solution.py:433
  17.2 0.2 turn.1
  17.3 0.2 collective-permute-start
  17.5 5.9 %collective-permute-start.1 = (f32[7,32,384]{2,1,0:T(8,128)S(1)}, f32[7,32,384]{2,1,0:T(8,128)S(1)}, u32[]{:S(2)}, u32[]{:S(2)}) collective-permute-start(f32[7,32,384]{2,1,0:T(8,128)S(1)} %get-tuple-element.12), channel_id=1, source_target_pairs={{1,2},{3,4},{5,6},{2,1},{4,3},{6,5},{9,10},{11,12},{13,14},{10,9},... | collective-permute-start | bytes 1032200 | tf_op jit(solution)/shard_map/ppermute | solution.py:466
  23.5 0.1 convert_element_type.15.mats_ref
  23.6 0.1 multiply_reduce_fusion
  23.7 0.1 copy.11
  23.8 4.9 %setup.1 = (bf16[2,192,1024]{2,1,0:T(8,128)(2,1)S(1)}, bf16[2,96,1024]{2,1,0:T(8,128)(2,1)S(1)}, bf16[2,256,512]{2,1,0:T(8,128)(2,1)S(1)}) custom-call(s32[64]{0:T(128)S(1)} %convert_element_type.15.mats_ref, f32[216]{0:T(256)S(1)} %reshape.43.factor_ref, f32[64,128]{1,0:T(8,128)S(1)} %pad.4.sten_ref), custom_call_target="tpu_custom_call" | custom-call | tf_op jit(solution)/shard_map/setup/pallas_call | solution.py:439
  28.7 0.0 collective-permute-done.first_ref.y1_ref
  28.7 2.3 %collective-permute-done.1.second_ref.y2_ref = f32[7,32,384]{2,1,0:T(8,128)S(1)} collective-permute-done((f32[7,32,384]{2,1,0:T(8,128)S(1)}, f32[7,32,384]{2,1,0:T(8,128)S(1)}, u32[]{:S(2)}, u32[]{:S(2)}) %collective-permute-start.1) | collective-permute-done | bytes 344096 | tf_op jit(solution)/shard_map/ppermute | solution.py:466
  31.0 0.1 sides.1
  31.1 0.1 collective-permute-start.2
  31.2 3.1 %collective-permute-start.3 = (f32[22,8,384]{2,1,0:T(8,128)S(1)}, f32[22,8,384]{2,1,0:T(8,128)S(1)}, u32[]{:S(2)}, u32[]{:S(2)}) collective-permute-start(f32[22,8,384]{2,1,0:T(8,128)S(1)} %get-tuple-element.15), channel_id=1, source_target_pairs={{32,64},{96,128},{160,192},{224,8},{40,72},{104,136},{168,200},{23... | collective-permute-start | bytes 811016 | tf_op jit(solution)/shard_map/ppermute | solution.py:477
  34.3 0.0 collective-permute-done.2.x1_ref
  34.3 6.8 %collective-permute-done.3.x2_ref = f32[22,8,384]{2,1,0:T(8,128)S(1)} collective-permute-done((f32[22,8,384]{2,1,0:T(8,128)S(1)}, f32[22,8,384]{2,1,0:T(8,128)S(1)}, u32[]{:S(2)}, u32[]{:S(2)}) %collective-permute-start.3) | collective-permute-done | bytes 270368 | tf_op jit(solution)/shard_map/ppermute | solution.py:477
  41.1 6.7 %cycle.1 = f32[8,96,128]{2,1,0:T(8,128)S(1)} custom-call(f32[8,32,384]{2,1,0:T(8,128)S(1)} %get-tuple-element.10.own_ref, f32[7,32,384]{2,1,0:T(8,128)S(1)} %collective-permute-done.first_ref.y1_ref, f32[7,32,384]{2,1,0:T(8,128)S(1)} %collective-permute-done.1.second_ref.y2_ref, f32[22,8,384]{2,1,0:T(8,128)S(1)} %collective-permute-done.2.x1_ref, ...), custom_call_target="tpu_custom_call" | custom-call | tf_op jit(solution)/shard_map/cycle/pallas_call | solution.py:479
  47.8 0.0 copy-start
  47.8 11.5 %all_to_all.10 = f32[8,96,128]{2,1,0:T(8,128)S(1)} all-to-all(f32[8,96,128]{2,1,0:T(8,128)S(1)} %cycle.1), channel_id=1, replica_groups=mesh['gz'=8,'gx'=4,'gy'=8] {'gz'}, dimensions={0} | all-to-all | bytes 786432 | tf_op jit(solution)/shard_map/all_to_all | solution.py:498
  59.3 0.0 copy-done
  59.3 1.5 %unpack.1 = (f32[8,3,8,256]{3,2,1,0:T(8,128)}, f32[8,3,8,256]{3,2,1,0:T(8,128)}) custom-call(f32[768,128]{1,0:T(8,128)S(1)} %bitcast.4, f32[8,3,8,256]{3,2,1,0:T(8,128)S(1)} %copy-done), custom_call_target="tpu_custom_call" | custom-call | tf_op jit(solution)/shard_map/unpack/pallas_call | solution.py:499
  (4 shorter events, 0.0 us)
Async XLA Ops:
  3.5 4.3 %copy-start.1 = (f32[8,3,3,3]{0,3,2,1:T(4,128)S(1)}, f32[8,3,3,3]{0,3,2,1:T(4,128)}, u32[]{:S(2)}) copy-start(f32[8,3,3,3]{0,3,2,1:T(4,128)} %param.8) | copy-start | bytes 2596
  3.6 13.6 %all-to-all-start = ((f32[8,104,128]{2,1,0:T(8,128)}), f32[8,104,128]{2,1,0:T(8,128)S(1)}, u32[]{:S(2)}, u32[]{:S(2)}) async-start(f32[8,104,128]{2,1,0:T(8,128)} %bitcast.5), calls=%async_computation | async-start | bytes 851968 | tf_op jit(solution)/shard_map/all_to_all | solution.py:433
  7.9 0.7 %copy-start.2 = (f32[8,3,3,3]{0,3,2,1:T(4,128)S(1)}, f32[8,3,3,3]{0,3,2,1:T(4,128)}, u32[]{:S(2)}) copy-start(f32[8,3,3,3]{0,3,2,1:T(4,128)} %param.9) | copy-start | bytes 2596
  17.3 11.4 %collective-permute-start = (f32[7,32,384]{2,1,0:T(8,128)S(1)}, f32[7,32,384]{2,1,0:T(8,128)S(1)}, u32[]{:S(2)}, u32[]{:S(2)}) collective-permute-start(f32[7,32,384]{2,1,0:T(8,128)S(1)} %get-tuple-element.11), channel_id=1, source_target_pairs={{0,1},{2,3},{4,5},{6,7},{1,0},{3,2},{5,4},{7,6},{8,9},{10,11},{12,... | collective-permute-start | bytes 1032200 | tf_op jit(solution)/shard_map/ppermute | solution.py:465
  17.5 13.5 %collective-permute-start.1 = (f32[7,32,384]{2,1,0:T(8,128)S(1)}, f32[7,32,384]{2,1,0:T(8,128)S(1)}, u32[]{:S(2)}, u32[]{:S(2)}) collective-permute-start(f32[7,32,384]{2,1,0:T(8,128)S(1)} %get-tuple-element.12), channel_id=1, source_target_pairs={{1,2},{3,4},{5,6},{2,1},{4,3},{6,5},{9,10},{11,12},{13,14},{10,9},... | collective-permute-start | bytes 1032200 | tf_op jit(solution)/shard_map/ppermute | solution.py:466
  31.1 3.2 %collective-permute-start.2 = (f32[22,8,384]{2,1,0:T(8,128)S(1)}, f32[22,8,384]{2,1,0:T(8,128)S(1)}, u32[]{:S(2)}, u32[]{:S(2)}) collective-permute-start(f32[22,8,384]{2,1,0:T(8,128)S(1)} %get-tuple-element.14), channel_id=1, source_target_pairs={{0,32},{64,96},{128,160},{192,224},{8,40},{72,104},{136,168},{200,... | collective-permute-start | bytes 811016 | tf_op jit(solution)/shard_map/ppermute | solution.py:476
  31.2 9.9 %collective-permute-start.3 = (f32[22,8,384]{2,1,0:T(8,128)S(1)}, f32[22,8,384]{2,1,0:T(8,128)S(1)}, u32[]{:S(2)}, u32[]{:S(2)}) collective-permute-start(f32[22,8,384]{2,1,0:T(8,128)S(1)} %get-tuple-element.15), channel_id=1, source_target_pairs={{32,64},{96,128},{160,192},{224,8},{40,72},{104,136},{168,200},{23... | collective-permute-start | bytes 811016 | tf_op jit(solution)/shard_map/ppermute | solution.py:477
  47.8 11.5 %copy-start = (f32[8,3,8,256]{3,2,1,0:T(8,128)S(1)}, f32[8,3,8,256]{3,2,1,0:T(8,128)}, u32[]{:S(2)}) copy-start(f32[8,3,8,256]{3,2,1,0:T(8,128)} %start_ref.1) | copy-start | bytes 589828

commit v5 on v4

--- a/solution.py
+++ b/solution.py
@@ -13,6 +13,8 @@
 XW = XT + 2 * XH
 YT = 8
 YW = YT + 2 * HALO
+RH = HALO - 1
+RW = YT + 2 * RH
 ROWS = 104
 NZ = 64
 NC = NZ // 2
@@ -59,10 +61,10 @@
                 at = h * 48 + f * 24 + c * 8 + z
                 out_ref[pl.ds(at, 8, stride=ROWS), :] = tile[z, :, h * 128 : h * 128 + 128]
     mats_copy.wait()
-    lane = lax.broadcasted_iota(jnp.int32, (8, 128), 1)
+    row = lax.broadcasted_iota(jnp.int32, (8, 128), 0)
     ids = jnp.zeros((8, 128), jnp.int32)
     for z in range(8):
-        ids = jnp.where(lane == z, mats_ref[z], ids)
+        ids = jnp.where(row == z, mats_ref[z], ids)
     for k in range(8):
         out_ref[k * ROWS + 96 : k * ROWS + 104, :] = ids.astype(F32)
 
@@ -88,32 +90,99 @@
         copy.wait()
 
 
-def turn_kernel(got_ref, own_ref, first_ref, second_ref):
-    halves = []
-    for h in range(2):
-        rows = [got_ref[g, h * 48 + q * 8 : h * 48 + q * 8 + 8] for q in range(6) for g in range(8)]
-        halves.append(jnp.transpose(jnp.concatenate(rows, axis=0)))
-    turned = jnp.concatenate(halves, axis=0).reshape(YT, XT, 384)
-    own_ref[...] = turned
+def exact(a, b):
+    return jnp.dot(a, b, precision=lax.Precision.HIGHEST, preferred_element_type=F32)
+
+
+def folded(value):
+    half = value.shape[0] // 2
+    lane = lax.broadcasted_iota(jnp.int32, (half, *value.shape[1:]), 2)
+    return jnp.where(lane < 192, value[:half], pltpu.roll(value[half:], 192, axis=2))
+
+
+def unfolded(value):
+    return value[:, :, 0:192], pltpu.roll(value, 192, axis=2)[:, :, 0:192]
+
+
+def turn_kernel(
+    got_ref, table_ref, own_ref, q_ref, sten_ref, first_ref, second_ref, down_ref, up_ref
+):
+    groups = range(8)
+    ids = jnp.concatenate([got_ref[g, 96:104] for g in groups], axis=0)
+    lane = lax.broadcasted_iota(jnp.int32, ids.shape, 1)
+    sten = exact((ids == lane.astype(F32)).astype(F32), table_ref[...])
+    sten_ref[...] = sten
+
+    def field(f, c):
+        at = f * 24 + c * 8
+        return jnp.concatenate(
+            [
+                jnp.concatenate(
+                    [got_ref[g, h * 48 + at : h * 48 + at + 8] for g in groups], axis=0
+                )
+                for h in range(2)
+            ],
+            axis=1,
+        )
+
+    start = [field(1, c) for c in range(3)]
+    q = couple(sten, 1, start)
+    diag = couple(sten, 0, start)
+    vert = couple(sten, 2, [above_below(part) for part in start])
+    lane = lax.broadcasted_iota(jnp.int32, (NZ, 256), 1)
+    x, y = lane % XT, lane // XT
+    resid = []
+    for c in range(3):
+        near = jnp.where(x > 0, pltpu.roll(q[c], 1, axis=1), 0.0)
+        near = near + jnp.where(x < XT - 1, pltpu.roll(q[c], 255, axis=1), 0.0)
+        near = near + jnp.where(y > 0, pltpu.roll(q[c], XT, axis=1), 0.0)
+        near = near + jnp.where(y < YT - 1, pltpu.roll(q[c], 256 - XT, axis=1), 0.0)
+        resid.append((field(0, c) - (diag[c] - vert[c])) + near)
+    own_ref[...] = jnp.transpose(jnp.concatenate(resid, axis=0)).reshape(YT, XT, 192)
+    q_ref[...] = jnp.transpose(jnp.concatenate(q, axis=0)).reshape(YT, XT, 192)
+    for ref, top, edge in ((down_ref, YT - RH, YT - 1), (up_ref, 0, 0)):
+        ref[0:RH, :, 0:192] = own_ref[top : top + RH]
+        ref[RH, :, 0:192] = q_ref[edge]
+        ref[RH + 1, :, 0:192] = jnp.zeros((XT, 192), F32)
+        for r in range(RH):
+            ref[RH + 1, r : r + 1, 0:192] = q_ref[top + r, 0:1]
+            ref[RH + 1, 8 + r : 9 + r, 0:192] = q_ref[top + r, XT - 1 : XT]
+    down, up = folded(down_ref[...]), folded(up_ref[...])
     even = lax.axis_index("gy") % 2 == 0
-    low, high = turned[:HALO], turned[YT - HALO :]
-    first_ref[...] = jnp.where(even, high, low)
-    second_ref[...] = jnp.where(even, low, high)
-
-
-def sides_kernel(own_ref, first_ref, second_ref, after_ref, send1_ref, send2_ref):
+    first_ref[...] = jnp.where(even, down, up)
+    second_ref[...] = jnp.where(even, up, down)
+
+
+def sides_kernel(
+    own_ref, q_ref, y1_ref, y2_ref, after_ref, resid_ref, edge_ref, send1_ref, send2_ref, wide_ref
+):
     even_x = lax.axis_index("gz") % 2 == 0
     even_y = lax.axis_index("gy") % 2 == 0
-
-    def put(rows, value):
-        left, right = value[:, 0:XH], value[:, XT - XH :]
-        send1_ref[rows] = jnp.where(even_x, right, left)
-        send2_ref[rows] = jnp.where(even_x, left, right)
-
-    first, second = first_ref[...], second_ref[...]
-    put(slice(0, HALO), jnp.where(even_y, second, first))
-    put(slice(HALO, HALO + YT), own_ref[...])
-    put(slice(HALO + YT, YW), jnp.where(even_y, first, second))
+    first, second = y1_ref[...], y2_ref[...]
+    sub = lax.broadcasted_iota(jnp.int32, (RW, XH, 192), 1)
+    edge_ref[...] = jnp.zeros((RW, XH, 192), F32)
+    resid_ref[RH : RH + YT] = own_ref[...]
+    for y in range(YT):
+        edge_ref[RH + y, 0:1] = q_ref[y, 0:1]
+        edge_ref[RH + y, 1:2] = q_ref[y, XT - 1 : XT]
+    for at, value, border, inside, mine in (
+        (0, jnp.where(even_y, second, first), RH - 1, RH, 0),
+        (RH + YT, jnp.where(even_y, first, second), RH + YT, RH + YT - 1, YT - 1),
+    ):
+        low, high = unfolded(value)
+        resid_ref[at : at + 4] = low
+        resid_ref[at + 4 : at + RH] = high[0:2]
+        resid_ref[border] = resid_ref[border] + q_ref[mine]
+        resid_ref[inside] = resid_ref[inside] + high[2]
+        for r in range(RH):
+            edge_ref[at + r, 0:1] = high[3, r : r + 1]
+            edge_ref[at + r, 1:2] = high[3, 8 + r : 9 + r]
+    wide_ref[:, :, 0:192] = jnp.where(sub == 7, edge_ref[:, 0:1], resid_ref[:, 0:XH])
+    left = folded(wide_ref[...])
+    wide_ref[:, :, 0:192] = jnp.where(sub == 0, edge_ref[:, 1:2], resid_ref[:, XT - XH :])
+    right = folded(wide_ref[...])
+    send1_ref[...] = jnp.where(even_x, right, left)
+    send2_ref[...] = jnp.where(even_x, left, right)
 
 
 def split(value):
@@ -182,33 +251,11 @@
 
 
 def setup_kernel(
-    mats_ref, factor_ref, sten_ref, fine_ref, coarse_ref, first_ref, line_ref, cline_ref
+    mats_ref, factor_ref, sten_ref, fine_ref, coarse_ref, line_ref, cline_ref
 ):
     sten = sten_ref[...]
     line_rows(mats_ref, factor_ref, line_ref, NZ, 1)
     line_rows(mats_ref, factor_ref, cline_ref, NC, 2)
-
-    row = lax.broadcasted_iota(jnp.int32, (NZ, 256), 0)
-    lane = lax.broadcasted_iota(jnp.int32, (NZ, 256), 1)
-    comp = lane // NZ - 1
-    layer = lane % NZ
-    same = (row == layer) & (comp >= 0)
-    near = ((row == layer + 1) | (row == layer - 1)) & (comp >= 0)
-
-    def picked(which, i):
-        at = which * 9 + i * 3
-        return jnp.where(
-            comp == 0,
-            sten[:, at : at + 1],
-            jnp.where(comp == 1, sten[:, at + 1 : at + 2], sten[:, at + 2 : at + 3]),
-        )
-
-    store_split(
-        first_ref,
-        0,
-        [jnp.where(same, picked(0, i), jnp.where(near, -picked(2, i), 0.0)) for i in range(3)],
-    )
-    store_split(first_ref, 256, [jnp.where(same, picked(1, i), 0.0) for i in range(3)])
 
     def level(sten_part, scale, ref, layers):
         blocks = [ref[i * layers : (i + 1) * layers, :] for i in range(3)]
@@ -230,9 +277,6 @@
     store_split(fine_ref, 256, kept)
     store_split(fine_ref, 512, lateral)
 
-    def exact(a, b):
-        return jnp.dot(a, b, precision=lax.Precision.HIGHEST, preferred_element_type=F32)
-
     layer_at = lax.broadcasted_iota(jnp.int32, (NC, NZ), 1) // 2
     pairs = (lax.broadcasted_iota(jnp.int32, (NC, NZ), 0) == layer_at).astype(F32)
     layer_at = lax.broadcasted_iota(jnp.int32, (NZ, NC), 0) // 2
@@ -257,16 +301,13 @@
 
 
 def cycle_kernel(
-    own_ref,
-    y1_ref,
-    y2_ref,
+    resid_ref,
+    edge_ref,
     x1_ref,
     x2_ref,
     fine_ref,
     coarse_ref,
-    first_ref,
     out_ref,
-    x_ref,
     r_ref,
     keep_ref,
     side_ref,
@@ -282,14 +323,6 @@
     at_top = gy == 0
     at_bottom = gy == lax.axis_size("gy") - 1
 
-    even_x = gz % 2 == 0
-    even_y = gy % 2 == 0
-    x_ref[:, 0:XH] = jnp.where(even_x, x2_ref[...], x1_ref[...])
-    x_ref[:, XH + XT :] = jnp.where(even_x, x1_ref[...], x2_ref[...])
-    x_ref[0:HALO, XH : XH + XT] = jnp.where(even_y, y2_ref[...], y1_ref[...])
-    x_ref[HALO : HALO + YT, XH : XH + XT] = own_ref[...]
-    x_ref[HALO + YT :, XH : XH + XT] = jnp.where(even_y, y1_ref[...], y2_ref[...])
-
     def product(halves, w_ref, at, width):
         high, low = halves
         wh = w_ref[0, :, at : at + width]
@@ -308,7 +341,12 @@
             value = src[a:b, :, lanes].reshape((b - a) * XW, -1)
             halves = split(value)
             for at, width, dst in jobs:
-                dst[a:b] = product(halves, w_ref, at, width).reshape(b - a, XW, width)
+                if isinstance(dst, tuple):
+                    both = product(halves, w_ref, at, width)
+                    for i, part in enumerate(dst):
+                        part[a:b] = both[:, i * 128 : i * 128 + 96].reshape(b - a, XW, 96)
+                else:
+                    dst[a:b] = product(halves, w_ref, at, width).reshape(b - a, XW, width)
 
     def spread(side, y):
         mid = side[y]
@@ -343,11 +381,26 @@
     inner = slice(XH, XH + XT)
     every = slice(None)
 
-    apply(
-        x_ref, slice(128, 384), 0, YW, first_ref, [(0, 192, keep_ref), (256, 192, side_ref)]
-    )
-    for y in range(1, YW - 1):
-        r_ref[y] = (x_ref[y, :, 0:192] - keep_ref[y]) + spread(side_ref, y)
+    even_x = gz % 2 == 0
+    sub = lax.broadcasted_iota(jnp.int32, (RW // 2, XH, 192), 1)
+    left = unfolded(jnp.where(even_x, x2_ref[...], x1_ref[...]))
+    right = unfolded(jnp.where(even_x, x1_ref[...], x2_ref[...]))
+    r_ref[1 : YW - 1, 2 * XH : XT] = resid_ref[:, XH : XT - XH]
+    for half in range(2):
+        at = slice(half * (RW // 2), (half + 1) * (RW // 2))
+        rows = slice(1 + at.start, 1 + at.stop)
+        from_left, from_right = left[half], right[half]
+        mine_left, mine_right = edge_ref[at, 0:1], edge_ref[at, 1:2]
+        r_ref[rows, 0:XH] = jnp.where(sub >= 2, from_left, 0.0) + jnp.where(
+            sub == 7, mine_left, 0.0
+        )
+        r_ref[rows, XH : 2 * XH] = resid_ref[at, 0:XH] + jnp.where(sub == 0, from_left[:, 0:1], 0.0)
+        r_ref[rows, XT : XH + XT] = resid_ref[at, XT - XH :] + jnp.where(
+            sub == 7, from_right[:, 7:8], 0.0
+        )
+        r_ref[rows, XH + XT :] = jnp.where(sub <= 5, from_right, 0.0) + jnp.where(
+            sub == 0, mine_right, 0.0
+        )
     clear(r_ref, 1, YW - 1)
     sum_ref[...] = r_ref[own, inner]
 
@@ -359,7 +412,7 @@
         clear(r_ref, lo + 1, hi - 1)
         sum_ref[...] += r_ref[own, inner]
 
-    apply(r_ref, every, 3, YW - 3, fine_ref, [(768, 96, ckeep_ref), (896, 96, cside_ref)])
+    apply(r_ref, every, 3, YW - 3, fine_ref, [(768, 224, (ckeep_ref, cside_ref))])
     apply(
         r_ref, every, HALO - 1, HALO + YT + 1, fine_ref, [(256, 192, keep_ref), (512, 192, side_ref)], 5
     )
@@ -372,7 +425,7 @@
 
     for sweep in (4, 5):
         lo, hi = sweep, YW - sweep
-        apply(rc_ref, every, lo, hi, coarse_ref, [(0, 96, ckeep_ref), (128, 96, cside_ref)], 5)
+        apply(rc_ref, every, lo, hi, coarse_ref, [(0, 224, (ckeep_ref, cside_ref))], 5)
         for y in range(lo + 1, hi - 1):
             rc_ref[y] = ckeep_ref[y] + spread(cside_ref, y)
         clear(rc_ref, lo + 1, hi - 1)
@@ -431,20 +484,32 @@
         name="pack",
     )(right_side, start_field, layer_material)
     got = lax.all_to_all(packed.reshape(8, ROWS, 128), "gz", 0, 0, tiled=True)
-    mats = got[:, 96, :8].reshape(-1).astype(jnp.int32)
-
-    onehot = (mats[:, None] == jnp.arange(stiffness.shape[0])[None, :]).astype(F32)
-    sten = jnp.sum(onehot[:, :, None] * stiffness.reshape(1, -1, 27), axis=1)
-    sten = jnp.pad(sten, ((0, 0), (0, 128 - 27)))
-    fine, coarse, first = pl.pallas_call(
+    mats = got[:, 96:, 0].reshape(-1).astype(jnp.int32)
+
+    table = jnp.pad(stiffness.reshape(-1, 27), ((0, 128 - stiffness.shape[0]), (0, 128 - 27)))
+    own, q, sten, send1, send2 = pl.pallas_call(
+        turn_kernel,
+        out_shape=(
+            shape(YT, XT, 192),
+            shape(YT, XT, 192),
+            shape(NZ, 128),
+            shape(4, XT, 384),
+            shape(4, XT, 384),
+        ),
+        in_specs=[VMEM, VMEM],
+        out_specs=(VMEM,) * 5,
+        scratch_shapes=[pltpu.VMEM((8, XT, 384), F32), pltpu.VMEM((8, XT, 384), F32)],
+        compiler_params=params(),
+        name="turn",
+    )(got, table)
+    fine, coarse = pl.pallas_call(
         setup_kernel,
         out_shape=(
             shape(2, 192, 1024, dtype=BF16),
             shape(2, 96, 1024, dtype=BF16),
-            shape(2, 256, 512, dtype=BF16),
         ),
         in_specs=[SMEM, SMEM, VMEM],
-        out_specs=(VMEM, VMEM, VMEM),
+        out_specs=(VMEM, VMEM),
         scratch_shapes=[
             pltpu.VMEM((192, 192), F32),
             pltpu.VMEM((96, 96), F32),
@@ -453,25 +518,23 @@
         name="setup",
     )(mats, line_factors.reshape(-1), sten)
 
-    own, send1, send2 = pl.pallas_call(
-        turn_kernel,
-        out_shape=(shape(YT, XT, 384), shape(HALO, XT, 384), shape(HALO, XT, 384)),
-        in_specs=[VMEM],
-        out_specs=(VMEM, VMEM, VMEM),
-        compiler_params=params(),
-        name="turn",
-    )(got)
     count_x, count_y, count_z = (lax.axis_size(axis) for axis in ("gx", "gy", "gz"))
     y1 = lax.ppermute(send1, "gy", swaps(range(count_y), 0))
     y2 = lax.ppermute(send2, "gy", swaps(range(count_y), 1))
-    send1, send2 = pl.pallas_call(
+    resid, edge, send1, send2 = pl.pallas_call(
         sides_kernel,
-        out_shape=(shape(YW, XH, 384), shape(YW, XH, 384)),
-        in_specs=[VMEM, VMEM, VMEM, pl.BlockSpec(memory_space=pl.ANY)],
-        out_specs=(VMEM, VMEM),
+        out_shape=(
+            shape(RW, XT, 192),
+            shape(RW, XH, 192),
+            shape(RW // 2, XH, 384),
+            shape(RW // 2, XH, 384),
+        ),
+        in_specs=[VMEM, VMEM, VMEM, VMEM, pl.BlockSpec(memory_space=pl.ANY)],
+        out_specs=(VMEM,) * 4,
+        scratch_shapes=[pltpu.VMEM((RW, XH, 384), F32)],
         compiler_params=params(),
         name="sides",
-    )(own, y1, y2, fine)
+    )(own, q, y1, y2, fine)
     along = [(i % count_z) * count_x + i // count_z for i in range(count_x * count_z)]
     x1 = lax.ppermute(send1, ("gz", "gx"), swaps(along, 0))
     x2 = lax.ppermute(send2, ("gz", "gx"), swaps(along, 1))
@@ -479,10 +542,9 @@
     out = pl.pallas_call(
         cycle_kernel,
         out_shape=shape(8, 96, 128),
-        in_specs=[VMEM] * 8,
+        in_specs=[VMEM] * 6,
         out_specs=VMEM,
         scratch_shapes=[
-            pltpu.VMEM((YW, XW, 384), F32),
             pltpu.VMEM((YW, XW, 192), F32),
             pltpu.VMEM((YW, XW, 192), F32),
             pltpu.VMEM((YW, XW, 192), F32),
@@ -494,7 +556,7 @@
         ],
         compiler_params=params(),
         name="cycle",
-    )(own, y1, y2, x1, x2, fine, coarse, first)
+    )(resid, edge, x1, x2, fine, coarse)
     back = lax.all_to_all(out, "gz", 0, 0, tiled=True)
     return pl.pallas_call(
         unpack_kernel,

time: 61.2 us -> 57.1 us (0.933)
  waiting for transfers between devices: 17.4 us -> 14.4 us
  local copies, waits for them, and re-layouts: 1.19 us -> 0.48 us
    ppermute x1, waiting for transfers between devices: 2.31 us -> 0.01 us  [on_device(): y2 = lax.ppermute(send2, 'gy', swaps(range(count_y), 1))]
    ppermute x1, waiting for transfers between devices: 6.82 us -> 5.24 us  [on_device(): x2 = lax.ppermute(send2, ('gz', 'gx'), swaps(along, 1))]
    pallas_call x1, Pallas kernels: 6.71 us -> 5.16 us  [on_device(): pl.pallas_call(cycle_kernel, out_shape=shape(8, 96, 128), in_specs=[VMEM]...]
    pallas_call x2, Pallas kernels: 0.23 us -> 1.45 us  [the longest x1 1.13 us: on_device(): pl.pallas_call(turn_kernel, out_shape=(shape(YT, XT, 192), shape(YT, XT,...]
    all_to_all x1, waiting for transfers between devices: 8.27 us -> 9.19 us  [on_device(): got = lax.all_to_all(packed.reshape(8, ROWS, 128), 'gz', 0, 0, tiled=True)]
    unnamed x7, local copies, waits for them, and re-layouts: 0.85 us -> 0.15 us
  transfers between devices with their start and end apart: 5 -> 5, of which waited for: 3 -> 2; matrix products, arithmetic and copies ran while one was open for 1% -> 1% of each run, Pallas kernels for 8% -> 8%
where the time goes in v5:
time: 57.1 us; the launch traced here: 56.7 us
  Pallas kernels  15.8 us (28%)
  waiting for transfers between devices  14.4 us (25%)
  starting transfers between devices  13.6 us (24%)
  blocking collectives  11.5 us (20%)
  between operations  0.75 us (1%)
    all_to_all x1, blocking collectives, on_device(): back = lax.all_to_all(out, 'gz', 0, 0, tiled=True)  11.5 us
    all_to_all x1, waiting for transfers between devices, on_device(): got = lax.all_to_all(packed.reshape(8, ROWS, 128), 'gz', 0, 0, tiled=True)  9.19 us
    ppermute x1, starting transfers between devices, on_device(): y2 = lax.ppermute(send2, 'gy', swaps(range(count_y), 1))  5.93 us
    ppermute x1, waiting for transfers between devices, on_device(): x2 = lax.ppermute(send2, ('gz', 'gx'), swaps(along, 1))  5.24 us
    pallas_call x1, Pallas kernels, on_device(): pl.pallas_call(cycle_kernel, out_shape=shape(8, 96, 128), in_specs=[VMEM]...  5.16 us
    pallas_call x1, Pallas kernels, on_device(): pl.pallas_call(setup_kernel, out_shape=(shape(2, 192, 1024, dtype=BF16),...  4.75 us
    all_to_all x1, starting transfers between devices, on_device(): got = lax.all_to_all(packed.reshape(8, ROWS, 128), 'gz', 0, 0, tiled=True)  4.31 us
    ppermute x1, starting transfers between devices, on_device(): x2 = lax.ppermute(send2, ('gz', 'gx'), swaps(along, 1))  3.05 us
  transfers between devices with their start and end apart: 5, of which 2 were waited for; matrix products, arithmetic and copies ran while one was open for 1% of the time, Pallas kernels for 8%

profile of v5, /device:TPU:104, one launch (start us, length us, event | category | flops | bytes accessed | tf_op | source)
XLA Modules:
  0.0 56.7 jit_solution(8032134460643186686)
XLA Ops:
  0.6 2.9 %pack.1 = f32[832,128]{1,0:T(8,128)} custom-call(f32[8,3,8,256]{3,2,1,0:T(8,128)} %load_hbm.1, f32[8,3,8,256]{3,2,1,0:T(8,128)} %start_ref.1, s32[8]{0:T(128)} %mats_hbm.1), custom_call_target="tpu_custom_call" | custom-call | tf_op jit(solution)/shard_map/pack/pallas_call | solution.py:472
  3.5 0.0 copy-start.1
  3.5 4.3 %all-to-all-start = ((f32[8,104,128]{2,1,0:T(8,128)}), f32[8,104,128]{2,1,0:T(8,128)S(1)}, u32[]{:S(2)}, u32[]{:S(2)}) async-start(f32[8,104,128]{2,1,0:T(8,128)} %bitcast.5), calls=%async_computation | async-start | bytes 851968 | tf_op jit(solution)/shard_map/all_to_all | solution.py:486
  7.9 0.0 copy-done.1
  7.9 0.1 copy.8
  8.0 0.0 copy-start.2
  8.0 9.2 %all-to-all-done.got_ref = f32[8,104,128]{2,1,0:T(8,128)S(1)} async-done(((f32[8,104,128]{2,1,0:T(8,128)}), f32[8,104,128]{2,1,0:T(8,128)S(1)}, u32[]{:S(2)}, u32[]{:S(2)}) %all-to-all-start) | async-done | bytes 426016 | tf_op jit(solution)/shard_map/all_to_all | solution.py:486
  17.2 1.1 %turn.1 = (f32[8,32,192]{2,1,0:T(8,128)S(1)}, f32[8,32,192]{2,1,0:T(8,128)S(1)}, f32[64,128]{1,0:T(8,128)S(1)}, f32[4,32,384]{2,1,0:T(8,128)S(1)}, f32[4,32,384]{2,1,0:T(8,128)S(1)}) custom-call(f32[8,104,128]{2,1,0:T(8,128)S(1)} %all-to-all-done.got_ref, f32[128,128]{1,0:T(8,128)S(1)} %pad.4.table_ref), custom_call_target="tpu_custom_call" | custom-call | tf_op jit(solution)/shard_map/turn/pallas_call | solution.py:490
  18.3 0.2 collective-permute-start
  18.5 5.9 %collective-permute-start.1 = (f32[4,32,384]{2,1,0:T(8,128)S(1)}, f32[4,32,384]{2,1,0:T(8,128)S(1)}, u32[]{:S(2)}, u32[]{:S(2)}) collective-permute-start(f32[4,32,384]{2,1,0:T(8,128)S(1)} %get-tuple-element.16), channel_id=1, source_target_pairs={{1,2},{3,4},{5,6},{2,1},{4,3},{6,5},{9,10},{11,12},{13,14},{10,9},... | collective-permute-start | bytes 589832 | tf_op jit(solution)/shard_map/ppermute | solution.py:523
  24.4 0.0 copy-done.2
  24.4 0.1 copy.9
  24.6 0.2 reshape.19.factor_ref
  24.7 0.2 fusion
  25.0 0.1 convert_element_type.8.mats_ref
  25.0 4.7 %setup.1 = (bf16[2,192,1024]{2,1,0:T(8,128)(2,1)S(1)}, bf16[2,96,1024]{2,1,0:T(8,128)(2,1)S(1)}) custom-call(s32[64]{0:T(128)S(1)} %convert_element_type.8.mats_ref, f32[216]{0:T(256)S(1)} %reshape.19.factor_ref, f32[64,128]{1,0:T(8,128)S(1)} %get-tuple-element.17.sten_ref), custom_call_target="tpu_custom_call" | custom-call | tf_op jit(solution)/shard_map/setup/pallas_call | solution.py:505
  29.8 0.0 collective-permute-done.y1_ref
  29.8 0.0 collective-permute-done.1.y2_ref
  29.8 0.3 sides.1
  30.1 0.1 collective-permute-start.2
  30.2 3.1 %collective-permute-start.3 = (f32[10,8,384]{2,1,0:T(8,128)S(1)}, f32[10,8,384]{2,1,0:T(8,128)S(1)}, u32[]{:S(2)}, u32[]{:S(2)}) collective-permute-start(f32[10,8,384]{2,1,0:T(8,128)S(1)} %get-tuple-element.22), channel_id=1, source_target_pairs={{32,64},{96,128},{160,192},{224,8},{40,72},{104,136},{168,200},{23... | collective-permute-start | bytes 368648 | tf_op jit(solution)/shard_map/ppermute | solution.py:540
  33.3 0.0 collective-permute-done.2.x1_ref
  33.3 5.2 %collective-permute-done.3.x2_ref = f32[10,8,384]{2,1,0:T(8,128)S(1)} collective-permute-done((f32[10,8,384]{2,1,0:T(8,128)S(1)}, f32[10,8,384]{2,1,0:T(8,128)S(1)}, u32[]{:S(2)}, u32[]{:S(2)}) %collective-permute-start.3) | collective-permute-done | bytes 122912 | tf_op jit(solution)/shard_map/ppermute | solution.py:540
  38.5 5.2 %cycle.1 = f32[8,96,128]{2,1,0:T(8,128)S(1)} custom-call(f32[20,32,192]{2,1,0:T(8,128)S(1)} %get-tuple-element.19.resid_ref, f32[20,8,192]{2,1,0:T(8,128)S(1)} %get-tuple-element.20.edge_ref, f32[10,8,384]{2,1,0:T(8,128)S(1)} %collective-permute-done.2.x1_ref, f32[10,8,384]{2,1,0:T(8,128)S(1)} %collective-permute-done.3.x2_ref, ...), custom_call_target="tpu_custom_call" | custom-call | tf_op jit(solution)/shard_map/cycle/pallas_call | solution.py:542
  43.7 0.0 copy-start
  43.7 11.5 %all_to_all.10 = f32[8,96,128]{2,1,0:T(8,128)S(1)} all-to-all(f32[8,96,128]{2,1,0:T(8,128)S(1)} %cycle.1), channel_id=1, replica_groups=mesh['gz'=8,'gx'=4,'gy'=8] {'gz'}, dimensions={0} | all-to-all | bytes 786432 | tf_op jit(solution)/shard_map/all_to_all | solution.py:560
  55.2 0.0 copy-done
  55.2 1.5 %unpack.1 = (f32[8,3,8,256]{3,2,1,0:T(8,128)}, f32[8,3,8,256]{3,2,1,0:T(8,128)}) custom-call(f32[768,128]{1,0:T(8,128)S(1)} %bitcast.4, f32[8,3,8,256]{3,2,1,0:T(8,128)S(1)} %copy-done), custom_call_target="tpu_custom_call" | custom-call | tf_op jit(solution)/shard_map/unpack/pallas_call | solution.py:561
  (2 shorter events, 0.0 us)
Async XLA Ops:
  3.5 4.3 %copy-start.1 = (f32[8,3,3,3]{0,3,2,1:T(4,128)S(1)}, f32[8,3,3,3]{0,3,2,1:T(4,128)}, u32[]{:S(2)}) copy-start(f32[8,3,3,3]{0,3,2,1:T(4,128)} %param.8) | copy-start | bytes 2596
  3.5 13.6 %all-to-all-start = ((f32[8,104,128]{2,1,0:T(8,128)}), f32[8,104,128]{2,1,0:T(8,128)S(1)}, u32[]{:S(2)}, u32[]{:S(2)}) async-start(f32[8,104,128]{2,1,0:T(8,128)} %bitcast.5), calls=%async_computation | async-start | bytes 851968 | tf_op jit(solution)/shard_map/all_to_all | solution.py:486
  8.0 16.5 %copy-start.2 = (f32[8,3,3,3]{0,3,2,1:T(4,128)S(1)}, f32[8,3,3,3]{0,3,2,1:T(4,128)}, u32[]{:S(2)}) copy-start(f32[8,3,3,3]{0,3,2,1:T(4,128)} %param.9) | copy-start | bytes 2596
  18.3 11.5 %collective-permute-start = (f32[4,32,384]{2,1,0:T(8,128)S(1)}, f32[4,32,384]{2,1,0:T(8,128)S(1)}, u32[]{:S(2)}, u32[]{:S(2)}) collective-permute-start(f32[4,32,384]{2,1,0:T(8,128)S(1)} %get-tuple-element.15), channel_id=1, source_target_pairs={{0,1},{2,3},{4,5},{6,7},{1,0},{3,2},{5,4},{7,6},{8,9},{10,11},{12,... | collective-permute-start | bytes 589832 | tf_op jit(solution)/shard_map/ppermute | solution.py:522
  18.5 11.3 %collective-permute-start.1 = (f32[4,32,384]{2,1,0:T(8,128)S(1)}, f32[4,32,384]{2,1,0:T(8,128)S(1)}, u32[]{:S(2)}, u32[]{:S(2)}) collective-permute-start(f32[4,32,384]{2,1,0:T(8,128)S(1)} %get-tuple-element.16), channel_id=1, source_target_pairs={{1,2},{3,4},{5,6},{2,1},{4,3},{6,5},{9,10},{11,12},{13,14},{10,9},... | collective-permute-start | bytes 589832 | tf_op jit(solution)/shard_map/ppermute | solution.py:523
  30.1 3.2 %collective-permute-start.2 = (f32[10,8,384]{2,1,0:T(8,128)S(1)}, f32[10,8,384]{2,1,0:T(8,128)S(1)}, u32[]{:S(2)}, u32[]{:S(2)}) collective-permute-start(f32[10,8,384]{2,1,0:T(8,128)S(1)} %get-tuple-element.21), channel_id=1, source_target_pairs={{0,32},{64,96},{128,160},{192,224},{8,40},{72,104},{136,168},{200,... | collective-permute-start | bytes 368648 | tf_op jit(solution)/shard_map/ppermute | solution.py:539
  30.2 8.3 %collective-permute-start.3 = (f32[10,8,384]{2,1,0:T(8,128)S(1)}, f32[10,8,384]{2,1,0:T(8,128)S(1)}, u32[]{:S(2)}, u32[]{:S(2)}) collective-permute-start(f32[10,8,384]{2,1,0:T(8,128)S(1)} %get-tuple-element.22), channel_id=1, source_target_pairs={{32,64},{96,128},{160,192},{224,8},{40,72},{104,136},{168,200},{23... | collective-permute-start | bytes 368648 | tf_op jit(solution)/shard_map/ppermute | solution.py:540
  43.7 11.5 %copy-start = (f32[8,3,8,256]{3,2,1,0:T(8,128)S(1)}, f32[8,3,8,256]{3,2,1,0:T(8,128)}, u32[]{:S(2)}) copy-start(f32[8,3,8,256]{3,2,1,0:T(8,128)} %start_ref.1) | copy-start | bytes 589828

commit v6 on v5

--- a/solution.py
+++ b/solution.py
@@ -250,12 +250,13 @@
     ref[1, :, at : at + value.shape[1]] = low
 
 
-def setup_kernel(
-    mats_ref, factor_ref, sten_ref, fine_ref, coarse_ref, line_ref, cline_ref
-):
-    sten = sten_ref[...]
+def lines_kernel(mats_ref, factor_ref, line_ref, cline_ref):
     line_rows(mats_ref, factor_ref, line_ref, NZ, 1)
     line_rows(mats_ref, factor_ref, cline_ref, NC, 2)
+
+
+def setup_kernel(line_ref, cline_ref, sten_ref, after_ref, fine_ref, coarse_ref):
+    sten = sten_ref[...]
 
     def level(sten_part, scale, ref, layers):
         blocks = [ref[i * layers : (i + 1) * layers, :] for i in range(3)]
@@ -318,10 +319,24 @@
     csum_ref,
 ):
     gz, gx, gy = (lax.axis_index(axis) for axis in ("gz", "gx", "gy"))
-    at_left = (gx == 0) & (gz == 0)
-    at_right = (gx == lax.axis_size("gx") - 1) & (gz == lax.axis_size("gz") - 1)
-    at_top = gy == 0
-    at_bottom = gy == lax.axis_size("gy") - 1
+
+    def unless(outside):
+        return jnp.where(outside, 0.0, 1.0).astype(F32)
+
+    at_left = unless((gx == 0) & (gz == 0))
+    at_right = unless((gx == lax.axis_size("gx") - 1) & (gz == lax.axis_size("gz") - 1))
+    at_top = unless(gy == 0)
+    at_bottom = unless(gy == lax.axis_size("gy") - 1)
+
+    def inside(value, y):
+        value = jnp.concatenate(
+            [value[0:XH] * at_left, value[XH : XH + XT], value[XH + XT :] * at_right], axis=0
+        )
+        if y < HALO:
+            value = value * at_top
+        if y >= HALO + YT:
+            value = value * at_bottom
+        return value
 
     def product(halves, w_ref, at, width):
         high, low = halves
@@ -336,17 +351,22 @@
     def chunks(lo, hi, size):
         return [(y, min(y + size, hi)) for y in range(lo, hi, size)]
 
-    def apply(src, lanes, lo, hi, w_ref, jobs, size=4):
+    def stage(src, lo, hi, w_ref, jobs, emit, size=4):
+        ready = lo + 1
         for a, b in chunks(lo, hi, size):
-            value = src[a:b, :, lanes].reshape((b - a) * XW, -1)
-            halves = split(value)
+            halves = split(src[a:b].reshape((b - a) * XW, -1))
             for at, width, dst in jobs:
+                value = product(halves, w_ref, at, width)
                 if isinstance(dst, tuple):
-                    both = product(halves, w_ref, at, width)
                     for i, part in enumerate(dst):
-                        part[a:b] = both[:, i * 128 : i * 128 + 96].reshape(b - a, XW, 96)
+                        part[a:b] = value[:, i * 128 : i * 128 + 96].reshape(b - a, XW, 96)
                 else:
-                    dst[a:b] = product(halves, w_ref, at, width).reshape(b - a, XW, width)
+                    dst[a:b] = value.reshape(b - a, XW, width)
+            for y in range(ready, a - 1):
+                emit(y)
+            ready = max(ready, a - 1)
+        for y in range(ready, hi - 1):
+            emit(y)
 
     def spread(side, y):
         mid = side[y]
@@ -354,32 +374,8 @@
             pltpu.roll(mid, 1, axis=0) + pltpu.roll(mid, XW - 1, axis=0)
         )
 
-    def clear(ref, lo, hi):
-        width = ref.shape[2]
-
-        @pl.when(at_left)
-        def _():
-            ref[lo:hi, 0:XH] = jnp.zeros((hi - lo, XH, width), F32)
-
-        @pl.when(at_right)
-        def _():
-            ref[lo:hi, XH + XT :] = jnp.zeros((hi - lo, XH, width), F32)
-
-        if lo < HALO:
-
-            @pl.when(at_top)
-            def _():
-                ref[lo:HALO] = jnp.zeros((HALO - lo, XW, width), F32)
-
-        if hi > HALO + YT:
-
-            @pl.when(at_bottom)
-            def _():
-                ref[HALO + YT : hi] = jnp.zeros((hi - HALO - YT, XW, width), F32)
-
     own = slice(HALO, HALO + YT)
     inner = slice(XH, XH + XT)
-    every = slice(None)
 
     even_x = gz % 2 == 0
     sub = lax.broadcasted_iota(jnp.int32, (RW // 2, XH, 192), 1)
@@ -401,48 +397,59 @@
         r_ref[rows, XH + XT :] = jnp.where(sub <= 5, from_right, 0.0) + jnp.where(
             sub == 0, mine_right, 0.0
         )
-    clear(r_ref, 1, YW - 1)
+    for y in range(1, YW - 1):
+        r_ref[y] = inside(r_ref[y], y)
     sum_ref[...] = r_ref[own, inner]
 
+    def next_fine(y):
+        r_ref[y] = inside(keep_ref[y] + spread(side_ref, y), y)
+
+    def next_coarse(y):
+        rc_ref[y] = inside(ckeep_ref[y] + spread(cside_ref, y), y)
+
     for sweep in (1, 2):
-        lo, hi = sweep, YW - sweep
-        apply(r_ref, every, lo, hi, fine_ref, [(256, 192, keep_ref), (512, 192, side_ref)])
-        for y in range(lo + 1, hi - 1):
-            r_ref[y] = keep_ref[y] + spread(side_ref, y)
-        clear(r_ref, lo + 1, hi - 1)
+        stage(
+            r_ref,
+            sweep,
+            YW - sweep,
+            fine_ref,
+            [(256, 192, keep_ref), (512, 192, side_ref)],
+            next_fine,
+        )
         sum_ref[...] += r_ref[own, inner]
 
-    apply(r_ref, every, 3, YW - 3, fine_ref, [(768, 224, (ckeep_ref, cside_ref))])
-    apply(
-        r_ref, every, HALO - 1, HALO + YT + 1, fine_ref, [(256, 192, keep_ref), (512, 192, side_ref)], 5
+    stage(r_ref, 3, YW - 3, fine_ref, [(768, 224, (ckeep_ref, cside_ref))], next_coarse)
+    stage(
+        r_ref,
+        HALO - 1,
+        HALO + YT + 1,
+        fine_ref,
+        [(256, 192, keep_ref), (512, 192, side_ref)],
+        next_fine,
+        5,
     )
-    for y in range(4, YW - 4):
-        rc_ref[y] = ckeep_ref[y] + spread(cside_ref, y)
-    clear(rc_ref, 4, YW - 4)
-    for y in range(HALO, HALO + YT):
-        r_ref[y] = keep_ref[y] + spread(side_ref, y)
-    csum_ref[HALO - 1 : HALO + YT + 1] = rc_ref[HALO - 1 : HALO + YT + 1]
-
+    near = slice(HALO - 1, HALO + YT + 1)
+    csum_ref[near] = rc_ref[near]
     for sweep in (4, 5):
-        lo, hi = sweep, YW - sweep
-        apply(rc_ref, every, lo, hi, coarse_ref, [(0, 224, (ckeep_ref, cside_ref))], 5)
-        for y in range(lo + 1, hi - 1):
-            rc_ref[y] = ckeep_ref[y] + spread(cside_ref, y)
-        clear(rc_ref, lo + 1, hi - 1)
-        csum_ref[HALO - 1 : HALO + YT + 1] += rc_ref[HALO - 1 : HALO + YT + 1]
-
-    apply(
+        stage(
+            rc_ref, sweep, YW - sweep, coarse_ref, [(0, 224, (ckeep_ref, cside_ref))], next_coarse
+        )
+        csum_ref[near] += rc_ref[near]
+
+    resid = []
+
+    def last(y):
+        resid.append(((r_ref[y] - keep_ref[y]) + spread(side_ref, y))[inner])
+
+    stage(
         csum_ref,
-        every,
         HALO - 1,
         HALO + YT + 1,
         coarse_ref,
         [(512, 192, keep_ref), (768, 192, side_ref)],
+        last,
         5,
     )
-    resid = []
-    for y in range(HALO, HALO + YT):
-        resid.append(((r_ref[y] - keep_ref[y]) + spread(side_ref, y))[inner])
     resid = jnp.concatenate(resid, axis=0)
     change = product(split(sum_ref[...].reshape(YT * XT, 192)), fine_ref, 0, 192)
     change = change + product(
@@ -502,22 +509,14 @@
         compiler_params=params(),
         name="turn",
     )(got, table)
-    fine, coarse = pl.pallas_call(
-        setup_kernel,
-        out_shape=(
-            shape(2, 192, 1024, dtype=BF16),
-            shape(2, 96, 1024, dtype=BF16),
-        ),
-        in_specs=[SMEM, SMEM, VMEM],
+    line, cline = pl.pallas_call(
+        lines_kernel,
+        out_shape=(shape(192, 192), shape(96, 96)),
+        in_specs=[SMEM, SMEM],
         out_specs=(VMEM, VMEM),
-        scratch_shapes=[
-            pltpu.VMEM((192, 192), F32),
-            pltpu.VMEM((96, 96), F32),
-        ],
         compiler_params=params(),
-        name="setup",
-    )(mats, line_factors.reshape(-1), sten)
-
+        name="lines",
+    )(mats, line_factors.reshape(-1))
     count_x, count_y, count_z = (lax.axis_size(axis) for axis in ("gx", "gy", "gz"))
     y1 = lax.ppermute(send1, "gy", swaps(range(count_y), 0))
     y2 = lax.ppermute(send2, "gy", swaps(range(count_y), 1))
@@ -534,11 +533,19 @@
         scratch_shapes=[pltpu.VMEM((RW, XH, 384), F32)],
         compiler_params=params(),
         name="sides",
-    )(own, q, y1, y2, fine)
+    )(own, q, y1, y2, line)
     along = [(i % count_z) * count_x + i // count_z for i in range(count_x * count_z)]
     x1 = lax.ppermute(send1, ("gz", "gx"), swaps(along, 0))
     x2 = lax.ppermute(send2, ("gz", "gx"), swaps(along, 1))
 
+    fine, coarse = pl.pallas_call(
+        setup_kernel,
+        out_shape=(shape(2, 192, 1024, dtype=BF16), shape(2, 96, 1024, dtype=BF16)),
+        in_specs=[VMEM, VMEM, VMEM, pl.BlockSpec(memory_space=pl.ANY)],
+        out_specs=(VMEM, VMEM),
+        compiler_params=params(),
+        name="setup",
+    )(line, cline, sten, edge)
     out = pl.pallas_call(
         cycle_kernel,
         out_shape=shape(8, 96, 128),

time: 57.1 us -> 55.2 us (0.967)
  Pallas kernels: 15.8 us -> 14.9 us
  waiting for transfers between devices: 14.4 us -> 13.5 us
    pallas_call x0 -> x1, Pallas kernels: none -> 3.82 us  [on_device(): pl.pallas_call(lines_kernel, out_shape=(shape(192, 192), shape(96, 96)),...]
    pallas_call x1, Pallas kernels: 4.75 us -> 0.98 us  [on_device(): pl.pallas_call(setup_kernel, out_shape=(shape(2, 192, 1024, dtype=BF16),...]
    ppermute x1, waiting for transfers between devices: 5.24 us -> 4.26 us  [on_device(): x2 = lax.ppermute(send2, ('gz', 'gx'), swaps(along, 1))]
    pallas_call x1, Pallas kernels: 5.16 us -> 4.2 us  [on_device(): pl.pallas_call(cycle_kernel, out_shape=shape(8, 96, 128), in_specs=[VMEM]...]
  transfers between devices with their start and end apart: 5 -> 5, of which waited for: 2 -> 2; matrix products, arithmetic and copies ran while one was open for 1% -> 1% of each run, Pallas kernels for 8% -> 9%
where the time goes in v6:
time: 55.2 us; the launch traced here: 54.8 us
  Pallas kernels  14.9 us (27%)
  starting transfers between devices  13.6 us (25%)
  waiting for transfers between devices  13.5 us (24%)
  blocking collectives  11.5 us (21%)
  between operations  0.75 us (1%)
    all_to_all x1, blocking collectives, on_device(): back = lax.all_to_all(out, 'gz', 0, 0, tiled=True)  11.5 us
    all_to_all x1, waiting for transfers between devices, on_device(): got = lax.all_to_all(packed.reshape(8, ROWS, 128), 'gz', 0, 0, tiled=True)  9.19 us
    ppermute x1, starting transfers between devices, on_device(): y2 = lax.ppermute(send2, 'gy', swaps(range(count_y), 1))  5.93 us
    all_to_all x1, starting transfers between devices, on_device(): got = lax.all_to_all(packed.reshape(8, ROWS, 128), 'gz', 0, 0, tiled=True)  4.31 us
    ppermute x1, waiting for transfers between devices, on_device(): x2 = lax.ppermute(send2, ('gz', 'gx'), swaps(along, 1))  4.26 us
    pallas_call x1, Pallas kernels, on_device(): pl.pallas_call(cycle_kernel, out_shape=shape(8, 96, 128), in_specs=[VMEM]...  4.2 us
    pallas_call x1, Pallas kernels, on_device(): pl.pallas_call(lines_kernel, out_shape=(shape(192, 192), shape(96, 96)),...  3.82 us
    ppermute x1, starting transfers between devices, on_device(): x2 = lax.ppermute(send2, ('gz', 'gx'), swaps(along, 1))  3.05 us
  transfers between devices with their start and end apart: 5, of which 2 were waited for; matrix products, arithmetic and copies ran while one was open for 1% of the time, Pallas kernels for 9%

profile of v6, /device:TPU:104, one launch (start us, length us, event | category | flops | bytes accessed | tf_op | source)
XLA Modules:
  0.0 54.8 jit_solution(5844810773402085301)
XLA Ops:
  0.6 2.9 %pack.1 = f32[832,128]{1,0:T(8,128)} custom-call(f32[8,3,8,256]{3,2,1,0:T(8,128)} %load_hbm.1, f32[8,3,8,256]{3,2,1,0:T(8,128)} %start_ref.1, s32[8]{0:T(128)} %mats_hbm.1), custom_call_target="tpu_custom_call" | custom-call | tf_op jit(solution)/shard_map/pack/pallas_call | solution.py:479
  3.5 0.0 copy-start.1
  3.5 4.3 %all-to-all-start = ((f32[8,104,128]{2,1,0:T(8,128)}), f32[8,104,128]{2,1,0:T(8,128)S(1)}, u32[]{:S(2)}, u32[]{:S(2)}) async-start(f32[8,104,128]{2,1,0:T(8,128)} %bitcast.5), calls=%async_computation | async-start | bytes 851968 | tf_op jit(solution)/shard_map/all_to_all | solution.py:493
  7.9 0.0 copy-done.1
  7.9 0.1 copy.8
  8.0 0.0 copy-start.2
  8.0 9.2 %all-to-all-done.got_ref = f32[8,104,128]{2,1,0:T(8,128)S(1)} async-done(((f32[8,104,128]{2,1,0:T(8,128)}), f32[8,104,128]{2,1,0:T(8,128)S(1)}, u32[]{:S(2)}, u32[]{:S(2)}) %all-to-all-start) | async-done | bytes 426016 | tf_op jit(solution)/shard_map/all_to_all | solution.py:493
  17.2 1.1 %turn.1 = (f32[8,32,192]{2,1,0:T(8,128)S(1)}, f32[8,32,192]{2,1,0:T(8,128)S(1)}, f32[64,128]{1,0:T(8,128)S(1)}, f32[4,32,384]{2,1,0:T(8,128)S(1)}, f32[4,32,384]{2,1,0:T(8,128)S(1)}) custom-call(f32[8,104,128]{2,1,0:T(8,128)S(1)} %all-to-all-done.got_ref, f32[128,128]{1,0:T(8,128)S(1)} %pad.4.table_ref), custom_call_target="tpu_custom_call" | custom-call | tf_op jit(solution)/shard_map/turn/pallas_call | solution.py:497
  18.3 0.2 collective-permute-start
  18.5 5.9 %collective-permute-start.1 = (f32[4,32,384]{2,1,0:T(8,128)S(1)}, f32[4,32,384]{2,1,0:T(8,128)S(1)}, u32[]{:S(2)}, u32[]{:S(2)}) collective-permute-start(f32[4,32,384]{2,1,0:T(8,128)S(1)} %get-tuple-element.18), channel_id=1, source_target_pairs={{1,2},{3,4},{5,6},{2,1},{4,3},{6,5},{9,10},{11,12},{13,14},{10,9},... | collective-permute-start | bytes 589832 | tf_op jit(solution)/shard_map/ppermute | solution.py:522
  24.4 0.0 copy-done.2
  24.4 0.1 copy.9
  24.6 0.2 reshape.19.factor_ref
  24.7 0.2 fusion
  24.9 0.1 convert_element_type.8.mats_ref
  25.0 3.8 %lines.1 = (f32[192,192]{1,0:T(8,128)S(1)}, f32[96,96]{1,0:T(8,128)S(1)}) custom-call(s32[64]{0:T(128)S(1)} %convert_element_type.8.mats_ref, f32[216]{0:T(256)S(1)} %reshape.19.factor_ref), custom_call_target="tpu_custom_call" | custom-call | tf_op jit(solution)/shard_map/lines/pallas_call | solution.py:512
  28.8 0.0 collective-permute-done.y1_ref
  28.9 0.0 collective-permute-done.1.y2_ref
  28.9 0.3 sides.1
  29.2 0.1 collective-permute-start.2
  29.3 3.1 %collective-permute-start.3 = (f32[10,8,384]{2,1,0:T(8,128)S(1)}, f32[10,8,384]{2,1,0:T(8,128)S(1)}, u32[]{:S(2)}, u32[]{:S(2)}) collective-permute-start(f32[10,8,384]{2,1,0:T(8,128)S(1)} %get-tuple-element.23), channel_id=1, source_target_pairs={{32,64},{96,128},{160,192},{224,8},{40,72},{104,136},{168,200},{23... | collective-permute-start | bytes 368648 | tf_op jit(solution)/shard_map/ppermute | solution.py:539
  32.4 1.0 %setup.1 = (bf16[2,192,1024]{2,1,0:T(8,128)(2,1)S(1)}, bf16[2,96,1024]{2,1,0:T(8,128)(2,1)S(1)}) custom-call(f32[192,192]{1,0:T(8,128)S(1)} %get-tuple-element.19.after_ref.line_ref, f32[96,96]{1,0:T(8,128)S(1)} %get-tuple-element.24.cline_ref, f32[64,128]{1,0:T(8,128)S(1)} %get-tuple-element.25.sten_ref, f32[20,8,192]{2,1,0:T(8,128)S(1)} %get-tuple-element.21.after_ref.edge_ref), custom_call_target="tpu_custom_call" | custom-call | tf_op jit(solution)/shard_map/setup/pallas_call | solution.py:541
  33.3 0.0 collective-permute-done.2.x1_ref
  33.3 4.3 %collective-permute-done.3.x2_ref = f32[10,8,384]{2,1,0:T(8,128)S(1)} collective-permute-done((f32[10,8,384]{2,1,0:T(8,128)S(1)}, f32[10,8,384]{2,1,0:T(8,128)S(1)}, u32[]{:S(2)}, u32[]{:S(2)}) %collective-permute-start.3) | collective-permute-done | bytes 122912 | tf_op jit(solution)/shard_map/ppermute | solution.py:539
  37.6 4.2 %cycle.1 = f32[8,96,128]{2,1,0:T(8,128)S(1)} custom-call(f32[20,32,192]{2,1,0:T(8,128)S(1)} %get-tuple-element.20.resid_ref, f32[20,8,192]{2,1,0:T(8,128)S(1)} %get-tuple-element.21.after_ref.edge_ref, f32[10,8,384]{2,1,0:T(8,128)S(1)} %collective-permute-done.2.x1_ref, f32[10,8,384]{2,1,0:T(8,128)S(1)} %collective-permute-done.3.x2_ref, ...), custom_call_target="tpu_custom_call" | custom-call | tf_op jit(solution)/shard_map/cycle/pallas_call | solution.py:549
  41.8 0.0 copy-start
  41.8 11.5 %all_to_all.10 = f32[8,96,128]{2,1,0:T(8,128)S(1)} all-to-all(f32[8,96,128]{2,1,0:T(8,128)S(1)} %cycle.1), channel_id=1, replica_groups=mesh['gz'=8,'gx'=4,'gy'=8] {'gz'}, dimensions={0} | all-to-all | bytes 786432 | tf_op jit(solution)/shard_map/all_to_all | solution.py:567
  53.3 0.0 copy-done
  53.3 1.5 %unpack.1 = (f32[8,3,8,256]{3,2,1,0:T(8,128)}, f32[8,3,8,256]{3,2,1,0:T(8,128)}) custom-call(f32[768,128]{1,0:T(8,128)S(1)} %bitcast.4, f32[8,3,8,256]{3,2,1,0:T(8,128)S(1)} %copy-done), custom_call_target="tpu_custom_call" | custom-call | tf_op jit(solution)/shard_map/unpack/pallas_call | solution.py:568
  (2 shorter events, 0.0 us)
Async XLA Ops:
  3.5 4.3 %copy-start.1 = (f32[8,3,3,3]{0,3,2,1:T(4,128)S(1)}, f32[8,3,3,3]{0,3,2,1:T(4,128)}, u32[]{:S(2)}) copy-start(f32[8,3,3,3]{0,3,2,1:T(4,128)} %param.8) | copy-start | bytes 2596
  3.5 13.6 %all-to-all-start = ((f32[8,104,128]{2,1,0:T(8,128)}), f32[8,104,128]{2,1,0:T(8,128)S(1)}, u32[]{:S(2)}, u32[]{:S(2)}) async-start(f32[8,104,128]{2,1,0:T(8,128)} %bitcast.5), calls=%async_computation | async-start | bytes 851968 | tf_op jit(solution)/shard_map/all_to_all | solution.py:493
  8.0 16.5 %copy-start.2 = (f32[8,3,3,3]{0,3,2,1:T(4,128)S(1)}, f32[8,3,3,3]{0,3,2,1:T(4,128)}, u32[]{:S(2)}) copy-start(f32[8,3,3,3]{0,3,2,1:T(4,128)} %param.9) | copy-start | bytes 2596
  18.3 10.6 %collective-permute-start = (f32[4,32,384]{2,1,0:T(8,128)S(1)}, f32[4,32,384]{2,1,0:T(8,128)S(1)}, u32[]{:S(2)}, u32[]{:S(2)}) collective-permute-start(f32[4,32,384]{2,1,0:T(8,128)S(1)} %get-tuple-element.17), channel_id=1, source_target_pairs={{0,1},{2,3},{4,5},{6,7},{1,0},{3,2},{5,4},{7,6},{8,9},{10,11},{12,... | collective-permute-start | bytes 589832 | tf_op jit(solution)/shard_map/ppermute | solution.py:521
  18.5 10.4 %collective-permute-start.1 = (f32[4,32,384]{2,1,0:T(8,128)S(1)}, f32[4,32,384]{2,1,0:T(8,128)S(1)}, u32[]{:S(2)}, u32[]{:S(2)}) collective-permute-start(f32[4,32,384]{2,1,0:T(8,128)S(1)} %get-tuple-element.18), channel_id=1, source_target_pairs={{1,2},{3,4},{5,6},{2,1},{4,3},{6,5},{9,10},{11,12},{13,14},{10,9},... | collective-permute-start | bytes 589832 | tf_op jit(solution)/shard_map/ppermute | solution.py:522
  29.2 4.1 %collective-permute-start.2 = (f32[10,8,384]{2,1,0:T(8,128)S(1)}, f32[10,8,384]{2,1,0:T(8,128)S(1)}, u32[]{:S(2)}, u32[]{:S(2)}) collective-permute-start(f32[10,8,384]{2,1,0:T(8,128)S(1)} %get-tuple-element.22), channel_id=1, source_target_pairs={{0,32},{64,96},{128,160},{192,224},{8,40},{72,104},{136,168},{200,... | collective-permute-start | bytes 368648 | tf_op jit(solution)/shard_map/ppermute | solution.py:538
  29.3 8.3 %collective-permute-start.3 = (f32[10,8,384]{2,1,0:T(8,128)S(1)}, f32[10,8,384]{2,1,0:T(8,128)S(1)}, u32[]{:S(2)}, u32[]{:S(2)}) collective-permute-start(f32[10,8,384]{2,1,0:T(8,128)S(1)} %get-tuple-element.23), channel_id=1, source_target_pairs={{32,64},{96,128},{160,192},{224,8},{40,72},{104,136},{168,200},{23... | collective-permute-start | bytes 368648 | tf_op jit(solution)/shard_map/ppermute | solution.py:539
  41.8 11.5 %copy-start = (f32[8,3,8,256]{3,2,1,0:T(8,128)S(1)}, f32[8,3,8,256]{3,2,1,0:T(8,128)}, u32[]{:S(2)}) copy-start(f32[8,3,8,256]{3,2,1,0:T(8,128)} %start_ref.1) | copy-start | bytes 589828

commit v7 on v6

--- a/solution.py
+++ b/solution.py
@@ -15,6 +15,7 @@
 YW = YT + 2 * HALO
 RH = HALO - 1
 RW = YT + 2 * RH
+MID = slice(8, 24)
 ROWS = 104
 NZ = 64
 NC = NZ // 2
@@ -301,87 +302,136 @@
     store_split(coarse_ref, 768, couple(sten, 1, spread))
 
 
-def cycle_kernel(
-    resid_ref,
-    edge_ref,
-    x1_ref,
-    x2_ref,
+def unless(outside):
+    return jnp.where(outside, 0.0, 1.0).astype(F32)
+
+
+def product(halves, w_ref, at, width):
+    high, low = halves
+    wh = w_ref[0, :, at : at + width]
+    wl = w_ref[1, :, at : at + width]
+
+    def dot(a, b):
+        return jnp.dot(a, b, preferred_element_type=F32)
+
+    return dot(high, wh) + (dot(high, wl) + dot(low, wh))
+
+
+def run_cycle(
+    sides,
+    spread,
+    inside,
     fine_ref,
     coarse_ref,
-    out_ref,
     r_ref,
     keep_ref,
-    side_ref,
     sum_ref,
     rc_ref,
     ckeep_ref,
-    cside_ref,
     csum_ref,
 ):
-    gz, gx, gy = (lax.axis_index(axis) for axis in ("gz", "gx", "gy"))
-
-    def unless(outside):
-        return jnp.where(outside, 0.0, 1.0).astype(F32)
-
+    def stage(i, src, lo, hi, w_ref, at, emit, size=6):
+        ready = lo + 1
+        for a in range(lo, hi, size):
+            b = min(a + size, hi)
+            halves = split(src[a:b].reshape((b - a) * XT, -1))
+            if isinstance(at, tuple):
+                for start, dst in zip(at, (keep_ref, sides[i])):
+                    value = product(halves, w_ref, start, 192)
+                    dst[a:b] = value.reshape(b - a, XT, 192)
+            else:
+                value = product(halves, w_ref, at, 224)
+                for start, dst in ((0, ckeep_ref), (128, sides[i])):
+                    dst[a:b] = value[:, start : start + 96].reshape(b - a, XT, 96)
+            for y in range(ready, a - 1):
+                emit(i, y)
+            ready = max(ready, a - 1)
+        for y in range(ready, hi - 1):
+            emit(i, y)
+
+    def next_fine(i, y):
+        r_ref[y] = inside(keep_ref[y] + spread(i, y), y)
+
+    def next_coarse(i, y):
+        rc_ref[y] = inside(ckeep_ref[y] + spread(i, y), y)
+
+    resid = []
+
+    def last(i, y):
+        resid.append(((r_ref[y] - keep_ref[y]) + spread(i, y))[MID])
+
+    own = slice(HALO, HALO + YT)
+    near = slice(HALO - 1, HALO + YT + 1)
+    sum_ref[...] = r_ref[own, MID]
+    for i, lo in ((0, 1), (1, 2)):
+        stage(i, r_ref, lo, YW - lo, fine_ref, (256, 512), next_fine)
+        sum_ref[...] += r_ref[own, MID]
+    stage(2, r_ref, 3, YW - 3, fine_ref, 768, next_coarse)
+    stage(3, r_ref, near.start, near.stop, fine_ref, (256, 512), next_fine, 5)
+    csum_ref[near] = rc_ref[near]
+    for i, lo in ((4, 4), (5, 5)):
+        stage(i, rc_ref, lo, YW - lo, coarse_ref, 0, next_coarse)
+        csum_ref[near] += rc_ref[near]
+    stage(6, csum_ref, near.start, near.stop, coarse_ref, (512, 768), last, 5)
+    change = product(split(sum_ref[...].reshape(YT * 16, 192)), fine_ref, 0, 192)
+    change = change + product(
+        split(csum_ref[own, MID].reshape(YT * 16, 96)), coarse_ref, 256, 192
+    )
+    return change.reshape(YT, 16, 192), jnp.stack(resid, axis=0)
+
+
+def rows_inside(value, y):
+    gy = lax.axis_index("gy")
+    if y < HALO:
+        value = value * unless(gy == 0)
+    if y >= HALO + YT:
+        value = value * unless(gy == lax.axis_size("gy") - 1)
+    return value
+
+
+def middle_kernel(resid_ref, fine_ref, coarse_ref, *refs):
+    sides, change_ref, out_ref, scratch = refs[:7], refs[7], refs[8], refs[9:]
+    r_ref = scratch[0]
+
+    def spread(i, y):
+        mid = sides[i][y]
+        return (sides[i][y - 1] + sides[i][y + 1]) + (
+            pltpu.roll(mid, 1, axis=0) + pltpu.roll(mid, XT - 1, axis=0)
+        )
+
+    for y in range(1, YW - 1):
+        r_ref[y] = rows_inside(resid_ref[y - 1], y)
+    change_ref[...], out_ref[...] = run_cycle(
+        sides, spread, rows_inside, fine_ref, coarse_ref, *scratch
+    )
+
+
+def strips_kernel(resid_ref, edge_ref, x1_ref, x2_ref, fine_ref, coarse_ref, *refs):
+    saved, change_ref, mid_ref, out_ref = refs[:7], refs[7], refs[8], refs[9]
+    side_ref, cside_ref, scratch = refs[10], refs[11], refs[12:]
+    r_ref = scratch[0]
+    gz, gx = lax.axis_index("gz"), lax.axis_index("gx")
     at_left = unless((gx == 0) & (gz == 0))
     at_right = unless((gx == lax.axis_size("gx") - 1) & (gz == lax.axis_size("gz") - 1))
-    at_top = unless(gy == 0)
-    at_bottom = unless(gy == lax.axis_size("gy") - 1)
+    sides = [cside_ref if i in (2, 4, 5) else side_ref for i in range(7)]
 
     def inside(value, y):
         value = jnp.concatenate(
-            [value[0:XH] * at_left, value[XH : XH + XT], value[XH + XT :] * at_right], axis=0
+            [value[0:XH] * at_left, value[XH : 3 * XH], value[3 * XH :] * at_right], axis=0
         )
-        if y < HALO:
-            value = value * at_top
-        if y >= HALO + YT:
-            value = value * at_bottom
-        return value
-
-    def product(halves, w_ref, at, width):
-        high, low = halves
-        wh = w_ref[0, :, at : at + width]
-        wl = w_ref[1, :, at : at + width]
-
-        def dot(a, b):
-            return jnp.dot(a, b, preferred_element_type=F32)
-
-        return dot(high, wh) + (dot(high, wl) + dot(low, wh))
-
-    def chunks(lo, hi, size):
-        return [(y, min(y + size, hi)) for y in range(lo, hi, size)]
-
-    def stage(src, lo, hi, w_ref, jobs, emit, size=4):
-        ready = lo + 1
-        for a, b in chunks(lo, hi, size):
-            halves = split(src[a:b].reshape((b - a) * XW, -1))
-            for at, width, dst in jobs:
-                value = product(halves, w_ref, at, width)
-                if isinstance(dst, tuple):
-                    for i, part in enumerate(dst):
-                        part[a:b] = value[:, i * 128 : i * 128 + 96].reshape(b - a, XW, 96)
-                else:
-                    dst[a:b] = value.reshape(b - a, XW, width)
-            for y in range(ready, a - 1):
-                emit(y)
-            ready = max(ready, a - 1)
-        for y in range(ready, hi - 1):
-            emit(y)
-
-    def spread(side, y):
+        return rows_inside(value, y)
+
+    def spread(i, y):
+        side = sides[i]
         mid = side[y]
-        return (side[y - 1] + side[y + 1]) + (
-            pltpu.roll(mid, 1, axis=0) + pltpu.roll(mid, XW - 1, axis=0)
-        )
-
-    own = slice(HALO, HALO + YT)
-    inner = slice(XH, XH + XT)
+        row = jnp.concatenate([mid[0:16], saved[i][y, MID], mid[16:32]], axis=0)
+        row = pltpu.roll(row, 1, axis=0) + pltpu.roll(row, XW - 1, axis=0)
+        return (side[y - 1] + side[y + 1]) + jnp.concatenate([row[0:16], row[XT:]], axis=0)
 
     even_x = gz % 2 == 0
     sub = lax.broadcasted_iota(jnp.int32, (RW // 2, XH, 192), 1)
     left = unfolded(jnp.where(even_x, x2_ref[...], x1_ref[...]))
     right = unfolded(jnp.where(even_x, x1_ref[...], x2_ref[...]))
-    r_ref[1 : YW - 1, 2 * XH : XT] = resid_ref[:, XH : XT - XH]
     for half in range(2):
         at = slice(half * (RW // 2), (half + 1) * (RW // 2))
         rows = slice(1 + at.start, 1 + at.stop)
@@ -391,78 +441,29 @@
             sub == 7, mine_left, 0.0
         )
         r_ref[rows, XH : 2 * XH] = resid_ref[at, 0:XH] + jnp.where(sub == 0, from_left[:, 0:1], 0.0)
-        r_ref[rows, XT : XH + XT] = resid_ref[at, XT - XH :] + jnp.where(
+        r_ref[rows, 2 * XH : 3 * XH] = resid_ref[at, XT - XH :] + jnp.where(
             sub == 7, from_right[:, 7:8], 0.0
         )
-        r_ref[rows, XH + XT :] = jnp.where(sub <= 5, from_right, 0.0) + jnp.where(
+        r_ref[rows, 3 * XH :] = jnp.where(sub <= 5, from_right, 0.0) + jnp.where(
             sub == 0, mine_right, 0.0
         )
     for y in range(1, YW - 1):
         r_ref[y] = inside(r_ref[y], y)
-    sum_ref[...] = r_ref[own, inner]
-
-    def next_fine(y):
-        r_ref[y] = inside(keep_ref[y] + spread(side_ref, y), y)
-
-    def next_coarse(y):
-        rc_ref[y] = inside(ckeep_ref[y] + spread(cside_ref, y), y)
-
-    for sweep in (1, 2):
-        stage(
-            r_ref,
-            sweep,
-            YW - sweep,
-            fine_ref,
-            [(256, 192, keep_ref), (512, 192, side_ref)],
-            next_fine,
-        )
-        sum_ref[...] += r_ref[own, inner]
-
-    stage(r_ref, 3, YW - 3, fine_ref, [(768, 224, (ckeep_ref, cside_ref))], next_coarse)
-    stage(
-        r_ref,
-        HALO - 1,
-        HALO + YT + 1,
-        fine_ref,
-        [(256, 192, keep_ref), (512, 192, side_ref)],
-        next_fine,
-        5,
-    )
-    near = slice(HALO - 1, HALO + YT + 1)
-    csum_ref[near] = rc_ref[near]
-    for sweep in (4, 5):
-        stage(
-            rc_ref, sweep, YW - sweep, coarse_ref, [(0, 224, (ckeep_ref, cside_ref))], next_coarse
-        )
-        csum_ref[near] += rc_ref[near]
-
-    resid = []
-
-    def last(y):
-        resid.append(((r_ref[y] - keep_ref[y]) + spread(side_ref, y))[inner])
-
-    stage(
-        csum_ref,
-        HALO - 1,
-        HALO + YT + 1,
-        coarse_ref,
-        [(512, 192, keep_ref), (768, 192, side_ref)],
-        last,
-        5,
-    )
-    resid = jnp.concatenate(resid, axis=0)
-    change = product(split(sum_ref[...].reshape(YT * XT, 192)), fine_ref, 0, 192)
-    change = change + product(
-        split(csum_ref[own, inner].reshape(YT * XT, 96)), coarse_ref, 256, 192
-    )
-    for f, value in enumerate((change, resid)):
-        turned = jnp.transpose(value)
+    change, resid = run_cycle(sides, spread, inside, fine_ref, coarse_ref, *scratch)
+    for f, (value, middle) in enumerate(((change, change_ref[...]), (resid, mid_ref[...]))):
+        value = jnp.concatenate([value[:, 0:8], middle, value[:, 8:16]], axis=1)
+        turned = jnp.transpose(value.reshape(YT * XT, 192))
         for c in range(3):
             for g in range(8):
                 rows = turned[c * NZ + g * 8 : c * NZ + g * 8 + 8]
                 for h in range(2):
                     at = h * 48 + f * 24 + c * 8
                     out_ref[g, at : at + 8, :] = rows[:, h * 128 : h * 128 + 128]
+
+
+def cycle_scratch():
+    fine, coarse = pltpu.VMEM((YW, XT, 192), F32), pltpu.VMEM((YW, XT, 96), F32)
+    return [fine, fine, pltpu.VMEM((YT, 16, 192), F32), coarse, coarse, coarse]
 
 
 def shape(*dims, dtype=F32):
@@ -546,24 +547,29 @@
         compiler_params=params(),
         name="setup",
     )(line, cline, sten, edge)
+    sides = tuple(shape(YW, XT, 96 if i in (2, 4, 5) else 192) for i in range(7))
+    middle = pl.pallas_call(
+        middle_kernel,
+        out_shape=(*sides, shape(YT, 16, 192), shape(YT, 16, 192)),
+        in_specs=[VMEM] * 3,
+        out_specs=(VMEM,) * 9,
+        scratch_shapes=cycle_scratch(),
+        compiler_params=params(),
+        name="middle",
+    )(resid, fine, coarse)
     out = pl.pallas_call(
-        cycle_kernel,
+        strips_kernel,
         out_shape=shape(8, 96, 128),
-        in_specs=[VMEM] * 6,
+        in_specs=[VMEM] * 15,
         out_specs=VMEM,
         scratch_shapes=[
-            pltpu.VMEM((YW, XW, 192), F32),
-            pltpu.VMEM((YW, XW, 192), F32),
-            pltpu.VMEM((YW, XW, 192), F32),
-            pltpu.VMEM((YT, XT, 192), F32),
-            pltpu.VMEM((YW, XW, 96), F32),
-            pltpu.VMEM((YW, XW, 96), F32),
-            pltpu.VMEM((YW, XW, 96), F32),
-            pltpu.VMEM((YW, XW, 96), F32),
+            pltpu.VMEM((YW, XT, 192), F32),
+            pltpu.VMEM((YW, XT, 96), F32),
+            *cycle_scratch(),
         ],
         compiler_params=params(),
-        name="cycle",
-    )(resid, edge, x1, x2, fine, coarse)
+        name="strips",
+    )(resid, edge, x1, x2, fine, coarse, *middle)
     back = lax.all_to_all(out, "gz", 0, 0, tiled=True)
     return pl.pallas_call(
         unpack_kernel,

time: 55.2 us -> 54.5 us (0.987)
  waiting for transfers between devices: 13.5 us -> 10.4 us
  Pallas kernels: 14.9 us -> 16.9 us
    ppermute x1, waiting for transfers between devices: 4.26 us -> 1.2 us  [on_device(): x2 = lax.ppermute(send2, ('gz', 'gx'), swaps(along, 1))]
    pallas_call x1 -> x2, Pallas kernels: 4.2 us -> 6.23 us  [the longest x1 3.19 us: on_device(): pl.pallas_call(strips_kernel, out_shape=shape(8, 96, 128), in_specs=[VMEM...]
  transfers between devices with their start and end apart: 5 -> 5, of which waited for: 2 -> 2; matrix products, arithmetic and copies ran while one was open for 1% -> 1% of each run, Pallas kernels for 9% -> 14%
where the time goes in v7:
time: 54.5 us; the launch traced here: 54.2 us
  Pallas kernels  16.9 us (31%)
  starting transfers between devices  13.6 us (25%)
  blocking collectives  11.8 us (22%)
  waiting for transfers between devices  10.4 us (19%)
  between operations  0.76 us (1%)
    all_to_all x1, blocking collectives, on_device(): back = lax.all_to_all(out, 'gz', 0, 0, tiled=True)  11.8 us
    all_to_all x1, waiting for transfers between devices, on_device(): got = lax.all_to_all(packed.reshape(8, ROWS, 128), 'gz', 0, 0, tiled=True)  9.19 us
    ppermute x1, starting transfers between devices, on_device(): y2 = lax.ppermute(send2, 'gy', swaps(range(count_y), 1))  5.93 us
    all_to_all x1, starting transfers between devices, on_device(): got = lax.all_to_all(packed.reshape(8, ROWS, 128), 'gz', 0, 0, tiled=True)  4.31 us
    pallas_call x1, Pallas kernels, on_device(): pl.pallas_call(lines_kernel, out_shape=(shape(192, 192), shape(96, 96)),...  3.82 us
    pallas_call x1, Pallas kernels, on_device(): pl.pallas_call(strips_kernel, out_shape=shape(8, 96, 128), in_specs=[VMEM...  3.19 us
    ppermute x1, starting transfers between devices, on_device(): x2 = lax.ppermute(send2, ('gz', 'gx'), swaps(along, 1))  3.05 us
    pallas_call x1, Pallas kernels, on_device(): pl.pallas_call(middle_kernel, out_shape=(*sides, shape(YT, 16, 192), shap...  3.04 us
  transfers between devices with their start and end apart: 5, of which 2 were waited for; matrix products, arithmetic and copies ran while one was open for 1% of the time, Pallas kernels for 14%

profile of v7, /device:TPU:104, one launch (start us, length us, event | category | flops | bytes accessed | tf_op | source)
XLA Modules:
  0.0 54.2 jit_solution(11707127045383327532)
XLA Ops:
  0.6 2.9 %pack.1 = f32[832,128]{1,0:T(8,128)} custom-call(f32[8,3,8,256]{3,2,1,0:T(8,128)} %load_hbm.1, f32[8,3,8,256]{3,2,1,0:T(8,128)} %start_ref.1, s32[8]{0:T(128)} %mats_hbm.1), custom_call_target="tpu_custom_call" | custom-call | tf_op jit(solution)/shard_map/pack/pallas_call | solution.py:480
  3.5 0.0 copy-start.1
  3.5 4.3 %all-to-all-start = ((f32[8,104,128]{2,1,0:T(8,128)}), f32[8,104,128]{2,1,0:T(8,128)S(1)}, u32[]{:S(2)}, u32[]{:S(2)}) async-start(f32[8,104,128]{2,1,0:T(8,128)} %bitcast.5), calls=%async_computation | async-start | bytes 851968 | tf_op jit(solution)/shard_map/all_to_all | solution.py:494
  7.9 0.0 copy-done.1
  7.9 0.1 copy.8
  8.0 0.0 copy-start.2
  8.0 9.2 %all-to-all-done.got_ref = f32[8,104,128]{2,1,0:T(8,128)S(1)} async-done(((f32[8,104,128]{2,1,0:T(8,128)}), f32[8,104,128]{2,1,0:T(8,128)S(1)}, u32[]{:S(2)}, u32[]{:S(2)}) %all-to-all-start) | async-done | bytes 426016 | tf_op jit(solution)/shard_map/all_to_all | solution.py:494
  17.2 1.1 %turn.1 = (f32[8,32,192]{2,1,0:T(8,128)S(1)}, f32[8,32,192]{2,1,0:T(8,128)S(1)}, f32[64,128]{1,0:T(8,128)S(1)}, f32[4,32,384]{2,1,0:T(8,128)S(1)}, f32[4,32,384]{2,1,0:T(8,128)S(1)}) custom-call(f32[8,104,128]{2,1,0:T(8,128)S(1)} %all-to-all-done.got_ref, f32[128,128]{1,0:T(8,128)S(1)} %pad.4.table_ref), custom_call_target="tpu_custom_call" | custom-call | tf_op jit(solution)/shard_map/turn/pallas_call | solution.py:498
  18.3 0.2 collective-permute-start
  18.5 5.9 %collective-permute-start.1 = (f32[4,32,384]{2,1,0:T(8,128)S(1)}, f32[4,32,384]{2,1,0:T(8,128)S(1)}, u32[]{:S(2)}, u32[]{:S(2)}) collective-permute-start(f32[4,32,384]{2,1,0:T(8,128)S(1)} %get-tuple-element.27), channel_id=1, source_target_pairs={{1,2},{3,4},{5,6},{2,1},{4,3},{6,5},{9,10},{11,12},{13,14},{10,9},... | collective-permute-start | bytes 589832 | tf_op jit(solution)/shard_map/ppermute | solution.py:523
  24.4 0.0 copy-done.2
  24.4 0.1 copy.9
  24.6 0.2 reshape.19.factor_ref
  24.7 0.2 fusion
  25.0 0.1 convert_element_type.8.mats_ref
  25.0 3.8 %lines.1 = (f32[192,192]{1,0:T(8,128)S(1)}, f32[96,96]{1,0:T(8,128)S(1)}) custom-call(s32[64]{0:T(128)S(1)} %convert_element_type.8.mats_ref, f32[216]{0:T(256)S(1)} %reshape.19.factor_ref), custom_call_target="tpu_custom_call" | custom-call | tf_op jit(solution)/shard_map/lines/pallas_call | solution.py:513
  28.8 0.0 collective-permute-done.y1_ref
  28.9 0.0 collective-permute-done.1.y2_ref
  28.9 0.3 sides.1
  29.2 0.1 collective-permute-start.2
  29.3 3.1 %collective-permute-start.3 = (f32[10,8,384]{2,1,0:T(8,128)S(1)}, f32[10,8,384]{2,1,0:T(8,128)S(1)}, u32[]{:S(2)}, u32[]{:S(2)}) collective-permute-start(f32[10,8,384]{2,1,0:T(8,128)S(1)} %get-tuple-element.32), channel_id=1, source_target_pairs={{32,64},{96,128},{160,192},{224,8},{40,72},{104,136},{168,200},{23... | collective-permute-start | bytes 368648 | tf_op jit(solution)/shard_map/ppermute | solution.py:540
  32.4 1.0 %setup.1 = (bf16[2,192,1024]{2,1,0:T(8,128)(2,1)S(1)}, bf16[2,96,1024]{2,1,0:T(8,128)(2,1)S(1)}) custom-call(f32[192,192]{1,0:T(8,128)S(1)} %get-tuple-element.28.after_ref.line_ref, f32[96,96]{1,0:T(8,128)S(1)} %get-tuple-element.33.cline_ref, f32[64,128]{1,0:T(8,128)S(1)} %get-tuple-element.34.sten_ref, f32[20,8,192]{2,1,0:T(8,128)S(1)} %get-tuple-element.30.after_ref.edge_ref), custom_call_target="tpu_custom_call" | custom-call | tf_op jit(solution)/shard_map/setup/pallas_call | solution.py:542
  33.3 3.0 %middle.1 = (f32[22,32,192]{2,1,0:T(8,128)S(1)}, f32[22,32,192]{2,1,0:T(8,128)S(1)}, f32[22,32,96]{2,1,0:T(8,128)S(1)}, f32[22,32,192]{2,1,0:T(8,128)S(1)}, f32[...) custom-call(f32[20,32,192]{2,1,0:T(8,128)S(1)} %get-tuple-element.29, ...), custom_call_target="tpu_custom_call" | custom-call | tf_op jit(solution)/shard_map/middle/pallas_call | solution.py:551
  36.4 0.0 collective-permute-done.2.x1_ref
  36.4 1.2 %collective-permute-done.3.x2_ref = f32[10,8,384]{2,1,0:T(8,128)S(1)} collective-permute-done((f32[10,8,384]{2,1,0:T(8,128)S(1)}, f32[10,8,384]{2,1,0:T(8,128)S(1)}, u32[]{:S(2)}, u32[]{:S(2)}) %collective-permute-start.3) | collective-permute-done | bytes 122912 | tf_op jit(solution)/shard_map/ppermute | solution.py:540
  37.6 3.2 %strips.1 = f32[8,96,128]{2,1,0:T(8,128)S(1)} custom-call(f32[20,32,192]{2,1,0:T(8,128)S(1)} %get-tuple-element.29.resid_ref, f32[20,8,192]{2,1,0:T(8,128)S(1)} %get-tuple-element.30.after_ref.edge_ref, f32[10,8,384]{2,1,0:T(8,128)S(1)} %collective-permute-done.2.x1_ref, f32[10,8,384]{2,1,0:T(8,128)S(1)} %collective-permute-done.3.x2_ref, ...), custom_call_target="tpu_custom_call" | custom-call | tf_op jit(solution)/shard_map/strips/pallas_call | solution.py:560
  40.8 0.0 copy-start
  40.8 11.8 %all_to_all.10 = f32[8,96,128]{2,1,0:T(8,128)S(1)} all-to-all(f32[8,96,128]{2,1,0:T(8,128)S(1)} %strips.1), channel_id=1, replica_groups=mesh['gz'=8,'gx'=4,'gy'=8] {'gz'}, dimensions={0} | all-to-all | bytes 786432 | tf_op jit(solution)/shard_map/all_to_all | solution.py:573
  52.6 0.0 copy-done
  52.6 1.5 %unpack.1 = (f32[8,3,8,256]{3,2,1,0:T(8,128)}, f32[8,3,8,256]{3,2,1,0:T(8,128)}) custom-call(f32[768,128]{1,0:T(8,128)S(1)} %bitcast.4, f32[8,3,8,256]{3,2,1,0:T(8,128)S(1)} %copy-done), custom_call_target="tpu_custom_call" | custom-call | tf_op jit(solution)/shard_map/unpack/pallas_call | solution.py:574
  (2 shorter events, 0.0 us)
Async XLA Ops:
  3.5 4.3 %copy-start.1 = (f32[8,3,3,3]{0,3,2,1:T(4,128)S(1)}, f32[8,3,3,3]{0,3,2,1:T(4,128)}, u32[]{:S(2)}) copy-start(f32[8,3,3,3]{0,3,2,1:T(4,128)} %param.8) | copy-start | bytes 2596
  3.5 13.6 %all-to-all-start = ((f32[8,104,128]{2,1,0:T(8,128)}), f32[8,104,128]{2,1,0:T(8,128)S(1)}, u32[]{:S(2)}, u32[]{:S(2)}) async-start(f32[8,104,128]{2,1,0:T(8,128)} %bitcast.5), calls=%async_computation | async-start | bytes 851968 | tf_op jit(solution)/shard_map/all_to_all | solution.py:494
  8.0 16.5 %copy-start.2 = (f32[8,3,3,3]{0,3,2,1:T(4,128)S(1)}, f32[8,3,3,3]{0,3,2,1:T(4,128)}, u32[]{:S(2)}) copy-start(f32[8,3,3,3]{0,3,2,1:T(4,128)} %param.9) | copy-start | bytes 2596
  18.3 10.6 %collective-permute-start = (f32[4,32,384]{2,1,0:T(8,128)S(1)}, f32[4,32,384]{2,1,0:T(8,128)S(1)}, u32[]{:S(2)}, u32[]{:S(2)}) collective-permute-start(f32[4,32,384]{2,1,0:T(8,128)S(1)} %get-tuple-element.26), channel_id=1, source_target_pairs={{0,1},{2,3},{4,5},{6,7},{1,0},{3,2},{5,4},{7,6},{8,9},{10,11},{12,... | collective-permute-start | bytes 589832 | tf_op jit(solution)/shard_map/ppermute | solution.py:522
  18.5 10.4 %collective-permute-start.1 = (f32[4,32,384]{2,1,0:T(8,128)S(1)}, f32[4,32,384]{2,1,0:T(8,128)S(1)}, u32[]{:S(2)}, u32[]{:S(2)}) collective-permute-start(f32[4,32,384]{2,1,0:T(8,128)S(1)} %get-tuple-element.27), channel_id=1, source_target_pairs={{1,2},{3,4},{5,6},{2,1},{4,3},{6,5},{9,10},{11,12},{13,14},{10,9},... | collective-permute-start | bytes 589832 | tf_op jit(solution)/shard_map/ppermute | solution.py:523
  29.2 7.2 %collective-permute-start.2 = (f32[10,8,384]{2,1,0:T(8,128)S(1)}, f32[10,8,384]{2,1,0:T(8,128)S(1)}, u32[]{:S(2)}, u32[]{:S(2)}) collective-permute-start(f32[10,8,384]{2,1,0:T(8,128)S(1)} %get-tuple-element.31), channel_id=1, source_target_pairs={{0,32},{64,96},{128,160},{192,224},{8,40},{72,104},{136,168},{200,... | collective-permute-start | bytes 368648 | tf_op jit(solution)/shard_map/ppermute | solution.py:539
  29.3 8.3 %collective-permute-start.3 = (f32[10,8,384]{2,1,0:T(8,128)S(1)}, f32[10,8,384]{2,1,0:T(8,128)S(1)}, u32[]{:S(2)}, u32[]{:S(2)}) collective-permute-start(f32[10,8,384]{2,1,0:T(8,128)S(1)} %get-tuple-element.32), channel_id=1, source_target_pairs={{32,64},{96,128},{160,192},{224,8},{40,72},{104,136},{168,200},{23... | collective-permute-start | bytes 368648 | tf_op jit(solution)/shard_map/ppermute | solution.py:540
  40.8 11.8 %copy-start = (f32[8,3,8,256]{3,2,1,0:T(8,128)S(1)}, f32[8,3,8,256]{3,2,1,0:T(8,128)}, u32[]{:S(2)}) copy-start(f32[8,3,8,256]{3,2,1,0:T(8,128)} %start_ref.1) | copy-start | bytes 589828

commit v8 on v7

--- a/solution.py
+++ b/solution.py
@@ -28,16 +28,34 @@
     return pltpu.CompilerParams(vmem_limit_bytes=mib * 1024 * 1024)
 
 
-def swap_blocks(tile):
+def swap_blocks(tile, form=0):
     sub = lax.broadcasted_iota(jnp.int32, tile.shape, 1)
     blk = lax.broadcasted_iota(jnp.int32, tile.shape, 2) // 32
     for bit in (1, 2, 4):
-        up = pltpu.roll(pltpu.roll(tile, 8 - bit, axis=1), 32 * bit, axis=2)
-        down = pltpu.roll(pltpu.roll(tile, bit, axis=1), 256 - 32 * bit, axis=2)
         in_sub = (sub & bit) != 0
         in_blk = (blk & bit) != 0
-        tile = jnp.where(in_sub == in_blk, tile, jnp.where(in_blk, up, down))
+        sub_up, sub_down = pltpu.roll(tile, 8 - bit, axis=1), pltpu.roll(tile, bit, axis=1)
+        if form == 0:
+            up = pltpu.roll(sub_up, 32 * bit, axis=2)
+            down = pltpu.roll(sub_down, 256 - 32 * bit, axis=2)
+            tile = jnp.where(in_sub == in_blk, tile, jnp.where(in_blk, up, down))
+        else:
+            by_sub = jnp.where(in_sub, sub_down, sub_up)
+            blk_up = pltpu.roll(tile, 256 - 32 * bit, axis=2)
+            blk_down = pltpu.roll(tile, 32 * bit, axis=2)
+            by_blk = jnp.where(in_blk, blk_down, blk_up)
+            same = in_sub == in_blk
+            tile = jnp.where(same, by_blk, by_sub) if form == 1 else jnp.where(same, by_sub, by_blk)
     return tile
+
+
+def odd_block():
+    return lax.axis_index("gx") % 2 == 1
+
+
+def x_slice():
+    gz = lax.axis_index("gz")
+    return jnp.where(odd_block(), lax.axis_size("gz") - 1 - gz, gz)
 
 
 def fetches(pairs, sems):
@@ -56,11 +74,16 @@
     )
     for i, (f, c) in enumerate(order):
         copies[i].wait()
-        tile = swap_blocks(in_ref[i])
-        for z in range(8):
-            for h in range(2):
-                at = h * 48 + f * 24 + c * 8 + z
-                out_ref[pl.ds(at, 8, stride=ROWS), :] = tile[z, :, h * 128 : h * 128 + 128]
+        for form in (0, 1):
+
+            @pl.when(odd_block() == (form == 1))
+            def _():
+                tile = swap_blocks(in_ref[i], form)
+                for z in range(8):
+                    for h in range(2):
+                        at = h * 48 + f * 24 + c * 8 + z
+                        out_ref[pl.ds(at, 8, stride=ROWS), :] = tile[z, :, h * 128 : h * 128 + 128]
+
     mats_copy.wait()
     row = lax.broadcasted_iota(jnp.int32, (8, 128), 0)
     ids = jnp.zeros((8, 128), jnp.int32)
@@ -71,22 +94,33 @@
 
 
 def unpack_kernel(got_ref, start_ref, field_hbm, resid_hbm, out_ref, sems):
-    copies = []
-    for f, ref in enumerate((field_hbm, resid_hbm)):
-        for c in range(3):
+    order = [(f, c) for f in range(2) for c in range(3)]
+    copies = [
+        pltpu.make_async_copy(
+            out_ref.at[i], (field_hbm, resid_hbm)[f].at[:, c], sems.at[i]
+        )
+        for i, (f, c) in enumerate(order)
+    ]
+
+    def fill(form):
+        for i, (f, c) in enumerate(order):
             halves = []
             for h in range(2):
                 at = h * 48 + f * 24 + c * 8
                 rows = [got_ref[pl.ds(at + z, 8, stride=96), :] for z in range(8)]
                 halves.append(jnp.stack(rows, axis=0))
-            tile = swap_blocks(jnp.concatenate(halves, axis=2))
+            tile = swap_blocks(jnp.concatenate(halves, axis=2), form)
             if f == 0:
                 tile = tile + start_ref[:, c]
-            i = f * 3 + c
             out_ref[i] = tile
-            copy = pltpu.make_async_copy(out_ref.at[i], ref.at[:, c], sems.at[i])
-            copy.start()
-            copies.append(copy)
+            copies[i].start()
+
+    for form in (0, 2):
+
+        @pl.when(odd_block() == (form == 2))
+        def _():
+            fill(form)
+
     for copy in copies:
         copy.wait()
 
@@ -157,7 +191,7 @@
 def sides_kernel(
     own_ref, q_ref, y1_ref, y2_ref, after_ref, resid_ref, edge_ref, send1_ref, send2_ref, wide_ref
 ):
-    even_x = lax.axis_index("gz") % 2 == 0
+    even_x = x_slice() % 2 == 0
     even_y = lax.axis_index("gy") % 2 == 0
     first, second = y1_ref[...], y2_ref[...]
     sub = lax.broadcasted_iota(jnp.int32, (RW, XH, 192), 1)
@@ -410,9 +444,9 @@
     saved, change_ref, mid_ref, out_ref = refs[:7], refs[7], refs[8], refs[9]
     side_ref, cside_ref, scratch = refs[10], refs[11], refs[12:]
     r_ref = scratch[0]
-    gz, gx = lax.axis_index("gz"), lax.axis_index("gx")
-    at_left = unless((gx == 0) & (gz == 0))
-    at_right = unless((gx == lax.axis_size("gx") - 1) & (gz == lax.axis_size("gz") - 1))
+    place, gx = x_slice(), lax.axis_index("gx")
+    at_left = unless((gx == 0) & (place == 0))
+    at_right = unless((gx == lax.axis_size("gx") - 1) & (place == lax.axis_size("gz") - 1))
     sides = [cside_ref if i in (2, 4, 5) else side_ref for i in range(7)]
 
     def inside(value, y):
@@ -428,7 +462,7 @@
         row = pltpu.roll(row, 1, axis=0) + pltpu.roll(row, XW - 1, axis=0)
         return (side[y - 1] + side[y + 1]) + jnp.concatenate([row[0:16], row[XT:]], axis=0)
 
-    even_x = gz % 2 == 0
+    even_x = place % 2 == 0
     sub = lax.broadcasted_iota(jnp.int32, (RW // 2, XH, 192), 1)
     left = unfolded(jnp.where(even_x, x2_ref[...], x1_ref[...]))
     right = unfolded(jnp.where(even_x, x1_ref[...], x2_ref[...]))
@@ -535,7 +569,11 @@
         compiler_params=params(),
         name="sides",
     )(own, q, y1, y2, line)
-    along = [(i % count_z) * count_x + i // count_z for i in range(count_x * count_z)]
+    along = [
+        (count_z - 1 - i if x % 2 else i) * count_x + x
+        for x in range(count_x)
+        for i in range(count_z)
+    ]
     x1 = lax.ppermute(send1, ("gz", "gx"), swaps(along, 0))
     x2 = lax.ppermute(send2, ("gz", "gx"), swaps(along, 1))
 

time: 54.5 us -> 53.2 us (0.976)
  waiting for transfers between devices: 10.4 us -> 9.2 us
    ppermute x1, waiting for transfers between devices: 1.2 us -> 0.01 us  [on_device(): x2 = lax.ppermute(send2, ('gz', 'gx'), swaps(along, 1))]
  transfers between devices with their start and end apart: 5 -> 5, of which waited for: 2 -> 1; matrix products, arithmetic and copies ran while one was open for 1% -> 1% of each run, Pallas kernels for 14% -> 15%
where the time goes in v8:
time: 53.2 us; the launch traced here: 52.9 us
  Pallas kernels  16.6 us (31%)
  starting transfers between devices  14.1 us (27%)
  blocking collectives  11.5 us (22%)
  waiting for transfers between devices  9.2 us (17%)
  between operations  0.77 us (1%)
    all_to_all x1, blocking collectives, on_device(): back = lax.all_to_all(out, 'gz', 0, 0, tiled=True)  11.5 us
    all_to_all x1, waiting for transfers between devices, on_device(): got = lax.all_to_all(packed.reshape(8, ROWS, 128), 'gz', 0, 0, tiled=True)  9.19 us
    ppermute x1, starting transfers between devices, on_device(): y2 = lax.ppermute(send2, 'gy', swaps(range(count_y), 1))  5.93 us
    all_to_all x1, starting transfers between devices, on_device(): got = lax.all_to_all(packed.reshape(8, ROWS, 128), 'gz', 0, 0, tiled=True)  4.31 us
    pallas_call x1, Pallas kernels, on_device(): pl.pallas_call(lines_kernel, out_shape=(shape(192, 192), shape(96, 96)),...  3.82 us
    ppermute x1, starting transfers between devices, on_device(): x2 = lax.ppermute(send2, ('gz', 'gx'), swaps(along, 1))  3.58 us
    pallas_call x1, Pallas kernels, on_device(): pl.pallas_call(strips_kernel, out_shape=shape(8, 96, 128), in_specs=[VMEM...  3.17 us
    pallas_call x1, Pallas kernels, on_device(): pl.pallas_call(middle_kernel, out_shape=(*sides, shape(YT, 16, 192), shap...  3.05 us
  transfers between devices with their start and end apart: 5, of which 1 were waited for; matrix products, arithmetic and copies ran while one was open for 1% of the time, Pallas kernels for 15%

profile of v8, /device:TPU:104, one launch (start us, length us, event | category | flops | bytes accessed | tf_op | source)
XLA Modules:
  0.0 52.9 jit_solution(11028023721062325607)
XLA Ops:
  0.6 2.8 %pack.1 = f32[832,128]{1,0:T(8,128)} custom-call(f32[8,3,8,256]{3,2,1,0:T(8,128)} %load_hbm.1, f32[8,3,8,256]{3,2,1,0:T(8,128)} %start_ref.1, s32[8]{0:T(128)} %mats_hbm.1), custom_call_target="tpu_custom_call" | custom-call | tf_op jit(solution)/shard_map/pack/pallas_call | solution.py:514
  3.4 0.0 copy-start.1
  3.5 4.3 %all-to-all-start = ((f32[8,104,128]{2,1,0:T(8,128)}), f32[8,104,128]{2,1,0:T(8,128)S(1)}, u32[]{:S(2)}, u32[]{:S(2)}) async-start(f32[8,104,128]{2,1,0:T(8,128)} %bitcast.5), calls=%async_computation | async-start | bytes 851968 | tf_op jit(solution)/shard_map/all_to_all | solution.py:528
  7.8 0.0 copy-done.1
  7.8 0.1 copy.8
  7.9 0.0 copy-start.2
  7.9 9.2 %all-to-all-done.got_ref = f32[8,104,128]{2,1,0:T(8,128)S(1)} async-done(((f32[8,104,128]{2,1,0:T(8,128)}), f32[8,104,128]{2,1,0:T(8,128)S(1)}, u32[]{:S(2)}, u32[]{:S(2)}) %all-to-all-start) | async-done | bytes 426016 | tf_op jit(solution)/shard_map/all_to_all | solution.py:528
  17.1 1.1 %turn.1 = (f32[8,32,192]{2,1,0:T(8,128)S(1)}, f32[8,32,192]{2,1,0:T(8,128)S(1)}, f32[64,128]{1,0:T(8,128)S(1)}, f32[4,32,384]{2,1,0:T(8,128)S(1)}, f32[4,32,384]{2,1,0:T(8,128)S(1)}) custom-call(f32[8,104,128]{2,1,0:T(8,128)S(1)} %all-to-all-done.got_ref, f32[128,128]{1,0:T(8,128)S(1)} %pad.4.table_ref), custom_call_target="tpu_custom_call" | custom-call | tf_op jit(solution)/shard_map/turn/pallas_call | solution.py:532
  18.2 0.2 collective-permute-start
  18.4 5.9 %collective-permute-start.1 = (f32[4,32,384]{2,1,0:T(8,128)S(1)}, f32[4,32,384]{2,1,0:T(8,128)S(1)}, u32[]{:S(2)}, u32[]{:S(2)}) collective-permute-start(f32[4,32,384]{2,1,0:T(8,128)S(1)} %get-tuple-element.27), channel_id=1, source_target_pairs={{1,2},{3,4},{5,6},{2,1},{4,3},{6,5},{9,10},{11,12},{13,14},{10,9},... | collective-permute-start | bytes 589832 | tf_op jit(solution)/shard_map/ppermute | solution.py:557
  24.3 0.0 copy-done.2
  24.3 0.1 copy.9
  24.5 0.2 reshape.19.factor_ref
  24.6 0.2 fusion
  24.9 0.1 convert_element_type.8.mats_ref
  24.9 3.8 %lines.1 = (f32[192,192]{1,0:T(8,128)S(1)}, f32[96,96]{1,0:T(8,128)S(1)}) custom-call(s32[64]{0:T(128)S(1)} %convert_element_type.8.mats_ref, f32[216]{0:T(256)S(1)} %reshape.19.factor_ref), custom_call_target="tpu_custom_call" | custom-call | tf_op jit(solution)/shard_map/lines/pallas_call | solution.py:547
  28.8 0.0 collective-permute-done.y1_ref
  28.8 0.0 collective-permute-done.1.y2_ref
  28.8 0.3 sides.1
  29.1 0.1 collective-permute-start.2
  29.2 3.6 %collective-permute-start.3 = (f32[10,8,384]{2,1,0:T(8,128)S(1)}, f32[10,8,384]{2,1,0:T(8,128)S(1)}, u32[]{:S(2)}, u32[]{:S(2)}) collective-permute-start(f32[10,8,384]{2,1,0:T(8,128)S(1)} %get-tuple-element.32), channel_id=1, source_target_pairs={{32,64},{96,128},{160,192},{224,232},{200,168},{136,104},{72,40},{... | collective-permute-start | bytes 368648 | tf_op jit(solution)/shard_map/ppermute | solution.py:578
  32.8 1.0 %setup.1 = (bf16[2,192,1024]{2,1,0:T(8,128)(2,1)S(1)}, bf16[2,96,1024]{2,1,0:T(8,128)(2,1)S(1)}) custom-call(f32[192,192]{1,0:T(8,128)S(1)} %get-tuple-element.28.after_ref.line_ref, f32[96,96]{1,0:T(8,128)S(1)} %get-tuple-element.33.cline_ref, f32[64,128]{1,0:T(8,128)S(1)} %get-tuple-element.34.sten_ref, f32[20,8,192]{2,1,0:T(8,128)S(1)} %get-tuple-element.30.after_ref.edge_ref), custom_call_target="tpu_custom_call" | custom-call | tf_op jit(solution)/shard_map/setup/pallas_call | solution.py:580
  33.8 3.0 %middle.1 = (f32[22,32,192]{2,1,0:T(8,128)S(1)}, f32[22,32,192]{2,1,0:T(8,128)S(1)}, f32[22,32,96]{2,1,0:T(8,128)S(1)}, f32[22,32,192]{2,1,0:T(8,128)S(1)}, f32[...) custom-call(f32[20,32,192]{2,1,0:T(8,128)S(1)} %get-tuple-element.29, ...), custom_call_target="tpu_custom_call" | custom-call | tf_op jit(solution)/shard_map/middle/pallas_call | solution.py:589
  36.8 0.0 collective-permute-done.2.x1_ref
  36.8 0.0 collective-permute-done.3.x2_ref
  36.9 3.2 %strips.1 = f32[8,96,128]{2,1,0:T(8,128)S(1)} custom-call(f32[20,32,192]{2,1,0:T(8,128)S(1)} %get-tuple-element.29.resid_ref, f32[20,8,192]{2,1,0:T(8,128)S(1)} %get-tuple-element.30.after_ref.edge_ref, f32[10,8,384]{2,1,0:T(8,128)S(1)} %collective-permute-done.2.x1_ref, f32[10,8,384]{2,1,0:T(8,128)S(1)} %collective-permute-done.3.x2_ref, ...), custom_call_target="tpu_custom_call" | custom-call | tf_op jit(solution)/shard_map/strips/pallas_call | solution.py:598
  40.0 0.0 copy-start
  40.0 11.5 %all_to_all.10 = f32[8,96,128]{2,1,0:T(8,128)S(1)} all-to-all(f32[8,96,128]{2,1,0:T(8,128)S(1)} %strips.1), channel_id=1, replica_groups=mesh['gz'=8,'gx'=4,'gy'=8] {'gz'}, dimensions={0} | all-to-all | bytes 786432 | tf_op jit(solution)/shard_map/all_to_all | solution.py:611
  51.5 0.0 copy-done
  51.5 1.4 %unpack.1 = (f32[8,3,8,256]{3,2,1,0:T(8,128)}, f32[8,3,8,256]{3,2,1,0:T(8,128)}) custom-call(f32[768,128]{1,0:T(8,128)S(1)} %bitcast.4, f32[8,3,8,256]{3,2,1,0:T(8,128)S(1)} %copy-done), custom_call_target="tpu_custom_call" | custom-call | tf_op jit(solution)/shard_map/unpack/pallas_call | solution.py:612
  (2 shorter events, 0.0 us)
Async XLA Ops:
  3.4 4.3 %copy-start.1 = (f32[8,3,3,3]{0,3,2,1:T(4,128)S(1)}, f32[8,3,3,3]{0,3,2,1:T(4,128)}, u32[]{:S(2)}) copy-start(f32[8,3,3,3]{0,3,2,1:T(4,128)} %param.8) | copy-start | bytes 2596
  3.5 13.6 %all-to-all-start = ((f32[8,104,128]{2,1,0:T(8,128)}), f32[8,104,128]{2,1,0:T(8,128)S(1)}, u32[]{:S(2)}, u32[]{:S(2)}) async-start(f32[8,104,128]{2,1,0:T(8,128)} %bitcast.5), calls=%async_computation | async-start | bytes 851968 | tf_op jit(solution)/shard_map/all_to_all | solution.py:528
  7.9 16.5 %copy-start.2 = (f32[8,3,3,3]{0,3,2,1:T(4,128)S(1)}, f32[8,3,3,3]{0,3,2,1:T(4,128)}, u32[]{:S(2)}) copy-start(f32[8,3,3,3]{0,3,2,1:T(4,128)} %param.9) | copy-start | bytes 2596
  18.2 10.6 %collective-permute-start = (f32[4,32,384]{2,1,0:T(8,128)S(1)}, f32[4,32,384]{2,1,0:T(8,128)S(1)}, u32[]{:S(2)}, u32[]{:S(2)}) collective-permute-start(f32[4,32,384]{2,1,0:T(8,128)S(1)} %get-tuple-element.26), channel_id=1, source_target_pairs={{0,1},{2,3},{4,5},{6,7},{1,0},{3,2},{5,4},{7,6},{8,9},{10,11},{12,... | collective-permute-start | bytes 589832 | tf_op jit(solution)/shard_map/ppermute | solution.py:556
  18.4 10.4 %collective-permute-start.1 = (f32[4,32,384]{2,1,0:T(8,128)S(1)}, f32[4,32,384]{2,1,0:T(8,128)S(1)}, u32[]{:S(2)}, u32[]{:S(2)}) collective-permute-start(f32[4,32,384]{2,1,0:T(8,128)S(1)} %get-tuple-element.27), channel_id=1, source_target_pairs={{1,2},{3,4},{5,6},{2,1},{4,3},{6,5},{9,10},{11,12},{13,14},{10,9},... | collective-permute-start | bytes 589832 | tf_op jit(solution)/shard_map/ppermute | solution.py:557
  29.1 7.7 %collective-permute-start.2 = (f32[10,8,384]{2,1,0:T(8,128)S(1)}, f32[10,8,384]{2,1,0:T(8,128)S(1)}, u32[]{:S(2)}, u32[]{:S(2)}) collective-permute-start(f32[10,8,384]{2,1,0:T(8,128)S(1)} %get-tuple-element.31), channel_id=1, source_target_pairs={{0,32},{64,96},{128,160},{192,224},{232,200},{168,136},{104,72},{4... | collective-permute-start | bytes 368648 | tf_op jit(solution)/shard_map/ppermute | solution.py:577
  29.2 7.7 %collective-permute-start.3 = (f32[10,8,384]{2,1,0:T(8,128)S(1)}, f32[10,8,384]{2,1,0:T(8,128)S(1)}, u32[]{:S(2)}, u32[]{:S(2)}) collective-permute-start(f32[10,8,384]{2,1,0:T(8,128)S(1)} %get-tuple-element.32), channel_id=1, source_target_pairs={{32,64},{96,128},{160,192},{224,232},{200,168},{136,104},{72,40},{... | collective-permute-start | bytes 368648 | tf_op jit(solution)/shard_map/ppermute | solution.py:578
  40.0 11.5 %copy-start = (f32[8,3,8,256]{3,2,1,0:T(8,128)S(1)}, f32[8,3,8,256]{3,2,1,0:T(8,128)}, u32[]{:S(2)}) copy-start(f32[8,3,8,256]{3,2,1,0:T(8,128)} %start_ref.1) | copy-start | bytes 589828

commit v9 on v8

--- a/solution.py
+++ b/solution.py
@@ -225,37 +225,32 @@
     return high, (value - high.astype(F32)).astype(BF16)
 
 
-def line_rows(mats_ref, factor_ref, dst_ref, layers, step):
+def up_row(mats_ref, factor_ref, dst_ref, layers, step, z, state):
     lane = lax.broadcasted_iota(jnp.int32, (1, 3 * layers), 1)
-
-    def up(z, state):
-        base = mats_ref[z * step] * 27
-        new = []
-        for i in range(3):
-            row = jnp.zeros((1, 3 * layers), F32)
-            for j in range(3):
-                row = jnp.where(lane == j * layers + z, factor_ref[base + i * 3 + j], row)
-            for j in range(3):
-                row = row + factor_ref[base + 9 + i * 3 + j] * state[j]
-            dst_ref[pl.ds(i * layers + z, 1), :] = row
-            new.append(row)
-        return tuple(new)
-
-    def down(t, state):
-        z = layers - 1 - t
-        base = mats_ref[z * step] * 27
-        new = []
-        for i in range(3):
-            row = dst_ref[pl.ds(i * layers + z, 1), :]
-            for j in range(3):
-                row = row + factor_ref[base + 18 + i * 3 + j] * state[j]
-            dst_ref[pl.ds(i * layers + z, 1), :] = row
-            new.append(row)
-        return tuple(new)
-
-    zero = tuple(jnp.zeros((1, 3 * layers), F32) for _ in range(3))
-    lax.fori_loop(0, layers, up, zero, unroll=8)
-    lax.fori_loop(0, layers, down, zero, unroll=8)
+    base = mats_ref[z * step] * 27
+    new = []
+    for i in range(3):
+        row = jnp.zeros((1, 3 * layers), F32)
+        for j in range(3):
+            row = jnp.where(lane == j * layers + z, factor_ref[base + i * 3 + j], row)
+        for j in range(3):
+            row = row + factor_ref[base + 9 + i * 3 + j] * state[j]
+        dst_ref[pl.ds(i * layers + z, 1), :] = row
+        new.append(row)
+    return new
+
+
+def down_row(mats_ref, factor_ref, dst_ref, layers, step, z, state):
+    lane = lax.broadcasted_iota(jnp.int32, (1, 3 * layers), 1)
+    base = mats_ref[z * step] * 27
+    new = []
+    for i in range(3):
+        row = jnp.where(lane == i * layers + z, 1.0, 0.0)
+        for j in range(3):
+            row = row + factor_ref[base + 18 + i * 3 + j] * state[j]
+        dst_ref[pl.ds(i * layers + z, 1), :] = row
+        new.append(row)
+    return new
 
 
 def couple(sten, which, blocks):
@@ -285,13 +280,27 @@
     ref[1, :, at : at + value.shape[1]] = low
 
 
-def lines_kernel(mats_ref, factor_ref, line_ref, cline_ref):
-    line_rows(mats_ref, factor_ref, line_ref, NZ, 1)
-    line_rows(mats_ref, factor_ref, cline_ref, NC, 2)
-
-
-def setup_kernel(line_ref, cline_ref, sten_ref, after_ref, fine_ref, coarse_ref):
+def lines_kernel(mats_ref, factor_ref, up_ref, down_ref, cup_ref, cdown_ref):
+    def step(t, state):
+        up, down, cup, cdown = (state[i * 3 : i * 3 + 3] for i in range(4))
+        for half in range(2):
+            z = 2 * t + half
+            up = up_row(mats_ref, factor_ref, up_ref, NZ, 1, z, up)
+            down = down_row(mats_ref, factor_ref, down_ref, NZ, 1, NZ - 1 - z, down)
+        cup = up_row(mats_ref, factor_ref, cup_ref, NC, 2, t, cup)
+        cdown = down_row(mats_ref, factor_ref, cdown_ref, NC, 2, NC - 1 - t, cdown)
+        return (*up, *down, *cup, *cdown)
+
+    fine, coarse = (jnp.zeros((1, 3 * n), F32) for n in (NZ, NC))
+    lax.fori_loop(0, NC, step, (fine,) * 6 + (coarse,) * 6, unroll=4)
+
+
+def setup_kernel(
+    up_ref, down_ref, cup_ref, cdown_ref, sten_ref, fine_ref, coarse_ref, line_ref, cline_ref
+):
     sten = sten_ref[...]
+    line_ref[...] = exact(down_ref[...], up_ref[...])
+    cline_ref[...] = exact(cdown_ref[...], cup_ref[...])
 
     def level(sten_part, scale, ref, layers):
         blocks = [ref[i * layers : (i + 1) * layers, :] for i in range(3)]
@@ -544,14 +553,23 @@
         compiler_params=params(),
         name="turn",
     )(got, table)
-    line, cline = pl.pallas_call(
+    lines = pl.pallas_call(
         lines_kernel,
-        out_shape=(shape(192, 192), shape(96, 96)),
+        out_shape=(shape(192, 192), shape(192, 192), shape(96, 96), shape(96, 96)),
         in_specs=[SMEM, SMEM],
-        out_specs=(VMEM, VMEM),
+        out_specs=(VMEM,) * 4,
         compiler_params=params(),
         name="lines",
     )(mats, line_factors.reshape(-1))
+    fine, coarse = pl.pallas_call(
+        setup_kernel,
+        out_shape=(shape(2, 192, 1024, dtype=BF16), shape(2, 96, 1024, dtype=BF16)),
+        in_specs=[VMEM] * 5,
+        out_specs=(VMEM, VMEM),
+        scratch_shapes=[pltpu.VMEM((192, 192), F32), pltpu.VMEM((96, 96), F32)],
+        compiler_params=params(),
+        name="setup",
+    )(*lines, sten)
     count_x, count_y, count_z = (lax.axis_size(axis) for axis in ("gx", "gy", "gz"))
     y1 = lax.ppermute(send1, "gy", swaps(range(count_y), 0))
     y2 = lax.ppermute(send2, "gy", swaps(range(count_y), 1))
@@ -568,7 +586,7 @@
         scratch_shapes=[pltpu.VMEM((RW, XH, 384), F32)],
         compiler_params=params(),
         name="sides",
-    )(own, q, y1, y2, line)
+    )(own, q, y1, y2, fine)
     along = [
         (count_z - 1 - i if x % 2 else i) * count_x + x
         for x in range(count_x)
@@ -577,14 +595,6 @@
     x1 = lax.ppermute(send1, ("gz", "gx"), swaps(along, 0))
     x2 = lax.ppermute(send2, ("gz", "gx"), swaps(along, 1))
 
-    fine, coarse = pl.pallas_call(
-        setup_kernel,
-        out_shape=(shape(2, 192, 1024, dtype=BF16), shape(2, 96, 1024, dtype=BF16)),
-        in_specs=[VMEM, VMEM, VMEM, pl.BlockSpec(memory_space=pl.ANY)],
-        out_specs=(VMEM, VMEM),
-        compiler_params=params(),
-        name="setup",
-    )(line, cline, sten, edge)
     sides = tuple(shape(YW, XT, 96 if i in (2, 4, 5) else 192) for i in range(7))
     middle = pl.pallas_call(
         middle_kernel,

time: 53.2 us -> 53 us (level)
  Pallas kernels: 16.6 us -> 16 us
    pallas_call x1, Pallas kernels: 3.82 us -> 2.91 us  [on_device(): pl.pallas_call(lines_kernel, out_shape=(shape(192, 192), shape(192, 192),...]
  transfers between devices with their start and end apart: 5 -> 5, of which waited for: 1 -> 2; matrix products, arithmetic and copies ran while one was open for 1% -> 1% of each run, Pallas kernels for 15% -> 14%
where the time goes in v9:
time: 53 us; the launch traced here: 52.4 us
  Pallas kernels  16 us (30%)
  starting transfers between devices  14.1 us (27%)
  blocking collectives  11.5 us (22%)
  waiting for transfers between devices  9.32 us (18%)
  between operations  0.77 us (1%)
    all_to_all x1, blocking collectives, on_device(): back = lax.all_to_all(out, 'gz', 0, 0, tiled=True)  11.5 us
    all_to_all x1, waiting for transfers between devices, on_device(): got = lax.all_to_all(packed.reshape(8, ROWS, 128), 'gz', 0, 0, tiled=True)  9.19 us
    ppermute x1, starting transfers between devices, on_device(): y2 = lax.ppermute(send2, 'gy', swaps(range(count_y), 1))  5.93 us
    all_to_all x1, starting transfers between devices, on_device(): got = lax.all_to_all(packed.reshape(8, ROWS, 128), 'gz', 0, 0, tiled=True)  4.31 us
    ppermute x1, starting transfers between devices, on_device(): x2 = lax.ppermute(send2, ('gz', 'gx'), swaps(along, 1))  3.58 us
    pallas_call x1, Pallas kernels, on_device(): pl.pallas_call(strips_kernel, out_shape=shape(8, 96, 128), in_specs=[VMEM...  3.17 us
    pallas_call x1, Pallas kernels, on_device(): pl.pallas_call(middle_kernel, out_shape=(*sides, shape(YT, 16, 192), shap...  3.04 us
    pallas_call x1, Pallas kernels, on_device(): pl.pallas_call(lines_kernel, out_shape=(shape(192, 192), shape(192, 192),...  2.91 us
  transfers between devices with their start and end apart: 5, of which 2 were waited for; matrix products, arithmetic and copies ran while one was open for 1% of the time, Pallas kernels for 14%

profile of v9, /device:TPU:104, one launch (start us, length us, event | category | flops | bytes accessed | tf_op | source)
XLA Modules:
  0.0 52.4 jit_solution(16448248149238870312)
XLA Ops:
  0.6 2.8 %pack.1 = f32[832,128]{1,0:T(8,128)} custom-call(f32[8,3,8,256]{3,2,1,0:T(8,128)} %load_hbm.1, f32[8,3,8,256]{3,2,1,0:T(8,128)} %start_ref.1, s32[8]{0:T(128)} %mats_hbm.1), custom_call_target="tpu_custom_call" | custom-call | tf_op jit(solution)/shard_map/pack/pallas_call | solution.py:523
  3.4 0.0 copy-start.1
  3.5 4.3 %all-to-all-start = ((f32[8,104,128]{2,1,0:T(8,128)}), f32[8,104,128]{2,1,0:T(8,128)S(1)}, u32[]{:S(2)}, u32[]{:S(2)}) async-start(f32[8,104,128]{2,1,0:T(8,128)} %bitcast.5), calls=%async_computation | async-start | bytes 851968 | tf_op jit(solution)/shard_map/all_to_all | solution.py:537
  7.8 0.0 copy-done.1
  7.8 0.1 copy.8
  7.9 0.0 copy-start.2
  7.9 9.2 %all-to-all-done.got_ref = f32[8,104,128]{2,1,0:T(8,128)S(1)} async-done(((f32[8,104,128]{2,1,0:T(8,128)}), f32[8,104,128]{2,1,0:T(8,128)S(1)}, u32[]{:S(2)}, u32[]{:S(2)}) %all-to-all-start) | async-done | bytes 426016 | tf_op jit(solution)/shard_map/all_to_all | solution.py:537
  17.1 1.1 %turn.1 = (f32[8,32,192]{2,1,0:T(8,128)S(1)}, f32[8,32,192]{2,1,0:T(8,128)S(1)}, f32[64,128]{1,0:T(8,128)S(1)}, f32[4,32,384]{2,1,0:T(8,128)S(1)}, f32[4,32,384]{2,1,0:T(8,128)S(1)}) custom-call(f32[8,104,128]{2,1,0:T(8,128)S(1)} %all-to-all-done.got_ref, f32[128,128]{1,0:T(8,128)S(1)} %pad.4.table_ref), custom_call_target="tpu_custom_call" | custom-call | tf_op jit(solution)/shard_map/turn/pallas_call | solution.py:541
  18.2 0.2 collective-permute-start
  18.4 5.9 %collective-permute-start.1 = (f32[4,32,384]{2,1,0:T(8,128)S(1)}, f32[4,32,384]{2,1,0:T(8,128)S(1)}, u32[]{:S(2)}, u32[]{:S(2)}) collective-permute-start(f32[4,32,384]{2,1,0:T(8,128)S(1)} %get-tuple-element.29), channel_id=1, source_target_pairs={{1,2},{3,4},{5,6},{2,1},{4,3},{6,5},{9,10},{11,12},{13,14},{10,9},... | collective-permute-start | bytes 589832 | tf_op jit(solution)/shard_map/ppermute | solution.py:575
  24.3 0.0 copy-done.2
  24.3 0.1 copy.9
  24.5 0.2 reshape.19.factor_ref
  24.6 0.2 fusion
  24.9 0.1 convert_element_type.8.mats_ref
  24.9 2.9 %lines.1 = (f32[192,192]{1,0:T(8,128)S(1)}, f32[192,192]{1,0:T(8,128)S(1)}, f32[96,96]{1,0:T(8,128)S(1)}, f32[96,96]{1,0:T(8,128)S(1)}) custom-call(s32[64]{0:T(128)S(1)} %convert_element_type.8.mats_ref, f32[216]{0:T(256)S(1)} %reshape.19.factor_ref), custom_call_target="tpu_custom_call" | custom-call | tf_op jit(solution)/shard_map/lines/pallas_call | solution.py:556
  27.8 1.3 %setup.1 = (bf16[2,192,1024]{2,1,0:T(8,128)(2,1)S(1)}, bf16[2,96,1024]{2,1,0:T(8,128)(2,1)S(1)}) custom-call(f32[192,192]{1,0:T(8,128)S(1)} %get-tuple-element.30.up_ref, f32[192,192]{1,0:T(8,128)S(1)} %get-tuple-element.31.down_ref, f32[96,96]{1,0:T(8,128)S(1)} %get-tuple-element.32.cup_ref, f32[96,96]{1,0:T(8,128)S(1)} %get-tuple-element.33.cdown_ref, ...), custom_call_target="tpu_custom_call" | custom-call | tf_op jit(solution)/shard_map/setup/pallas_call | solution.py:564
  29.1 0.0 collective-permute-done.y1_ref
  29.1 0.0 collective-permute-done.1.y2_ref
  29.1 0.3 sides.1
  29.5 0.1 collective-permute-start.2
  29.6 3.6 %collective-permute-start.3 = (f32[10,8,384]{2,1,0:T(8,128)S(1)}, f32[10,8,384]{2,1,0:T(8,128)S(1)}, u32[]{:S(2)}, u32[]{:S(2)}) collective-permute-start(f32[10,8,384]{2,1,0:T(8,128)S(1)} %get-tuple-element.39), channel_id=1, source_target_pairs={{32,64},{96,128},{160,192},{224,232},{200,168},{136,104},{72,40},{... | collective-permute-start | bytes 368648 | tf_op jit(solution)/shard_map/ppermute | solution.py:596
  33.2 3.0 %middle.1 = (f32[22,32,192]{2,1,0:T(8,128)S(1)}, f32[22,32,192]{2,1,0:T(8,128)S(1)}, f32[22,32,96]{2,1,0:T(8,128)S(1)}, f32[22,32,192]{2,1,0:T(8,128)S(1)}, f32[...) custom-call(f32[20,32,192]{2,1,0:T(8,128)S(1)} %get-tuple-element.36, ...), custom_call_target="tpu_custom_call" | custom-call | tf_op jit(solution)/shard_map/middle/pallas_call | solution.py:599
  36.2 0.0 collective-permute-done.2.x1_ref
  36.2 0.1 collective-permute-done.3.x2_ref
  36.3 3.2 %strips.1 = f32[8,96,128]{2,1,0:T(8,128)S(1)} custom-call(f32[20,32,192]{2,1,0:T(8,128)S(1)} %get-tuple-element.36.resid_ref, f32[20,8,192]{2,1,0:T(8,128)S(1)} %get-tuple-element.37.edge_ref, f32[10,8,384]{2,1,0:T(8,128)S(1)} %collective-permute-done.2.x1_ref, f32[10,8,384]{2,1,0:T(8,128)S(1)} %collective-permute-done.3.x2_ref, ...), custom_call_target="tpu_custom_call" | custom-call | tf_op jit(solution)/shard_map/strips/pallas_call | solution.py:608
  39.5 0.0 copy-start
  39.5 11.5 %all_to_all.10 = f32[8,96,128]{2,1,0:T(8,128)S(1)} all-to-all(f32[8,96,128]{2,1,0:T(8,128)S(1)} %strips.1), channel_id=1, replica_groups=mesh['gz'=8,'gx'=4,'gy'=8] {'gz'}, dimensions={0} | all-to-all | bytes 786432 | tf_op jit(solution)/shard_map/all_to_all | solution.py:621
  51.0 0.0 copy-done
  51.0 1.4 %unpack.1 = (f32[8,3,8,256]{3,2,1,0:T(8,128)}, f32[8,3,8,256]{3,2,1,0:T(8,128)}) custom-call(f32[768,128]{1,0:T(8,128)S(1)} %bitcast.4, f32[8,3,8,256]{3,2,1,0:T(8,128)S(1)} %copy-done), custom_call_target="tpu_custom_call" | custom-call | tf_op jit(solution)/shard_map/unpack/pallas_call | solution.py:622
  (2 shorter events, 0.0 us)
Async XLA Ops:
  3.4 4.3 %copy-start.1 = (f32[8,3,3,3]{0,3,2,1:T(4,128)S(1)}, f32[8,3,3,3]{0,3,2,1:T(4,128)}, u32[]{:S(2)}) copy-start(f32[8,3,3,3]{0,3,2,1:T(4,128)} %param.8) | copy-start | bytes 2596
  3.5 13.6 %all-to-all-start = ((f32[8,104,128]{2,1,0:T(8,128)}), f32[8,104,128]{2,1,0:T(8,128)S(1)}, u32[]{:S(2)}, u32[]{:S(2)}) async-start(f32[8,104,128]{2,1,0:T(8,128)} %bitcast.5), calls=%async_computation | async-start | bytes 851968 | tf_op jit(solution)/shard_map/all_to_all | solution.py:537
  7.9 16.5 %copy-start.2 = (f32[8,3,3,3]{0,3,2,1:T(4,128)S(1)}, f32[8,3,3,3]{0,3,2,1:T(4,128)}, u32[]{:S(2)}) copy-start(f32[8,3,3,3]{0,3,2,1:T(4,128)} %param.9) | copy-start | bytes 2596
  18.2 10.9 %collective-permute-start = (f32[4,32,384]{2,1,0:T(8,128)S(1)}, f32[4,32,384]{2,1,0:T(8,128)S(1)}, u32[]{:S(2)}, u32[]{:S(2)}) collective-permute-start(f32[4,32,384]{2,1,0:T(8,128)S(1)} %get-tuple-element.28), channel_id=1, source_target_pairs={{0,1},{2,3},{4,5},{6,7},{1,0},{3,2},{5,4},{7,6},{8,9},{10,11},{12,... | collective-permute-start | bytes 589832 | tf_op jit(solution)/shard_map/ppermute | solution.py:574
  18.4 10.7 %collective-permute-start.1 = (f32[4,32,384]{2,1,0:T(8,128)S(1)}, f32[4,32,384]{2,1,0:T(8,128)S(1)}, u32[]{:S(2)}, u32[]{:S(2)}) collective-permute-start(f32[4,32,384]{2,1,0:T(8,128)S(1)} %get-tuple-element.29), channel_id=1, source_target_pairs={{1,2},{3,4},{5,6},{2,1},{4,3},{6,5},{9,10},{11,12},{13,14},{10,9},... | collective-permute-start | bytes 589832 | tf_op jit(solution)/shard_map/ppermute | solution.py:575
  29.5 6.7 %collective-permute-start.2 = (f32[10,8,384]{2,1,0:T(8,128)S(1)}, f32[10,8,384]{2,1,0:T(8,128)S(1)}, u32[]{:S(2)}, u32[]{:S(2)}) collective-permute-start(f32[10,8,384]{2,1,0:T(8,128)S(1)} %get-tuple-element.38), channel_id=1, source_target_pairs={{0,32},{64,96},{128,160},{192,224},{232,200},{168,136},{104,72},{4... | collective-permute-start | bytes 368648 | tf_op jit(solution)/shard_map/ppermute | solution.py:595
  29.6 6.8 %collective-permute-start.3 = (f32[10,8,384]{2,1,0:T(8,128)S(1)}, f32[10,8,384]{2,1,0:T(8,128)S(1)}, u32[]{:S(2)}, u32[]{:S(2)}) collective-permute-start(f32[10,8,384]{2,1,0:T(8,128)S(1)} %get-tuple-element.39), channel_id=1, source_target_pairs={{32,64},{96,128},{160,192},{224,232},{200,168},{136,104},{72,40},{... | collective-permute-start | bytes 368648 | tf_op jit(solution)/shard_map/ppermute | solution.py:596
  39.5 11.5 %copy-start = (f32[8,3,8,256]{3,2,1,0:T(8,128)S(1)}, f32[8,3,8,256]{3,2,1,0:T(8,128)}, u32[]{:S(2)}) copy-start(f32[8,3,8,256]{3,2,1,0:T(8,128)} %start_ref.1) | copy-start | bytes 589828

commit v10 on v9

--- a/solution.py
+++ b/solution.py
@@ -96,14 +96,12 @@
 def unpack_kernel(got_ref, start_ref, field_hbm, resid_hbm, out_ref, sems):
     order = [(f, c) for f in range(2) for c in range(3)]
     copies = [
-        pltpu.make_async_copy(
-            out_ref.at[i], (field_hbm, resid_hbm)[f].at[:, c], sems.at[i]
-        )
-        for i, (f, c) in enumerate(order)
+        pltpu.make_async_copy(out_ref.at[f], ref, sems.at[f])
+        for f, ref in enumerate((field_hbm, resid_hbm))
     ]
 
     def fill(form):
-        for i, (f, c) in enumerate(order):
+        for f, c in order:
             halves = []
             for h in range(2):
                 at = h * 48 + f * 24 + c * 8
@@ -112,8 +110,9 @@
             tile = swap_blocks(jnp.concatenate(halves, axis=2), form)
             if f == 0:
                 tile = tile + start_ref[:, c]
-            out_ref[i] = tile
-            copies[i].start()
+            out_ref[f, :, c] = tile
+            if c == 2:
+                copies[f].start()
 
     for form in (0, 2):
 
@@ -624,7 +623,7 @@
         out_shape=(shape(8, 3, 8, 256), shape(8, 3, 8, 256)),
         in_specs=[VMEM, VMEM],
         out_specs=(HBM, HBM),
-        scratch_shapes=[pltpu.VMEM((6, 8, 8, 256), F32), pltpu.SemaphoreType.DMA((6,))],
+        scratch_shapes=[pltpu.VMEM((2, 8, 3, 8, 256), F32), pltpu.SemaphoreType.DMA((2,))],
         compiler_params=params(),
         name="unpack",
     )(back.reshape(768, 128), start_field)

time: 53 us -> 53 us (level)
  no operation moved by 1% of the time
where the time goes in v10:
time: 53 us; the launch traced here: 52.4 us
  Pallas kernels  16 us (30%)
  starting transfers between devices  14.1 us (27%)
  blocking collectives  11.5 us (22%)
  waiting for transfers between devices  9.32 us (18%)
  between operations  0.77 us (1%)
    all_to_all x1, blocking collectives, on_device(): back = lax.all_to_all(out, 'gz', 0, 0, tiled=True)  11.5 us
    all_to_all x1, waiting for transfers between devices, on_device(): got = lax.all_to_all(packed.reshape(8, ROWS, 128), 'gz', 0, 0, tiled=True)  9.19 us
    ppermute x1, starting transfers between devices, on_device(): y2 = lax.ppermute(send2, 'gy', swaps(range(count_y), 1))  5.93 us
    all_to_all x1, starting transfers between devices, on_device(): got = lax.all_to_all(packed.reshape(8, ROWS, 128), 'gz', 0, 0, tiled=True)  4.31 us
    ppermute x1, starting transfers between devices, on_device(): x2 = lax.ppermute(send2, ('gz', 'gx'), swaps(along, 1))  3.58 us
    pallas_call x1, Pallas kernels, on_device(): pl.pallas_call(strips_kernel, out_shape=shape(8, 96, 128), in_specs=[VMEM...  3.17 us
    pallas_call x1, Pallas kernels, on_device(): pl.pallas_call(middle_kernel, out_shape=(*sides, shape(YT, 16, 192), shap...  3.04 us
    pallas_call x1, Pallas kernels, on_device(): pl.pallas_call(lines_kernel, out_shape=(shape(192, 192), shape(192, 192),...  2.91 us
  transfers between devices with their start and end apart: 5, of which 2 were waited for; matrix products, arithmetic and copies ran while one was open for 1% of the time, Pallas kernels for 14%

profile of v10, /device:TPU:104, one launch (start us, length us, event | category | flops | bytes accessed | tf_op | source)
XLA Modules:
  0.0 52.4 jit_solution(7634579204335333691)
XLA Ops:
  0.6 2.8 %pack.1 = f32[832,128]{1,0:T(8,128)} custom-call(f32[8,3,8,256]{3,2,1,0:T(8,128)} %load_hbm.1, f32[8,3,8,256]{3,2,1,0:T(8,128)} %start_ref.1, s32[8]{0:T(128)} %mats_hbm.1), custom_call_target="tpu_custom_call" | custom-call | tf_op jit(solution)/shard_map/pack/pallas_call | solution.py:522
  3.4 0.0 copy-start.1
  3.5 4.3 %all-to-all-start = ((f32[8,104,128]{2,1,0:T(8,128)}), f32[8,104,128]{2,1,0:T(8,128)S(1)}, u32[]{:S(2)}, u32[]{:S(2)}) async-start(f32[8,104,128]{2,1,0:T(8,128)} %bitcast.5), calls=%async_computation | async-start | bytes 851968 | tf_op jit(solution)/shard_map/all_to_all | solution.py:536
  7.8 0.0 copy-done.1
  7.8 0.1 copy.8
  7.9 0.0 copy-start.2
  7.9 9.2 %all-to-all-done.got_ref = f32[8,104,128]{2,1,0:T(8,128)S(1)} async-done(((f32[8,104,128]{2,1,0:T(8,128)}), f32[8,104,128]{2,1,0:T(8,128)S(1)}, u32[]{:S(2)}, u32[]{:S(2)}) %all-to-all-start) | async-done | bytes 426016 | tf_op jit(solution)/shard_map/all_to_all | solution.py:536
  17.1 1.1 %turn.1 = (f32[8,32,192]{2,1,0:T(8,128)S(1)}, f32[8,32,192]{2,1,0:T(8,128)S(1)}, f32[64,128]{1,0:T(8,128)S(1)}, f32[4,32,384]{2,1,0:T(8,128)S(1)}, f32[4,32,384]{2,1,0:T(8,128)S(1)}) custom-call(f32[8,104,128]{2,1,0:T(8,128)S(1)} %all-to-all-done.got_ref, f32[128,128]{1,0:T(8,128)S(1)} %pad.4.table_ref), custom_call_target="tpu_custom_call" | custom-call | tf_op jit(solution)/shard_map/turn/pallas_call | solution.py:540
  18.2 0.2 collective-permute-start
  18.4 5.9 %collective-permute-start.1 = (f32[4,32,384]{2,1,0:T(8,128)S(1)}, f32[4,32,384]{2,1,0:T(8,128)S(1)}, u32[]{:S(2)}, u32[]{:S(2)}) collective-permute-start(f32[4,32,384]{2,1,0:T(8,128)S(1)} %get-tuple-element.29), channel_id=1, source_target_pairs={{1,2},{3,4},{5,6},{2,1},{4,3},{6,5},{9,10},{11,12},{13,14},{10,9},... | collective-permute-start | bytes 589832 | tf_op jit(solution)/shard_map/ppermute | solution.py:574
  24.3 0.0 copy-done.2
  24.3 0.1 copy.9
  24.5 0.2 reshape.19.factor_ref
  24.6 0.2 fusion
  24.9 0.1 convert_element_type.8.mats_ref
  24.9 2.9 %lines.1 = (f32[192,192]{1,0:T(8,128)S(1)}, f32[192,192]{1,0:T(8,128)S(1)}, f32[96,96]{1,0:T(8,128)S(1)}, f32[96,96]{1,0:T(8,128)S(1)}) custom-call(s32[64]{0:T(128)S(1)} %convert_element_type.8.mats_ref, f32[216]{0:T(256)S(1)} %reshape.19.factor_ref), custom_call_target="tpu_custom_call" | custom-call | tf_op jit(solution)/shard_map/lines/pallas_call | solution.py:555
  27.8 1.3 %setup.1 = (bf16[2,192,1024]{2,1,0:T(8,128)(2,1)S(1)}, bf16[2,96,1024]{2,1,0:T(8,128)(2,1)S(1)}) custom-call(f32[192,192]{1,0:T(8,128)S(1)} %get-tuple-element.30.up_ref, f32[192,192]{1,0:T(8,128)S(1)} %get-tuple-element.31.down_ref, f32[96,96]{1,0:T(8,128)S(1)} %get-tuple-element.32.cup_ref, f32[96,96]{1,0:T(8,128)S(1)} %get-tuple-element.33.cdown_ref, ...), custom_call_target="tpu_custom_call" | custom-call | tf_op jit(solution)/shard_map/setup/pallas_call | solution.py:563
  29.1 0.0 collective-permute-done.y1_ref
  29.1 0.0 collective-permute-done.1.y2_ref
  29.1 0.3 sides.1
  29.5 0.1 collective-permute-start.2
  29.6 3.6 %collective-permute-start.3 = (f32[10,8,384]{2,1,0:T(8,128)S(1)}, f32[10,8,384]{2,1,0:T(8,128)S(1)}, u32[]{:S(2)}, u32[]{:S(2)}) collective-permute-start(f32[10,8,384]{2,1,0:T(8,128)S(1)} %get-tuple-element.39), channel_id=1, source_target_pairs={{32,64},{96,128},{160,192},{224,232},{200,168},{136,104},{72,40},{... | collective-permute-start | bytes 368648 | tf_op jit(solution)/shard_map/ppermute | solution.py:595
  33.2 3.0 %middle.1 = (f32[22,32,192]{2,1,0:T(8,128)S(1)}, f32[22,32,192]{2,1,0:T(8,128)S(1)}, f32[22,32,96]{2,1,0:T(8,128)S(1)}, f32[22,32,192]{2,1,0:T(8,128)S(1)}, f32[...) custom-call(f32[20,32,192]{2,1,0:T(8,128)S(1)} %get-tuple-element.36, ...), custom_call_target="tpu_custom_call" | custom-call | tf_op jit(solution)/shard_map/middle/pallas_call | solution.py:598
  36.2 0.0 collective-permute-done.2.x1_ref
  36.2 0.1 collective-permute-done.3.x2_ref
  36.3 3.2 %strips.1 = f32[8,96,128]{2,1,0:T(8,128)S(1)} custom-call(f32[20,32,192]{2,1,0:T(8,128)S(1)} %get-tuple-element.36.resid_ref, f32[20,8,192]{2,1,0:T(8,128)S(1)} %get-tuple-element.37.edge_ref, f32[10,8,384]{2,1,0:T(8,128)S(1)} %collective-permute-done.2.x1_ref, f32[10,8,384]{2,1,0:T(8,128)S(1)} %collective-permute-done.3.x2_ref, ...), custom_call_target="tpu_custom_call" | custom-call | tf_op jit(solution)/shard_map/strips/pallas_call | solution.py:607
  39.5 0.0 copy-start
  39.5 11.5 %all_to_all.10 = f32[8,96,128]{2,1,0:T(8,128)S(1)} all-to-all(f32[8,96,128]{2,1,0:T(8,128)S(1)} %strips.1), channel_id=1, replica_groups=mesh['gz'=8,'gx'=4,'gy'=8] {'gz'}, dimensions={0} | all-to-all | bytes 786432 | tf_op jit(solution)/shard_map/all_to_all | solution.py:620
  51.0 0.0 copy-done
  51.0 1.4 %unpack.1 = (f32[8,3,8,256]{3,2,1,0:T(8,128)}, f32[8,3,8,256]{3,2,1,0:T(8,128)}) custom-call(f32[768,128]{1,0:T(8,128)S(1)} %bitcast.4, f32[8,3,8,256]{3,2,1,0:T(8,128)S(1)} %copy-done), custom_call_target="tpu_custom_call" | custom-call | tf_op jit(solution)/shard_map/unpack/pallas_call | solution.py:621
  (2 shorter events, 0.0 us)
Async XLA Ops:
  3.4 4.3 %copy-start.1 = (f32[8,3,3,3]{0,3,2,1:T(4,128)S(1)}, f32[8,3,3,3]{0,3,2,1:T(4,128)}, u32[]{:S(2)}) copy-start(f32[8,3,3,3]{0,3,2,1:T(4,128)} %param.8) | copy-start | bytes 2596
  3.5 13.6 %all-to-all-start = ((f32[8,104,128]{2,1,0:T(8,128)}), f32[8,104,128]{2,1,0:T(8,128)S(1)}, u32[]{:S(2)}, u32[]{:S(2)}) async-start(f32[8,104,128]{2,1,0:T(8,128)} %bitcast.5), calls=%async_computation | async-start | bytes 851968 | tf_op jit(solution)/shard_map/all_to_all | solution.py:536
  7.9 16.5 %copy-start.2 = (f32[8,3,3,3]{0,3,2,1:T(4,128)S(1)}, f32[8,3,3,3]{0,3,2,1:T(4,128)}, u32[]{:S(2)}) copy-start(f32[8,3,3,3]{0,3,2,1:T(4,128)} %param.9) | copy-start | bytes 2596
  18.2 10.9 %collective-permute-start = (f32[4,32,384]{2,1,0:T(8,128)S(1)}, f32[4,32,384]{2,1,0:T(8,128)S(1)}, u32[]{:S(2)}, u32[]{:S(2)}) collective-permute-start(f32[4,32,384]{2,1,0:T(8,128)S(1)} %get-tuple-element.28), channel_id=1, source_target_pairs={{0,1},{2,3},{4,5},{6,7},{1,0},{3,2},{5,4},{7,6},{8,9},{10,11},{12,... | collective-permute-start | bytes 589832 | tf_op jit(solution)/shard_map/ppermute | solution.py:573
  18.4 10.7 %collective-permute-start.1 = (f32[4,32,384]{2,1,0:T(8,128)S(1)}, f32[4,32,384]{2,1,0:T(8,128)S(1)}, u32[]{:S(2)}, u32[]{:S(2)}) collective-permute-start(f32[4,32,384]{2,1,0:T(8,128)S(1)} %get-tuple-element.29), channel_id=1, source_target_pairs={{1,2},{3,4},{5,6},{2,1},{4,3},{6,5},{9,10},{11,12},{13,14},{10,9},... | collective-permute-start | bytes 589832 | tf_op jit(solution)/shard_map/ppermute | solution.py:574
  29.5 6.7 %collective-permute-start.2 = (f32[10,8,384]{2,1,0:T(8,128)S(1)}, f32[10,8,384]{2,1,0:T(8,128)S(1)}, u32[]{:S(2)}, u32[]{:S(2)}) collective-permute-start(f32[10,8,384]{2,1,0:T(8,128)S(1)} %get-tuple-element.38), channel_id=1, source_target_pairs={{0,32},{64,96},{128,160},{192,224},{232,200},{168,136},{104,72},{4... | collective-permute-start | bytes 368648 | tf_op jit(solution)/shard_map/ppermute | solution.py:594
  29.6 6.8 %collective-permute-start.3 = (f32[10,8,384]{2,1,0:T(8,128)S(1)}, f32[10,8,384]{2,1,0:T(8,128)S(1)}, u32[]{:S(2)}, u32[]{:S(2)}) collective-permute-start(f32[10,8,384]{2,1,0:T(8,128)S(1)} %get-tuple-element.39), channel_id=1, source_target_pairs={{32,64},{96,128},{160,192},{224,232},{200,168},{136,104},{72,40},{... | collective-permute-start | bytes 368648 | tf_op jit(solution)/shard_map/ppermute | solution.py:595
  39.5 11.5 %copy-start = (f32[8,3,8,256]{3,2,1,0:T(8,128)S(1)}, f32[8,3,8,256]{3,2,1,0:T(8,128)}, u32[]{:S(2)}) copy-start(f32[8,3,8,256]{3,2,1,0:T(8,128)} %start_ref.1) | copy-start | bytes 589828
